TPU v7x, 32 devices: a whole 2x2x4 slice. The times are simulated.
32 devices in a mesh: grp: 1, seg: 32 (over z, y, x, core).
Axes of the slice: x: 2, y: 2, z: 4, core: 2. Of those that a mesh axis runs over, the one named last changes fastest.
Arguments:
- tokens: bfloat16 [32, 2048, 1024], P(('grp', 'seg')), may hold values from -6 to 6
- cotangent: bfloat16 [32, 2048, 1024], P(('grp', 'seg')), may hold values from -6 to 6
- routing: int32 [32, 64], P(('grp', 'seg')), may hold values from 0 to 15
- w_up: bfloat16 [64, 512, 1024], P(None, 'seg'), may hold values from -1.5 to 1.5
- w_down: bfloat16 [64, 512, 1024], P(None, 'seg'), may hold values from -2 to 2
- momentum_up: float32 [64, 512, 1024], P('grp', 'seg'), may hold values from -24 to 24
- momentum_down: float32 [64, 512, 1024], P('grp', 'seg'), may hold values from -24 to 24
Outputs:
- layer_out: bfloat16 [32, 2048, 1024], P(('grp', 'seg'))
- token_grad: bfloat16 [32, 2048, 1024], P(('grp', 'seg'))
- new_momentum_up: float32 [64, 512, 1024], P('grp', 'seg')
- new_momentum_down: float32 [64, 512, 1024], P('grp', 'seg')
- new_up: bfloat16 [64, 512, 1024], P('grp', 'seg')
- new_down: bfloat16 [64, 512, 1024], P('grp', 'seg')
Inputs may be any that keep to these rules, and one draw needn't show every extreme that they name: The routing weight of a segment and expert is this numerator over 512.
All inputs are finite; a program needn't handle non-finite values.
Results may differ from a plain program's by a relative error of at most 0.0075.
Values may be sent and summed in bfloat16 or wider, within the bound.
No kernel may reach another device: no remote copies, remote signals or barrier semaphores. Data moves between devices by JAX's collectives and lax.ppermute only.
A program may use at most 128 MiB of HBM per device.

v0:
```python
import jax
import jax.numpy as jnp
from jax import lax
from jax.sharding import PartitionSpec as P


def gelu_parts(pre):
    act = 0.5 * pre * (1.0 + lax.erf(pre * 0.7071067811865476))
    slope = (
        0.5 * (1.0 + lax.erf(pre * 0.7071067811865476))
        + pre * jnp.exp(-0.5 * pre * pre) * 0.3989422804014327
    )
    return (act, slope)


def spread(mix, rows):
    segs, experts = mix.shape
    columns = experts * rows
    pick = lax.broadcasted_iota(jnp.int32, (experts, columns), 1) // rows
    pick = pick == lax.broadcasted_iota(jnp.int32, (experts, columns), 0)
    wide = jnp.dot(mix, pick.astype(mix.dtype), preferred_element_type=jnp.float32)
    wide = wide.astype(mix.dtype)[:, None, :]
    shape = (segs, rows, columns)
    same = lax.broadcasted_iota(jnp.int32, shape, 1) == lax.broadcasted_iota(jnp.int32, shape, 2) % rows
    full = jnp.where(same, wide, jnp.zeros((), mix.dtype))
    return full.reshape(segs * rows, columns)


def exchange(blocks):
    return lax.all_to_all(blocks, "seg", split_axis=0, concat_axis=0, tiled=True)


def body(tokens, cotangent, routing, w_up, w_down, momentum_up, momentum_down):
    group_count = lax.axis_size("grp")
    seg_count = lax.axis_size("seg")
    group_index = lax.axis_index("grp")
    experts, slice_rows, width = w_up.shape
    owned = experts // group_count
    hidden = seg_count * slice_rows

    routes = exchange(jnp.broadcast_to(routing[:, None, :], (seg_count, 1, experts)))
    mix = (routes[:, 0].astype(jnp.float32) / (8.0 * experts)).astype(jnp.bfloat16)
    mixer = spread(mix, slice_rows)

    def merged(weights):
        flat = weights.reshape(experts * slice_rows, width)
        sums = jnp.dot(mixer, flat, preferred_element_type=jnp.float32).astype(jnp.bfloat16)
        blocks = exchange(sums.reshape(seg_count, slice_rows, width))
        return blocks.reshape(hidden, width)

    def returned(grads):
        blocks = exchange(grads.astype(jnp.bfloat16).reshape(seg_count, slice_rows, width))
        part = lax.dot_general(
            mixer,
            blocks.reshape(hidden, width),
            (((0,), (0,)), ((), ())),
            preferred_element_type=jnp.float32,
        ).reshape(experts, slice_rows, width)
        if group_count == 1:
            return part
        part = lax.psum_scatter(
            part.astype(jnp.bfloat16), "grp", scatter_dimension=0, tiled=True
        )
        return part.astype(jnp.float32)

    def updated(weights, momentum, grad):
        own = weights
        if group_count > 1:
            own = lax.dynamic_slice_in_dim(weights, group_index * owned, owned, 0)
        new_momentum = 0.9 * momentum + grad
        new = (own.astype(jnp.float32) - 0.01 * new_momentum).astype(jnp.bfloat16)
        return new_momentum, new

    inputs = tokens[0]
    grads = cotangent[0]
    up = merged(w_up)
    down = merged(w_down)
    pre = lax.dot_general(
        inputs, up, (((1,), (1,)), ((), ())), preferred_element_type=jnp.float32
    )
    act_full, slope = gelu_parts(pre)
    act = act_full.astype(jnp.bfloat16)
    grad_down = returned(
        lax.dot_general(act, grads, (((0,), (0,)), ((), ())), preferred_element_type=jnp.float32)
    )
    d_act = lax.dot_general(
        grads, down, (((1,), (1,)), ((), ())), preferred_element_type=jnp.float32
    )
    d_pre = (d_act * slope).astype(jnp.bfloat16)
    grad_up = returned(
        lax.dot_general(d_pre, inputs, (((0,), (0,)), ((), ())), preferred_element_type=jnp.float32)
    )
    layer_out = jnp.dot(act, down, preferred_element_type=jnp.float32).astype(jnp.bfloat16)
    token_grad = jnp.dot(d_pre, up, preferred_element_type=jnp.float32).astype(jnp.bfloat16)
    new_momentum_down, new_down = updated(w_down, momentum_down, grad_down)
    new_momentum_up, new_up = updated(w_up, momentum_up, grad_up)
    return (layer_out[None], token_grad[None], new_momentum_up, new_momentum_down, new_up, new_down)


def solution(mesh):
    in_specs = (
        P(("grp", "seg"), None, None),
        P(("grp", "seg"), None, None),
        P(("grp", "seg"), None),
        P(None, "seg", None),
        P(None, "seg", None),
        P("grp", "seg", None),
        P("grp", "seg", None),
    )
    out_specs = (
        P(("grp", "seg"), None, None),
        P(("grp", "seg"), None, None),
        P("grp", "seg", None),
        P("grp", "seg", None),
        P("grp", "seg", None),
        P("grp", "seg", None),
    )
    return jax.shard_map(body, mesh=mesh, in_specs=in_specs, out_specs=out_specs, check_vma=False)
```

profile of v0, /device:TPU:0, one launch (start us, length us, event | category | flops | bytes accessed | tf_op | source)
XLA Modules:
  0.0 146.7 jit_solution(10345669224138586053)
XLA Ops:
  0.6 1.3 broadcast_in_dim.32
  1.9 7.3 %all-to-all-start = ((s32[32,1,64]{2,1,0:T(1,128)}), s32[32,1,64]{2,1,0:T(1,128)S(1)}, u32[]{:S(2)}, u32[]{:S(2)}) async-start(s32[32,1,64]{2,1,0:T(1,128)} %broadcast_in_dim.32), calls=%async_computation | async-start | bytes 32768 | tf_op jit(solution)/shard_map/all_to_all | solution.py:30
  9.3 7.1 %all-to-all-done = s32[32,1,64]{2,1,0:T(1,128)S(1)} async-done(((s32[32,1,64]{2,1,0:T(1,128)}), s32[32,1,64]{2,1,0:T(1,128)S(1)}, u32[]{:S(2)}, u32[]{:S(2)}) %all-to-all-start) | async-done | bytes 8224 | tf_op jit(solution)/shard_map/all_to_all | solution.py:30
  16.3 0.2 convolution_convert_fusion.2
  16.5 0.2 fusion.20
  16.7 0.0 copy-start.1
  16.8 4.0 %convolution_convert_fusion.1 = bf16[512,1024]{1,0:T(8,128)(2,1)} fusion(bf16[512,1024]{1,0:T(8,128)(2,1)S(1)} %bitcast.87, bf16[1024,1024]{1,0:T(8,128)(2,1)} %bitcast.86), kind=kOutput, calls=%fused_computation.32 | convolution fusion | flops 1074266112 | bytes 4194304 | tf_op jit(solution)/shard_map/dot_general | solution.py:47
  20.7 3.4 %all-to-all-start.1 = ((bf16[32,16,1024]{2,1,0:T(8,128)(2,1)}), bf16[32,16,1024]{2,1,0:T(8,128)(2,1)}, u32[]{:S(2)}, u32[]{:S(2)}) async-start(bf16[32,16,1024]{2,1,0:T(8,128)(2,1)} %bitcast.92), calls=%async_computation.1 | async-start | bytes 2097152 | tf_op jit(solution)/shard_map/all_to_all | solution.py:30
  24.1 0.0 copy-done.1
  24.1 2.2 %convolution_convert_fusion = bf16[512,1024]{1,0:T(8,128)(2,1)} fusion(bf16[512,1024]{1,0:T(8,128)(2,1)S(1)} %bitcast.88, bf16[1024,1024]{1,0:T(8,128)(2,1)S(1)} %bitcast.85), kind=kOutput, calls=%fused_computation.31 | convolution fusion | flops 1074266112 | bytes 4194304 | tf_op jit(solution)/shard_map/dot_general | solution.py:47
  26.4 23.9 %all-to-all-done.1 = bf16[32,16,1024]{2,1,0:T(8,128)(2,1)} async-done(((bf16[32,16,1024]{2,1,0:T(8,128)(2,1)}), bf16[32,16,1024]{2,1,0:T(8,128)(2,1)}, u32[]{:S(2)}, u32[]{:S(2)}) %all-to-all-start.1) | async-done | bytes 1048608 | tf_op jit(solution)/shard_map/all_to_all | solution.py:30
  50.3 3.5 %all-to-all-start.2 = ((bf16[32,16,1024]{2,1,0:T(8,128)(2,1)}), bf16[32,16,1024]{2,1,0:T(8,128)(2,1)S(1)}, u32[]{:S(2)}, u32[]{:S(2)}) async-start(bf16[32,16,1024]{2,1,0:T(8,128)(2,1)} %bitcast.91), calls=%async_computation.2 | async-start | bytes 2097152 | tf_op jit(solution)/shard_map/all_to_all | solution.py:30
  53.8 0.0 copy-start.5
  53.9 7.3 %fusion.11 = (bf16[2048,512]{0,1:T(8,128)(2,1)S(1)}, f32[512,2048]{1,0:T(8,128)}) fusion(bf16[512,1024]{1,0:T(8,128)(2,1)} %bitcast.6, bf16[1,2048,1024]{2,1,0:T(8,128)(2,1)} %param.7), kind=kOutput, calls=%fused_computation.14 | convolution fusion | flops 2152726528 | bytes 11534336 | tf_op jit(solution)/shard_map/dot_general | solution.py:78
  61.1 0.0 copy-start.7
  61.1 1.3 copy-done.7
  62.4 0.0 copy-done.5
  62.4 3.3 %fusion.25 = bf16[512,1024]{1,0:T(8,128)(2,1)} fusion(bf16[2048,512]{0,1:T(8,128)(2,1)S(1)} %get-tuple-element.6, bf16[1,2048,1024]{2,1,0:T(8,128)(2,1)S(1)} %copy-done.5), kind=kOutput, calls=%fused_computation.34 | convolution fusion | flops 2148007936 | bytes 7340032 | tf_op jit(solution)/shard_map/dot_general | solution.py:84
  65.8 14.3 %all-to-all-done.2 = bf16[32,16,1024]{2,1,0:T(8,128)(2,1)S(1)} async-done(((bf16[32,16,1024]{2,1,0:T(8,128)(2,1)}), bf16[32,16,1024]{2,1,0:T(8,128)(2,1)S(1)}, u32[]{:S(2)}, u32[]{:S(2)}) %all-to-all-start.2) | async-done | bytes 1048608 | tf_op jit(solution)/shard_map/all_to_all | solution.py:30
  80.0 0.0 copy-start.3
  80.1 3.6 %all-to-all-start.4 = ((bf16[32,16,1024]{2,1,0:T(8,128)(2,1)}), bf16[32,16,1024]{2,1,0:T(8,128)(2,1)S(1)}, u32[]{:S(2)}, u32[]{:S(2)}) async-start(bf16[32,16,1024]{2,1,0:T(8,128)(2,1)} %bitcast.22), calls=%async_computation.4 | async-start | bytes 2097152 | tf_op jit(solution)/shard_map/all_to_all | solution.py:30
  83.7 0.0 copy-start.6
  83.7 6.5 %fusion.5 = bf16[2048,512]{0,1:T(8,128)(2,1)S(1)} fusion(f32[512,2048]{1,0:T(8,128)} %get-tuple-element.7, bf16[512,1024]{1,0:T(8,128)(2,1)S(1)} %bitcast.89, bf16[1,2048,1024]{2,1,0:T(8,128)(2,1)} %param.8), kind=kOutput, calls=%fused_computation.6 | convolution fusion | flops 2157969408 | bytes 11534336 | tf_op jit(solution)/shard_map/dot_general | solution.py:86
  90.2 0.0 copy-done.3
  90.2 0.0 copy-start.9
  90.2 1.3 copy-done.9
  91.5 0.0 copy-done.6
  91.5 3.3 %fusion.22 = bf16[512,1024]{1,0:T(8,128)(2,1)} fusion(bf16[2048,512]{0,1:T(8,128)(2,1)S(1)} %fusion.5, bf16[1,2048,1024]{2,1,0:T(8,128)(2,1)S(1)} %copy-done.6), kind=kOutput, calls=%fused_computation.33 | convolution fusion | flops 2148007936 | bytes 7340032 | tf_op jit(solution)/shard_map/dot_general | solution.py:91
  94.8 15.1 %all-to-all-done.4 = bf16[32,16,1024]{2,1,0:T(8,128)(2,1)S(1)} async-done(((bf16[32,16,1024]{2,1,0:T(8,128)(2,1)}), bf16[32,16,1024]{2,1,0:T(8,128)(2,1)S(1)}, u32[]{:S(2)}, u32[]{:S(2)}) %all-to-all-start.4) | async-done | bytes 1048608 | tf_op jit(solution)/shard_map/all_to_all | solution.py:30
  109.9 3.8 %all-to-all-start.3 = ((bf16[32,16,1024]{2,1,0:T(8,128)(2,1)}), bf16[32,16,1024]{2,1,0:T(8,128)(2,1)S(1)}, u32[]{:S(2)}, u32[]{:S(2)}) async-start(bf16[32,16,1024]{2,1,0:T(8,128)(2,1)} %bitcast.19), calls=%async_computation.3 | async-start | bytes 2097152 | tf_op jit(solution)/shard_map/all_to_all | solution.py:30
  113.7 0.1 iota.73
  113.8 1.3 fusion.28
  115.0 1.5 %copy.18 = bf16[1024,512]{1,0:T(8,128)(2,1)S(1)} copy(bf16[1024,512]{0,1:T(8,128)(2,1)} %fusion.28) | data formatting | bytes 2097152 | tf_op jit(solution)/shard_map/dot_general | solution.py:53
  116.5 0.0 copy-start.4
  116.6 0.0 copy-start.8
  116.6 6.4 %convert_bitcast_fusion = bf16[1,2048,1024]{2,1,0:T(8,128)(2,1)} fusion(bf16[2048,512]{0,1:T(8,128)(2,1)} %copy-done.9, bf16[512,1024]{1,0:T(8,128)(2,1)} %bitcast.6), kind=kOutput, calls=%fused_computation.25 | convolution fusion | flops 2149580800 | bytes 7340032 | tf_op jit(solution)/shard_map/dot_general | solution.py:94
  123.0 0.0 copy-done.4
  123.0 0.0 copy-done.8
  123.0 0.0 copy-start
  123.0 0.0 copy-start.2
  123.0 4.4 %convert_bitcast_fusion.1 = bf16[1,2048,1024]{2,1,0:T(8,128)(2,1)} fusion(bf16[2048,512]{0,1:T(8,128)(2,1)S(1)} %copy-done.8, bf16[512,1024]{1,0:T(8,128)(2,1)S(1)} %bitcast.90), kind=kOutput, calls=%fused_computation.26 | convolution fusion | flops 2149580800 | bytes 7340032 | tf_op jit(solution)/shard_map/dot_general | solution.py:93
  127.4 0.0 copy-done
  127.4 0.0 copy-done.2
  127.4 4.2 %subtract_convert_fusion = (bf16[64,16,1024]{2,1,0:T(8,128)(2,1)}, f32[64,16,1024]{2,1,0:T(8,128)}) fusion(bf16[64,16,1024]{2,1,0:T(8,128)(2,1)S(1)} %copy-done.2, bf16[64,16,512]{2,1,0:T(8,128)(2,1)S(1)} %bitcast.81, bf16[512,1024,1]{1,0,2:T(8,128)(2,1)S(1)} %bitcast.83, f32[64,16,1024]{2,1,0:T(8,128)S(1)} %copy-done), kind=kOutput, calls=%fused_computation.21 | convolution fusion | flops 1080033280 | bytes 14680064 | tf_op jit(solution)/shard_map/dot_general | solution.py:53
  131.6 8.1 %all-to-all-done.3 = bf16[32,16,1024]{2,1,0:T(8,128)(2,1)S(1)} async-done(((bf16[32,16,1024]{2,1,0:T(8,128)(2,1)}), bf16[32,16,1024]{2,1,0:T(8,128)(2,1)S(1)}, u32[]{:S(2)}, u32[]{:S(2)}) %all-to-all-start.3) | async-done | bytes 1048608 | tf_op jit(solution)/shard_map/all_to_all | solution.py:30
  139.7 7.0 %subtract_convert_fusion.1 = (bf16[64,16,1024]{2,1,0:T(8,128)(2,1)}, f32[64,16,1024]{2,1,0:T(8,128)}) fusion(bf16[64,16,1024]{2,1,0:T(8,128)(2,1)} %param.10, bf16[64,16,512]{2,1,0:T(8,128)(2,1)S(1)} %bitcast.82, bf16[512,1024,1]{1,0,2:T(8,128)(2,1)S(1)} %bitcast.84, f32[64,16,1024]{2,1,0:T(8,128)} %param.12), kind=kOutput, calls=%fused_computation.22 | convolution fusion | flops 1080033280 | bytes 14680064 | tf_op jit(solution)/shard_map/dot_general | solution.py:53
  (5 shorter events, 0.0 us)
Async XLA Ops:
  1.9 14.4 %all-to-all-start = ((s32[32,1,64]{2,1,0:T(1,128)}), s32[32,1,64]{2,1,0:T(1,128)S(1)}, u32[]{:S(2)}, u32[]{:S(2)}) async-start(s32[32,1,64]{2,1,0:T(1,128)} %broadcast_in_dim.32), calls=%async_computation | async-start | bytes 32768 | tf_op jit(solution)/shard_map/all_to_all | solution.py:30
  16.7 7.4 %copy-start.1 = (bf16[64,16,1024]{2,1,0:T(8,128)(2,1)S(1)}, bf16[64,16,1024]{2,1,0:T(8,128)(2,1)}, u32[]{:S(2)}) copy-start(bf16[64,16,1024]{2,1,0:T(8,128)(2,1)} %param.11) | copy-start | bytes 6291460
  20.7 29.6 %all-to-all-start.1 = ((bf16[32,16,1024]{2,1,0:T(8,128)(2,1)}), bf16[32,16,1024]{2,1,0:T(8,128)(2,1)}, u32[]{:S(2)}, u32[]{:S(2)}) async-start(bf16[32,16,1024]{2,1,0:T(8,128)(2,1)} %bitcast.92), calls=%async_computation.1 | async-start | bytes 2097152 | tf_op jit(solution)/shard_map/all_to_all | solution.py:30
  50.3 29.8 %all-to-all-start.2 = ((bf16[32,16,1024]{2,1,0:T(8,128)(2,1)}), bf16[32,16,1024]{2,1,0:T(8,128)(2,1)S(1)}, u32[]{:S(2)}, u32[]{:S(2)}) async-start(bf16[32,16,1024]{2,1,0:T(8,128)(2,1)} %bitcast.91), calls=%async_computation.2 | async-start | bytes 2097152 | tf_op jit(solution)/shard_map/all_to_all | solution.py:30
  53.8 8.6 %copy-start.5 = (bf16[1,2048,1024]{2,1,0:T(8,128)(2,1)S(1)}, bf16[1,2048,1024]{2,1,0:T(8,128)(2,1)}, u32[]{:S(2)}) copy-start(bf16[1,2048,1024]{2,1,0:T(8,128)(2,1)} %param.8) | copy-start | bytes 12582916
  61.1 1.3 copy-start.7
  80.0 10.1 %copy-start.3 = (bf16[32,16,1024]{2,1,0:T(8,128)(2,1)}, bf16[32,16,1024]{2,1,0:T(8,128)(2,1)S(1)}, u32[]{:S(2)}) copy-start(bf16[32,16,1024]{2,1,0:T(8,128)(2,1)S(1)} %all-to-all-done.2) | copy-start | bytes 3145732
  80.1 29.8 %all-to-all-start.4 = ((bf16[32,16,1024]{2,1,0:T(8,128)(2,1)}), bf16[32,16,1024]{2,1,0:T(8,128)(2,1)S(1)}, u32[]{:S(2)}, u32[]{:S(2)}) async-start(bf16[32,16,1024]{2,1,0:T(8,128)(2,1)} %bitcast.22), calls=%async_computation.4 | async-start | bytes 2097152 | tf_op jit(solution)/shard_map/all_to_all | solution.py:30
  83.7 7.8 %copy-start.6 = (bf16[1,2048,1024]{2,1,0:T(8,128)(2,1)S(1)}, bf16[1,2048,1024]{2,1,0:T(8,128)(2,1)}, u32[]{:S(2)}) copy-start(bf16[1,2048,1024]{2,1,0:T(8,128)(2,1)} %param.7) | copy-start | bytes 12582916
  90.2 1.3 copy-start.9
  109.9 29.8 %all-to-all-start.3 = ((bf16[32,16,1024]{2,1,0:T(8,128)(2,1)}), bf16[32,16,1024]{2,1,0:T(8,128)(2,1)S(1)}, u32[]{:S(2)}, u32[]{:S(2)}) async-start(bf16[32,16,1024]{2,1,0:T(8,128)(2,1)} %bitcast.19), calls=%async_computation.3 | async-start | bytes 2097152 | tf_op jit(solution)/shard_map/all_to_all | solution.py:30
  116.5 6.4 %copy-start.4 = (bf16[32,16,1024]{2,1,0:T(8,128)(2,1)S(1)}, bf16[32,16,1024]{2,1,0:T(8,128)(2,1)}, u32[]{:S(2)}) copy-start(bf16[32,16,1024]{2,1,0:T(8,128)(2,1)} %copy-done.3) | copy-start | bytes 3145732
  116.6 6.4 %copy-start.8 = (bf16[2048,512]{0,1:T(8,128)(2,1)S(1)}, bf16[2048,512]{0,1:T(8,128)(2,1)}, u32[]{:S(2)}) copy-start(bf16[2048,512]{0,1:T(8,128)(2,1)} %copy-done.7) | copy-start | bytes 6291460
  123.0 4.4 %copy-start = (f32[64,16,1024]{2,1,0:T(8,128)S(1)}, f32[64,16,1024]{2,1,0:T(8,128)}, u32[]{:S(2)}) copy-start(f32[64,16,1024]{2,1,0:T(8,128)} %param.13) | copy-start | bytes 12582916
  123.0 4.4 %copy-start.2 = (bf16[64,16,1024]{2,1,0:T(8,128)(2,1)S(1)}, bf16[64,16,1024]{2,1,0:T(8,128)(2,1)}, u32[]{:S(2)}) copy-start(bf16[64,16,1024]{2,1,0:T(8,128)(2,1)} %param.11) | copy-start | bytes 6291460
where the time goes:
time: 147 us
  waiting for transfers between devices  68.4 us (47%)
  matrix products  48.7 us (33%)
  starting transfers between devices  21.7 us (15%)
  local copies, waits for them, and re-layouts  5.52 us (4%)
  other arithmetic  1.52 us (1%)
    all_to_all x5, waiting for transfers between devices, exchange(): lax.all_to_all(blocks, 'seg', split_axis=0, concat_axis=0, tiled=True)  68.4 us
    all_to_all x5, starting transfers between devices, exchange(): lax.all_to_all(blocks, 'seg', split_axis=0, concat_axis=0, tiled=True)  21.7 us
    dot_general x2, matrix products, returned(): lax.dot_general(mixer, blocks.reshape(hidden, width), (((0,), (0,)), ((),...  11.2 us
    dot_general x1, matrix products, body(): lax.dot_general(inputs, up, (((1,), (1,)), ((), ())), preferred_element_t...  7.27 us
    dot_general x1, matrix products, body(): lax.dot_general(grads, down, (((1,), (1,)), ((), ())), preferred_element_...  6.46 us
    dot_general x1, matrix products, body(): jnp.dot(d_pre, up, preferred_element_type=jnp.float32).astype(jnp.bfloat16)  6.4 us
    dot_general x2, matrix products, merged(): jnp.dot(mixer, flat, preferred_element_type=jnp.float32)  6.19 us
    dot_general x1, matrix products, body(): jnp.dot(act, down, preferred_element_type=jnp.float32).astype(jnp.bfloat16)  4.4 us
  transfers between devices with their start and end apart: 5, of which 5 were waited for; matrix products, arithmetic and copies ran while one was open for 28% of the time, Pallas kernels for 0%

commit v1 on v0

v1 whole, which is shorter than its diff:
```python
import functools

import jax
import jax.numpy as jnp
from jax import lax
from jax.experimental import pallas as pl
from jax.experimental.pallas import tpu as pltpu
from jax.sharding import PartitionSpec as P


def gelu_parts(pre):
    act = 0.5 * pre * (1.0 + lax.erf(pre * 0.7071067811865476))
    slope = (
        0.5 * (1.0 + lax.erf(pre * 0.7071067811865476))
        + pre * jnp.exp(-0.5 * pre * pre) * 0.3989422804014327
    )
    return (act, slope)


def mix_kernel(rows, route_ref, weight_ref, sum_ref, mixer_ref):
    @pl.when(pl.program_id(0) == 0)
    def _():
        segs, _, experts = route_ref.shape
        columns = experts * rows
        mix = (route_ref[:, 0, :].astype(jnp.float32) / (8.0 * experts)).astype(jnp.bfloat16)
        pick = lax.broadcasted_iota(jnp.int32, (experts, columns), 1) // rows
        pick = pick == lax.broadcasted_iota(jnp.int32, (experts, columns), 0)
        pick = jnp.where(pick, 1.0, 0.0).astype(jnp.bfloat16)
        wide = jnp.dot(mix, pick, preferred_element_type=jnp.float32)
        same = lax.broadcasted_iota(jnp.int32, (rows, columns), 0)
        same = same == lax.broadcasted_iota(jnp.int32, (rows, columns), 1) % rows
        for s in range(segs):
            line = jnp.broadcast_to(wide[s : s + 1, :], (rows, columns))
            mixer_ref[s * rows : (s + 1) * rows, :] = jnp.where(same, line, 0.0).astype(jnp.bfloat16)

    sum_ref[...] = jnp.dot(
        mixer_ref[...], weight_ref[...], preferred_element_type=jnp.float32
    ).astype(jnp.bfloat16)


def mix_first(routes, weights):
    segs = routes.shape[0]
    experts, rows, width = weights.shape
    tile = width // 4
    return pl.pallas_call(
        functools.partial(mix_kernel, rows),
        grid=(width // tile,),
        in_specs=[
            pl.BlockSpec(routes.shape, lambda i: (0, 0, 0)),
            pl.BlockSpec((experts * rows, tile), lambda i: (0, i)),
        ],
        out_specs=[
            pl.BlockSpec((segs * rows, tile), lambda i: (0, i)),
            pl.BlockSpec((segs * rows, experts * rows), lambda i: (0, 0)),
        ],
        out_shape=[
            jax.ShapeDtypeStruct((segs * rows, width), jnp.bfloat16),
            jax.ShapeDtypeStruct((segs * rows, experts * rows), jnp.bfloat16),
        ],
        compiler_params=pltpu.CompilerParams(vmem_limit_bytes=12 << 20),
        name="mix_first",
    )(routes, weights.reshape(experts * rows, width))


def update_kernel(mixer_ref, grad_ref, weight_ref, momentum_ref, new_momentum_ref, new_ref):
    part = jnp.dot(mixer_ref[...], grad_ref[...], preferred_element_type=jnp.float32)
    moved = 0.9 * momentum_ref[...] + part
    new_momentum_ref[...] = moved
    new_ref[...] = (weight_ref[...].astype(jnp.float32) - 0.01 * moved).astype(jnp.bfloat16)


def update(mixer, grads, weights, momentum):
    experts, rows, width = weights.shape
    lines = experts * rows
    tile = lines // 4
    block = pl.BlockSpec((tile, width), lambda i: (i, 0))
    grads = pltpu.with_memory_space_constraint(grads, pltpu.VMEM)
    momentum = pltpu.with_memory_space_constraint(momentum.reshape(lines, width), pltpu.HBM)
    new_momentum, new = pl.pallas_call(
        update_kernel,
        grid=(lines // tile,),
        in_specs=[
            pl.BlockSpec((tile, mixer.shape[1]), lambda i: (i, 0)),
            pl.BlockSpec(memory_space=pltpu.VMEM),
            block,
            block,
        ],
        out_specs=[block, block],
        out_shape=[
            jax.ShapeDtypeStruct((lines, width), jnp.float32),
            jax.ShapeDtypeStruct((lines, width), jnp.bfloat16),
        ],
        compiler_params=pltpu.CompilerParams(vmem_limit_bytes=20 << 20),
        name="update",
    )(mixer, grads, weights.reshape(lines, width), momentum)
    return new_momentum.reshape(weights.shape), new.reshape(weights.shape)


def exchange(blocks):
    return lax.all_to_all(blocks, "seg", split_axis=0, concat_axis=0, tiled=True)


def body(tokens, cotangent, routing, w_up, w_down, momentum_up, momentum_down):
    group_count = lax.axis_size("grp")
    seg_count = lax.axis_size("seg")
    group_index = lax.axis_index("grp")
    experts, slice_rows, width = w_up.shape
    owned = experts // group_count
    hidden = seg_count * slice_rows

    routes = exchange(jnp.broadcast_to(routing[:, None, :], (seg_count, 1, experts)))
    first, mixer = mix_first(routes, w_up)

    def delivered(sums):
        return exchange(sums.reshape(seg_count, slice_rows, width)).reshape(hidden, width)

    def returned(grads):
        return delivered(grads.astype(jnp.bfloat16))

    turned = mixer.T

    def updated(weights, momentum, grads):
        if group_count == 1:
            return update(turned, grads, weights, momentum)
        part = jnp.dot(turned, grads, preferred_element_type=jnp.float32)
        part = part.astype(jnp.bfloat16).reshape(experts, slice_rows, width)
        part = lax.psum_scatter(part, "grp", scatter_dimension=0, tiled=True)
        own = lax.dynamic_slice_in_dim(weights, group_index * owned, owned, 0)
        new_momentum = 0.9 * momentum + part.astype(jnp.float32)
        new = (own.astype(jnp.float32) - 0.01 * new_momentum).astype(jnp.bfloat16)
        return new_momentum, new

    inputs = tokens[0]
    grads = cotangent[0]
    up = delivered(first)
    flat_down = w_down.reshape(experts * slice_rows, width)
    second = jnp.dot(mixer, flat_down, preferred_element_type=jnp.float32)
    down = delivered(second.astype(jnp.bfloat16))
    pre = lax.dot_general(
        inputs, up, (((1,), (1,)), ((), ())), preferred_element_type=jnp.float32
    )
    act_full, slope = gelu_parts(pre)
    act = act_full.astype(jnp.bfloat16)
    grad_down = returned(
        lax.dot_general(act, grads, (((0,), (0,)), ((), ())), preferred_element_type=jnp.float32)
    )
    d_act = lax.dot_general(
        grads, down, (((1,), (1,)), ((), ())), preferred_element_type=jnp.float32
    )
    d_pre = (d_act * slope).astype(jnp.bfloat16)
    grad_up = returned(
        lax.dot_general(d_pre, inputs, (((0,), (0,)), ((), ())), preferred_element_type=jnp.float32)
    )
    new_momentum_down, new_down = updated(w_down, momentum_down, grad_down)
    act, d_pre, new_momentum_down, new_down = lax.optimization_barrier(
        (act, d_pre, new_momentum_down, new_down)
    )
    layer_out = jnp.dot(act, down, preferred_element_type=jnp.float32).astype(jnp.bfloat16)
    token_grad = jnp.dot(d_pre, up, preferred_element_type=jnp.float32).astype(jnp.bfloat16)
    new_momentum_up, new_up = updated(w_up, momentum_up, grad_up)
    return (layer_out[None], token_grad[None], new_momentum_up, new_momentum_down, new_up, new_down)


def solution(mesh):
    in_specs = (
        P(("grp", "seg"), None, None),
        P(("grp", "seg"), None, None),
        P(("grp", "seg"), None),
        P(None, "seg", None),
        P(None, "seg", None),
        P("grp", "seg", None),
        P("grp", "seg", None),
    )
    out_specs = (
        P(("grp", "seg"), None, None),
        P(("grp", "seg"), None, None),
        P("grp", "seg", None),
        P("grp", "seg", None),
        P("grp", "seg", None),
        P("grp", "seg", None),
    )
    return jax.shard_map(body, mesh=mesh, in_specs=in_specs, out_specs=out_specs, check_vma=False)
```

time: 147 us -> 147 us (level)
  matrix products: 48.7 us -> 32.8 us
  Pallas kernels: 0 us -> 15.2 us
  blocking collectives: 0 us -> 14.3 us
  waiting for transfers between devices: 68.4 us -> 60.7 us
  starting transfers between devices: 21.7 us -> 14.5 us
  local copies, waits for them, and re-layouts: 5.52 us -> 8.02 us
  other arithmetic: 1.52 us -> 0 us
    dot_general x5 -> x1, matrix products: 17.6 us -> 2.22 us  [body(): second = jnp.dot(mixer, flat_down, preferred_element_type=jnp.float32)]
    pallas_call x0 -> x3, Pallas kernels: none -> 15.2 us  [the longest x2 12.7 us: update(): pl.pallas_call(update_kernel, grid=(lines // tile,), in_specs=[pl.BlockSp...]
    all_to_all x0 -> x1, blocking collectives: none -> 14.3 us  [exchange(): lax.all_to_all(blocks, 'seg', split_axis=0, concat_axis=0, tiled=True)]
    all_to_all x5 -> x4, waiting for transfers between devices: 68.4 us -> 60.7 us  [exchange(): lax.all_to_all(blocks, 'seg', split_axis=0, concat_axis=0, tiled=True)]
    all_to_all x5 -> x4, starting transfers between devices: 21.7 us -> 14.5 us  [exchange(): lax.all_to_all(blocks, 'seg', split_axis=0, concat_axis=0, tiled=True)]
    unnamed x20 -> x26, local copies, waits for them, and re-layouts: 2.68 us -> 6.81 us
    dot_general x1 -> x0, local copies, waits for them, and re-layouts: 1.49 us -> none  [returned(): lax.dot_general(mixer, blocks.reshape(hidden, width), (((0,), (0,)), ((),...]
  transfers between devices with their start and end apart: 5 -> 4, of which waited for: 5 -> 4; matrix products, arithmetic and copies ran while one was open for 28% -> 23% of each run, Pallas kernels for 0% -> 4%
where the time goes in v1:
time: 147 us; the launch traced here: 146 us
  waiting for transfers between devices  60.7 us (41%)
  matrix products  32.8 us (22%)
  Pallas kernels  15.2 us (10%)
  starting transfers between devices  14.5 us (10%)
  blocking collectives  14.3 us (10%)
  local copies, waits for them, and re-layouts  8.02 us (5%)
    all_to_all x4, waiting for transfers between devices, exchange(): lax.all_to_all(blocks, 'seg', split_axis=0, concat_axis=0, tiled=True)  60.7 us
    all_to_all x4, starting transfers between devices, exchange(): lax.all_to_all(blocks, 'seg', split_axis=0, concat_axis=0, tiled=True)  14.5 us
    all_to_all x1, blocking collectives, exchange(): lax.all_to_all(blocks, 'seg', split_axis=0, concat_axis=0, tiled=True)  14.3 us
    pallas_call x2, Pallas kernels, update(): pl.pallas_call(update_kernel, grid=(lines // tile,), in_specs=[pl.BlockSp...  12.7 us
    dot_general x1, matrix products, body(): lax.dot_general(inputs, up, (((1,), (1,)), ((), ())), preferred_element_t...  7.27 us
    unnamed x26, local copies, waits for them, and re-layouts  6.81 us
    dot_general x1, matrix products, body(): lax.dot_general(grads, down, (((1,), (1,)), ((), ())), preferred_element_...  6.45 us
    dot_general x1, matrix products, body(): jnp.dot(d_pre, up, preferred_element_type=jnp.float32).astype(jnp.bfloat16)  5.77 us
  transfers between devices with their start and end apart: 4, of which 4 were waited for; matrix products, arithmetic and copies ran while one was open for 23% of the time, Pallas kernels for 4%

profile of v1, /device:TPU:0, one launch (start us, length us, event | category | flops | bytes accessed | tf_op | source)
XLA Modules:
  0.0 146.2 jit_solution(926284224716100257)
XLA Ops:
  0.6 0.7 broadcast_in_dim.15
  1.3 14.3 %all_to_all.25.route_ref = s32[32,1,64]{2,1,0:T(1,128)S(1)} all-to-all(s32[32,1,64]{2,1,0:T(1,128)S(1)} %broadcast_in_dim.15), channel_id=1, replica_groups=mesh['grp'=1,'seg'=32] {'seg'}, dimensions={0} | all-to-all | bytes 16384 | tf_op jit(solution)/shard_map/all_to_all | solution.py:100
  15.6 0.0 copy-start
  15.6 1.6 %copy-done = bf16[64,16,1024]{2,1,0:T(8,128)(2,1)S(1)} copy-done((bf16[64,16,1024]{2,1,0:T(8,128)(2,1)S(1)}, bf16[64,16,1024]{2,1,0:T(8,128)(2,1)}, u32[]{:S(2)}) %copy-start) | copy-done | bytes 2097176
  17.2 0.0 copy-start.2
  17.2 2.5 %mix_first.1 = (bf16[512,1024]{1,0:T(8,128)(2,1)S(1)}, bf16[512,1024]{1,0:T(8,128)(2,1)S(1)}) custom-call(s32[32,1,64]{2,1,0:T(1,128)S(1)} %all_to_all.25.route_ref, bf16[1024,1024]{1,0:T(8,128)(2,1)S(1)} %bitcast.70), custom_call_target="tpu_custom_call" | custom-call | tf_op jit(solution)/shard_map/mix_first/pallas_call | solution.py:45
  19.7 0.0 copy-start.4
  19.7 1.0 copy-done.4
  20.7 3.4 %all-to-all-start.1 = ((bf16[32,16,1024]{2,1,0:T(8,128)(2,1)}), bf16[32,16,1024]{2,1,0:T(8,128)(2,1)}, u32[]{:S(2)}, u32[]{:S(2)}) async-start(bf16[32,16,1024]{2,1,0:T(8,128)(2,1)} %bitcast.75), calls=%async_computation.1 | async-start | bytes 2097152 | tf_op jit(solution)/shard_map/all_to_all | solution.py:100
  24.1 0.0 copy-done.2
  24.1 2.2 %convolution_convert_fusion = bf16[512,1024]{1,0:T(8,128)(2,1)} fusion(bf16[512,1024]{1,0:T(8,128)(2,1)S(1)} %get-tuple-element.17, bf16[1024,1024]{1,0:T(8,128)(2,1)S(1)} %bitcast.73), kind=kOutput, calls=%fused_computation.23 | convolution fusion | flops 1074266112 | bytes 4194304 | tf_op jit(solution)/shard_map/dot_general | solution.py:137
  26.3 23.9 %all-to-all-done.1 = bf16[32,16,1024]{2,1,0:T(8,128)(2,1)} async-done(((bf16[32,16,1024]{2,1,0:T(8,128)(2,1)}), bf16[32,16,1024]{2,1,0:T(8,128)(2,1)}, u32[]{:S(2)}, u32[]{:S(2)}) %all-to-all-start.1) | async-done | bytes 1048608 | tf_op jit(solution)/shard_map/all_to_all | solution.py:100
  50.2 3.5 %all-to-all-start.2 = ((bf16[32,16,1024]{2,1,0:T(8,128)(2,1)}), bf16[32,16,1024]{2,1,0:T(8,128)(2,1)S(1)}, u32[]{:S(2)}, u32[]{:S(2)}) async-start(bf16[32,16,1024]{2,1,0:T(8,128)(2,1)} %bitcast.81), calls=%async_computation.2 | async-start | bytes 2097152 | tf_op jit(solution)/shard_map/all_to_all | solution.py:100
  53.8 0.0 copy-start.7
  53.8 7.3 %fusion.11 = (bf16[2048,512]{0,1:T(8,128)(2,1)S(1)}, f32[512,2048]{1,0:T(8,128)}) fusion(bf16[512,1024]{1,0:T(8,128)(2,1)} %bitcast.3, bf16[1,2048,1024]{2,1,0:T(8,128)(2,1)} %param.7), kind=kOutput, calls=%fused_computation.14 | convolution fusion | flops 2152726528 | bytes 11534336 | tf_op jit(solution)/shard_map/dot_general | solution.py:139
  61.1 0.0 copy-start.9
  61.1 1.3 copy-done.9
  62.4 0.0 copy-done.7
  62.4 3.3 %fusion.23 = bf16[512,1024]{1,0:T(8,128)(2,1)} fusion(bf16[2048,512]{0,1:T(8,128)(2,1)S(1)} %get-tuple-element.20, bf16[1,2048,1024]{2,1,0:T(8,128)(2,1)S(1)} %copy-done.7), kind=kOutput, calls=%fused_computation.25 | convolution fusion | flops 2148007936 | bytes 7340032 | tf_op jit(solution)/shard_map/dot_general | solution.py:145
  65.7 14.3 %all-to-all-done.2 = bf16[32,16,1024]{2,1,0:T(8,128)(2,1)S(1)} async-done(((bf16[32,16,1024]{2,1,0:T(8,128)(2,1)}), bf16[32,16,1024]{2,1,0:T(8,128)(2,1)S(1)}, u32[]{:S(2)}, u32[]{:S(2)}) %all-to-all-start.2) | async-done | bytes 1048608 | tf_op jit(solution)/shard_map/all_to_all | solution.py:100
  80.0 0.0 copy-start.5
  80.0 3.6 %all-to-all-start.3 = ((bf16[32,16,1024]{2,1,0:T(8,128)(2,1)}), bf16[32,16,1024]{2,1,0:T(8,128)(2,1)S(1)}, u32[]{:S(2)}, u32[]{:S(2)}) async-start(bf16[32,16,1024]{2,1,0:T(8,128)(2,1)} %bitcast.82), calls=%async_computation.3 | async-start | bytes 2097152 | tf_op jit(solution)/shard_map/all_to_all | solution.py:100
  83.6 0.0 copy-start.8
  83.6 6.4 %fusion.5 = bf16[2048,512]{0,1:T(8,128)(2,1)S(1)} fusion(f32[512,2048]{1,0:T(8,128)} %get-tuple-element.27, bf16[512,1024]{1,0:T(8,128)(2,1)S(1)} %bitcast.78, bf16[1,2048,1024]{2,1,0:T(8,128)(2,1)} %param.8), kind=kOutput, calls=%fused_computation.6 | convolution fusion | flops 2157969408 | bytes 11534336 | tf_op jit(solution)/shard_map/dot_general | solution.py:147
  90.1 0.0 copy-done.5
  90.1 0.0 copy-start.11
  90.1 1.3 copy-done.11
  91.4 0.0 copy-done.8
  91.4 3.3 %fusion.20 = bf16[512,1024]{1,0:T(8,128)(2,1)} fusion(bf16[2048,512]{0,1:T(8,128)(2,1)S(1)} %fusion.5, bf16[1,2048,1024]{2,1,0:T(8,128)(2,1)S(1)} %copy-done.8), kind=kOutput, calls=%fused_computation.24 | convolution fusion | flops 2148007936 | bytes 7340032 | tf_op jit(solution)/shard_map/dot_general | solution.py:152
  94.7 15.1 %all-to-all-done.3 = bf16[32,16,1024]{2,1,0:T(8,128)(2,1)S(1)} async-done(((bf16[32,16,1024]{2,1,0:T(8,128)(2,1)}), bf16[32,16,1024]{2,1,0:T(8,128)(2,1)S(1)}, u32[]{:S(2)}, u32[]{:S(2)}) %all-to-all-start.3) | async-done | bytes 1048608 | tf_op jit(solution)/shard_map/all_to_all | solution.py:100
  109.8 3.9 %all-to-all-start.4 = ((bf16[32,16,1024]{2,1,0:T(8,128)(2,1)}), bf16[32,16,1024]{2,1,0:T(8,128)(2,1)}, u32[]{:S(2)}, u32[]{:S(2)}) async-start(bf16[32,16,1024]{2,1,0:T(8,128)(2,1)} %bitcast.80), calls=%async_computation.4 | async-start | bytes 2097152 | tf_op jit(solution)/shard_map/all_to_all | solution.py:100
  113.8 0.5 copy.13
  114.3 0.0 copy-start.3
  114.3 1.6 %copy-done.3 = bf16[64,16,1024]{2,1,0:T(8,128)(2,1)S(1)} copy-done((bf16[64,16,1024]{2,1,0:T(8,128)(2,1)S(1)}, bf16[64,16,1024]{2,1,0:T(8,128)(2,1)}, u32[]{:S(2)}) %copy-start.3) | copy-done | bytes 2097176
  115.9 0.0 copy-start.6
  115.9 0.0 copy-start.10
  115.9 6.3 %update.2 = (f32[1024,1024]{1,0:T(8,128)}, bf16[1024,1024]{1,0:T(8,128)(2,1)}) custom-call(bf16[1024,512]{1,0:T(8,128)(2,1)S(1)} %bitcast.68, bf16[512,1024]{1,0:T(8,128)(2,1)S(1)} %bitcast.72, bf16[1024,1024]{1,0:T(8,128)(2,1)S(1)} %bitcast.74, f32[1024,1024]{1,0:T(8,128)} %bitcast.76), custom_call_target="tpu_custom_call" | custom-call | tf_op jit(solution)/shard_map/update/pallas_call | solution.py:79
  122.2 0.0 copy-done.6
  122.2 0.0 copy-done.10
  122.2 0.0 copy-start.12
  122.2 4.4 %convert_bitcast_fusion.1 = bf16[1,2048,1024]{2,1,0:T(8,128)(2,1)} fusion(bf16[2048,512]{0,1:T(8,128)(2,1)S(1)} %copy-done.10, bf16[512,1024]{1,0:T(8,128)(2,1)S(1)} %bitcast.79), kind=kOutput, calls=%fused_computation.22 | convolution fusion | flops 2149580800 | bytes 7340032 | tf_op jit(solution)/shard_map/dot_general | solution.py:158
  126.6 0.0 copy-done.12
  126.6 0.0 copy-start.1
  126.6 5.8 %convert_bitcast_fusion = bf16[1,2048,1024]{2,1,0:T(8,128)(2,1)} fusion(bf16[2048,512]{0,1:T(8,128)(2,1)S(1)} %copy-done.12, bf16[512,1024]{1,0:T(8,128)(2,1)} %bitcast.3), kind=kOutput, calls=%fused_computation.21 | convolution fusion | flops 2149580800 | bytes 7340032 | tf_op jit(solution)/shard_map/dot_general | solution.py:159
  132.4 7.4 %all-to-all-done.4 = bf16[32,16,1024]{2,1,0:T(8,128)(2,1)} async-done(((bf16[32,16,1024]{2,1,0:T(8,128)(2,1)}), bf16[32,16,1024]{2,1,0:T(8,128)(2,1)}, u32[]{:S(2)}, u32[]{:S(2)}) %all-to-all-start.4) | async-done | bytes 1048608 | tf_op jit(solution)/shard_map/all_to_all | solution.py:100
  139.8 0.0 copy-done.1
  139.8 6.4 %update.3 = (f32[1024,1024]{1,0:T(8,128)}, bf16[1024,1024]{1,0:T(8,128)(2,1)}) custom-call(bf16[1024,512]{1,0:T(8,128)(2,1)S(1)} %bitcast.69, bf16[512,1024]{1,0:T(8,128)(2,1)} %bitcast.20.grad_ref, bf16[1024,1024]{1,0:T(8,128)(2,1)S(1)} %bitcast.71, f32[1024,1024]{1,0:T(8,128)} %bitcast.77), custom_call_target="tpu_custom_call" | custom-call | tf_op jit(solution)/shard_map/update/pallas_call | solution.py:79
Async XLA Ops:
  15.6 1.6 %copy-start = (bf16[64,16,1024]{2,1,0:T(8,128)(2,1)S(1)}, bf16[64,16,1024]{2,1,0:T(8,128)(2,1)}, u32[]{:S(2)}) copy-start(bf16[64,16,1024]{2,1,0:T(8,128)(2,1)} %param.10) | copy-start | bytes 6291460
  17.2 6.9 %copy-start.2 = (bf16[64,16,1024]{2,1,0:T(8,128)(2,1)S(1)}, bf16[64,16,1024]{2,1,0:T(8,128)(2,1)}, u32[]{:S(2)}) copy-start(bf16[64,16,1024]{2,1,0:T(8,128)(2,1)} %param.11) | copy-start | bytes 6291460
  19.7 1.0 copy-start.4
  20.7 29.6 %all-to-all-start.1 = ((bf16[32,16,1024]{2,1,0:T(8,128)(2,1)}), bf16[32,16,1024]{2,1,0:T(8,128)(2,1)}, u32[]{:S(2)}, u32[]{:S(2)}) async-start(bf16[32,16,1024]{2,1,0:T(8,128)(2,1)} %bitcast.75), calls=%async_computation.1 | async-start | bytes 2097152 | tf_op jit(solution)/shard_map/all_to_all | solution.py:100
  50.2 29.8 %all-to-all-start.2 = ((bf16[32,16,1024]{2,1,0:T(8,128)(2,1)}), bf16[32,16,1024]{2,1,0:T(8,128)(2,1)S(1)}, u32[]{:S(2)}, u32[]{:S(2)}) async-start(bf16[32,16,1024]{2,1,0:T(8,128)(2,1)} %bitcast.81), calls=%async_computation.2 | async-start | bytes 2097152 | tf_op jit(solution)/shard_map/all_to_all | solution.py:100
  53.8 8.6 %copy-start.7 = (bf16[1,2048,1024]{2,1,0:T(8,128)(2,1)S(1)}, bf16[1,2048,1024]{2,1,0:T(8,128)(2,1)}, u32[]{:S(2)}) copy-start(bf16[1,2048,1024]{2,1,0:T(8,128)(2,1)} %param.8) | copy-start | bytes 12582916
  61.1 1.3 copy-start.9
  80.0 10.1 %copy-start.5 = (bf16[32,16,1024]{2,1,0:T(8,128)(2,1)}, bf16[32,16,1024]{2,1,0:T(8,128)(2,1)S(1)}, u32[]{:S(2)}) copy-start(bf16[32,16,1024]{2,1,0:T(8,128)(2,1)S(1)} %all-to-all-done.2) | copy-start | bytes 3145732
  80.0 29.8 %all-to-all-start.3 = ((bf16[32,16,1024]{2,1,0:T(8,128)(2,1)}), bf16[32,16,1024]{2,1,0:T(8,128)(2,1)S(1)}, u32[]{:S(2)}, u32[]{:S(2)}) async-start(bf16[32,16,1024]{2,1,0:T(8,128)(2,1)} %bitcast.82), calls=%async_computation.3 | async-start | bytes 2097152 | tf_op jit(solution)/shard_map/all_to_all | solution.py:100
  83.6 7.8 %copy-start.8 = (bf16[1,2048,1024]{2,1,0:T(8,128)(2,1)S(1)}, bf16[1,2048,1024]{2,1,0:T(8,128)(2,1)}, u32[]{:S(2)}) copy-start(bf16[1,2048,1024]{2,1,0:T(8,128)(2,1)} %param.7) | copy-start | bytes 12582916
  90.1 1.3 copy-start.11
  109.8 29.9 %all-to-all-start.4 = ((bf16[32,16,1024]{2,1,0:T(8,128)(2,1)}), bf16[32,16,1024]{2,1,0:T(8,128)(2,1)}, u32[]{:S(2)}, u32[]{:S(2)}) async-start(bf16[32,16,1024]{2,1,0:T(8,128)(2,1)} %bitcast.80), calls=%async_computation.4 | async-start | bytes 2097152 | tf_op jit(solution)/shard_map/all_to_all | solution.py:100
  114.3 1.6 %copy-start.3 = (bf16[64,16,1024]{2,1,0:T(8,128)(2,1)S(1)}, bf16[64,16,1024]{2,1,0:T(8,128)(2,1)}, u32[]{:S(2)}) copy-start(bf16[64,16,1024]{2,1,0:T(8,128)(2,1)} %param.11) | copy-start | bytes 6291460
  115.9 6.3 %copy-start.6 = (bf16[32,16,1024]{2,1,0:T(8,128)(2,1)S(1)}, bf16[32,16,1024]{2,1,0:T(8,128)(2,1)}, u32[]{:S(2)}) copy-start(bf16[32,16,1024]{2,1,0:T(8,128)(2,1)} %copy-done.5) | copy-start | bytes 3145732
  115.9 6.3 %copy-start.10 = (bf16[2048,512]{0,1:T(8,128)(2,1)S(1)}, bf16[2048,512]{0,1:T(8,128)(2,1)}, u32[]{:S(2)}) copy-start(bf16[2048,512]{0,1:T(8,128)(2,1)} %copy-done.9) | copy-start | bytes 6291460
  122.2 4.4 %copy-start.12 = (bf16[2048,512]{0,1:T(8,128)(2,1)S(1)}, bf16[2048,512]{0,1:T(8,128)(2,1)}, u32[]{:S(2)}) copy-start(bf16[2048,512]{0,1:T(8,128)(2,1)} %copy-done.11) | copy-start | bytes 6291460
  126.6 13.2 %copy-start.1 = (bf16[64,16,1024]{2,1,0:T(8,128)(2,1)S(1)}, bf16[64,16,1024]{2,1,0:T(8,128)(2,1)}, u32[]{:S(2)}) copy-start(bf16[64,16,1024]{2,1,0:T(8,128)(2,1)} %param.10) | copy-start | bytes 6291460

commit v2 on v1

--- a/solution.py
+++ b/solution.py
@@ -6,6 +6,8 @@
 from jax.experimental import pallas as pl
 from jax.experimental.pallas import tpu as pltpu
 from jax.sharding import PartitionSpec as P
+
+PIECES = 4
 
 
 def gelu_parts(pre):
@@ -33,8 +35,10 @@
             line = jnp.broadcast_to(wide[s : s + 1, :], (rows, columns))
             mixer_ref[s * rows : (s + 1) * rows, :] = jnp.where(same, line, 0.0).astype(jnp.bfloat16)
 
+    tile = sum_ref.shape[1]
+    here = pl.ds(pl.multiple_of(pl.program_id(0) * tile, tile), tile)
     sum_ref[...] = jnp.dot(
-        mixer_ref[...], weight_ref[...], preferred_element_type=jnp.float32
+        mixer_ref[...], weight_ref[:, here], preferred_element_type=jnp.float32
     ).astype(jnp.bfloat16)
 
 
@@ -47,14 +51,14 @@
         grid=(width // tile,),
         in_specs=[
             pl.BlockSpec(routes.shape, lambda i: (0, 0, 0)),
-            pl.BlockSpec((experts * rows, tile), lambda i: (0, i)),
+            pl.BlockSpec(memory_space=pltpu.VMEM),
         ],
         out_specs=[
             pl.BlockSpec((segs * rows, tile), lambda i: (0, i)),
             pl.BlockSpec((segs * rows, experts * rows), lambda i: (0, 0)),
         ],
         out_shape=[
-            jax.ShapeDtypeStruct((segs * rows, width), jnp.bfloat16),
+            pltpu.HBM((segs * rows, width), jnp.bfloat16),
             jax.ShapeDtypeStruct((segs * rows, experts * rows), jnp.bfloat16),
         ],
         compiler_params=pltpu.CompilerParams(vmem_limit_bytes=12 << 20),
@@ -62,38 +66,91 @@
     )(routes, weights.reshape(experts * rows, width))
 
 
-def update_kernel(mixer_ref, grad_ref, weight_ref, momentum_ref, new_momentum_ref, new_ref):
-    part = jnp.dot(mixer_ref[...], grad_ref[...], preferred_element_type=jnp.float32)
-    moved = 0.9 * momentum_ref[...] + part
-    new_momentum_ref[...] = moved
-    new_ref[...] = (weight_ref[...].astype(jnp.float32) - 0.01 * moved).astype(jnp.bfloat16)
-
-
-def update(mixer, grads, weights, momentum):
+def fetch_kernel(count, *refs):
+    sources, targets, sems = refs[:count], refs[count : 2 * count], refs[2 * count]
+    copies = [
+        pltpu.make_async_copy(source, target, sems.at[i])
+        for i, (source, target) in enumerate(zip(sources, targets))
+    ]
+    for copy in copies:
+        copy.start()
+    for copy in copies:
+        copy.wait()
+
+
+def fetch(*arrays):
+    count = len(arrays)
+    return pl.pallas_call(
+        functools.partial(fetch_kernel, count),
+        in_specs=[pl.BlockSpec(memory_space=pltpu.HBM)] * count,
+        out_specs=[pl.BlockSpec(memory_space=pltpu.VMEM)] * count,
+        out_shape=[pltpu.VMEM(array.shape, array.dtype) for array in arrays],
+        scratch_shapes=[pltpu.SemaphoreType.DMA((count,))],
+        compiler_params=pltpu.CompilerParams(vmem_limit_bytes=1 << 20),
+        name="fetch",
+    )(*(pltpu.with_memory_space_constraint(array, pltpu.HBM) for array in arrays))
+
+
+def update_kernel(
+    count, mixer_ref, weight_ref, grad_hbm, momentum_hbm, new_momentum_hbm, new_hbm,
+    grad_ref, momentum_ref, new_ref, grad_sem, in_sems, out_sems,
+):
+    lines = momentum_ref.shape[0] // count
+    parts = [slice(i * lines, (i + 1) * lines) for i in range(count)]
+    first = pltpu.make_async_copy(grad_hbm, grad_ref, grad_sem)
+    first.start()
+    reads = [
+        pltpu.make_async_copy(momentum_hbm.at[here, :], momentum_ref.at[here, :], in_sems.at[i])
+        for i, here in enumerate(parts)
+    ]
+    for read in reads:
+        read.start()
+    first.wait()
+    writes = []
+    for i, here in enumerate(parts):
+        part = jnp.dot(mixer_ref[here, :], grad_ref[...], preferred_element_type=jnp.float32)
+        reads[i].wait()
+        moved = 0.9 * momentum_ref[here, :] + part
+        momentum_ref[here, :] = moved
+        rounded = weight_ref[here, :].astype(jnp.float32) - 0.01 * moved
+        new_ref[here, :] = rounded.astype(jnp.bfloat16)
+        pairs = ((momentum_ref, new_momentum_hbm), (new_ref, new_hbm))
+        for j, (source, target) in enumerate(pairs):
+            write = pltpu.make_async_copy(source.at[here, :], target.at[here, :], out_sems.at[i, j])
+            write.start()
+            writes.append(write)
+    for write in writes:
+        write.wait()
+
+
+def update_last(mixer, grads, weights, momentum):
     experts, rows, width = weights.shape
     lines = experts * rows
-    tile = lines // 4
-    block = pl.BlockSpec((tile, width), lambda i: (i, 0))
-    grads = pltpu.with_memory_space_constraint(grads, pltpu.VMEM)
+    count = PIECES if experts % PIECES == 0 else 1
+    mixer = pltpu.with_memory_space_constraint(mixer, pltpu.VMEM)
+    weights = pltpu.with_memory_space_constraint(weights.reshape(lines, width), pltpu.VMEM)
     momentum = pltpu.with_memory_space_constraint(momentum.reshape(lines, width), pltpu.HBM)
+    vmem, hbm = pl.BlockSpec(memory_space=pltpu.VMEM), pl.BlockSpec(memory_space=pltpu.HBM)
     new_momentum, new = pl.pallas_call(
-        update_kernel,
-        grid=(lines // tile,),
-        in_specs=[
-            pl.BlockSpec((tile, mixer.shape[1]), lambda i: (i, 0)),
-            pl.BlockSpec(memory_space=pltpu.VMEM),
-            block,
-            block,
-        ],
-        out_specs=[block, block],
+        functools.partial(update_kernel, count),
+        in_specs=[vmem, vmem, pl.BlockSpec(memory_space=pl.ANY), hbm],
+        out_specs=[hbm, hbm],
         out_shape=[
             jax.ShapeDtypeStruct((lines, width), jnp.float32),
             jax.ShapeDtypeStruct((lines, width), jnp.bfloat16),
         ],
-        compiler_params=pltpu.CompilerParams(vmem_limit_bytes=20 << 20),
-        name="update",
-    )(mixer, grads, weights.reshape(lines, width), momentum)
-    return new_momentum.reshape(weights.shape), new.reshape(weights.shape)
+        scratch_shapes=[
+            pltpu.VMEM(grads.shape, grads.dtype),
+            pltpu.VMEM((lines, width), jnp.float32),
+            pltpu.VMEM((lines, width), jnp.bfloat16),
+            pltpu.SemaphoreType.DMA,
+            pltpu.SemaphoreType.DMA((count,)),
+            pltpu.SemaphoreType.DMA((count, 2)),
+        ],
+        compiler_params=pltpu.CompilerParams(vmem_limit_bytes=12 << 20),
+        name="update_last",
+    )(mixer, weights, grads, momentum)
+    return new_momentum.reshape(experts, rows, width), new.reshape(experts, rows, width)
 
 
 def exchange(blocks):
@@ -109,7 +166,8 @@
     hidden = seg_count * slice_rows
 
     routes = exchange(jnp.broadcast_to(routing[:, None, :], (seg_count, 1, experts)))
-    first, mixer = mix_first(routes, w_up)
+    (early_up,) = fetch(w_up)
+    first, mixer = mix_first(routes, early_up)
 
     def delivered(sums):
         return exchange(sums.reshape(seg_count, slice_rows, width)).reshape(hidden, width)
@@ -120,14 +178,15 @@
     turned = mixer.T
 
     def updated(weights, momentum, grads):
-        if group_count == 1:
-            return update(turned, grads, weights, momentum)
         part = jnp.dot(turned, grads, preferred_element_type=jnp.float32)
-        part = part.astype(jnp.bfloat16).reshape(experts, slice_rows, width)
-        part = lax.psum_scatter(part, "grp", scatter_dimension=0, tiled=True)
-        own = lax.dynamic_slice_in_dim(weights, group_index * owned, owned, 0)
-        new_momentum = 0.9 * momentum + part.astype(jnp.float32)
-        new = (own.astype(jnp.float32) - 0.01 * new_momentum).astype(jnp.bfloat16)
+        part = part.reshape(experts, slice_rows, width)
+        if group_count > 1:
+            part = part.astype(jnp.bfloat16)
+            part = lax.psum_scatter(part, "grp", scatter_dimension=0, tiled=True)
+            part = part.astype(jnp.float32)
+            weights = lax.dynamic_slice_in_dim(weights, group_index * owned, owned, 0)
+        new_momentum = 0.9 * momentum + part
+        new = (weights.astype(jnp.float32) - 0.01 * new_momentum).astype(jnp.bfloat16)
         return new_momentum, new
 
     inputs = tokens[0]
@@ -157,7 +216,12 @@
     )
     layer_out = jnp.dot(act, down, preferred_element_type=jnp.float32).astype(jnp.bfloat16)
     token_grad = jnp.dot(d_pre, up, preferred_element_type=jnp.float32).astype(jnp.bfloat16)
-    new_momentum_up, new_up = updated(w_up, momentum_up, grad_up)
+    layer_out, token_grad, late_up = lax.optimization_barrier((layer_out, token_grad, w_up))
+    if group_count == 1:
+        (late_up,) = fetch(late_up)
+        new_momentum_up, new_up = update_last(turned, grad_up, late_up, momentum_up)
+    else:
+        new_momentum_up, new_up = updated(late_up, momentum_up, grad_up)
     return (layer_out[None], token_grad[None], new_momentum_up, new_momentum_down, new_up, new_down)
 
 

time: 147 us -> 145 us (0.986)
  blocking collectives: 14.3 us -> 0 us
  matrix products: 32.8 us -> 40.7 us
  starting transfers between devices: 14.5 us -> 21.2 us
  waiting for transfers between devices: 60.7 us -> 64.5 us
  local copies, waits for them, and re-layouts: 8.02 us -> 4.47 us
  Pallas kernels: 15.2 us -> 12.7 us
    all_to_all x1 -> x0, blocking collectives: 14.3 us -> none  [exchange(): lax.all_to_all(blocks, 'seg', split_axis=0, concat_axis=0, tiled=True)]
    dot_general x0 -> x1, matrix products: none -> 7.17 us  [updated(): part = jnp.dot(turned, grads, preferred_element_type=jnp.float32)]
    all_to_all x4 -> x5, starting transfers between devices: 14.5 us -> 21.2 us  [exchange(): lax.all_to_all(blocks, 'seg', split_axis=0, concat_axis=0, tiled=True)]
    unnamed x26 -> x16, local copies, waits for them, and re-layouts: 6.81 us -> 2.66 us
    all_to_all x4 -> x5, waiting for transfers between devices: 60.7 us -> 64.5 us  [exchange(): lax.all_to_all(blocks, 'seg', split_axis=0, concat_axis=0, tiled=True)]
    pallas_call x2 -> x3, Pallas kernels: 12.7 us -> 9.64 us  [the longest x1 6.44 us: update_last(): pl.pallas_call(functools.partial(update_kernel, count), in_specs=[vmem, v...]
    dot_general x1, matrix products: 2.22 us -> 3.82 us  [body(): second = jnp.dot(mixer, flat_down, preferred_element_type=jnp.float32)]
  transfers between devices with their start and end apart: 4 -> 5, of which waited for: 4 -> 5; matrix products, arithmetic and copies ran while one was open for 23% -> 29% of each run, Pallas kernels for 4% -> 2%
where the time goes in v2:
time: 145 us
  waiting for transfers between devices  64.5 us (44%)
  matrix products  40.7 us (28%)
  starting transfers between devices  21.2 us (15%)
  Pallas kernels  12.7 us (9%)
  local copies, waits for them, and re-layouts  4.47 us (3%)
    all_to_all x5, waiting for transfers between devices, exchange(): lax.all_to_all(blocks, 'seg', split_axis=0, concat_axis=0, tiled=True)  64.5 us
    all_to_all x5, starting transfers between devices, exchange(): lax.all_to_all(blocks, 'seg', split_axis=0, concat_axis=0, tiled=True)  21.2 us
    dot_general x1, matrix products, updated(): part = jnp.dot(turned, grads, preferred_element_type=jnp.float32)  7.17 us
    dot_general x1, matrix products, body(): lax.dot_general(inputs, up, (((1,), (1,)), ((), ())), preferred_element_t...  6.66 us
    pallas_call x1, Pallas kernels, update_last(): pl.pallas_call(functools.partial(update_kernel, count), in_specs=[vmem, v...  6.44 us
    dot_general x1, matrix products, body(): lax.dot_general(grads, down, (((1,), (1,)), ((), ())), preferred_element_...  6.2 us
    dot_general x1, matrix products, body(): jnp.dot(act, down, preferred_element_type=jnp.float32).astype(jnp.bfloat16)  5.77 us
    dot_general x1, matrix products, body(): jnp.dot(d_pre, up, preferred_element_type=jnp.float32).astype(jnp.bfloat16)  4.4 us
  transfers between devices with their start and end apart: 5, of which 5 were waited for; matrix products, arithmetic and copies ran while one was open for 29% of the time, Pallas kernels for 2%

profile of v2, /device:TPU:0, one launch (start us, length us, event | category | flops | bytes accessed | tf_op | source)
XLA Modules:
  0.0 144.5 jit_solution(6793867668160120719)
XLA Ops:
  0.6 1.3 broadcast_in_dim.15
  1.9 7.3 %all-to-all-start = ((s32[32,1,64]{2,1,0:T(1,128)}), s32[32,1,64]{2,1,0:T(1,128)S(1)}, u32[]{:S(2)}, u32[]{:S(2)}) async-start(s32[32,1,64]{2,1,0:T(1,128)} %broadcast_in_dim.15), calls=%async_computation | async-start | bytes 32768 | tf_op jit(solution)/shard_map/all_to_all | solution.py:157
  9.2 1.6 %fetch.2 = bf16[64,16,1024]{2,1,0:T(8,128)(2,1)S(1)} custom-call(bf16[64,16,1024]{2,1,0:T(8,128)(2,1)} %refs_0_.2), custom_call_target="tpu_custom_call" | custom-call | tf_op jit(solution)/shard_map/fetch/pallas_call | solution.py:83
  10.8 5.5 %all-to-all-done.route_ref = s32[32,1,64]{2,1,0:T(1,128)S(1)} async-done(((s32[32,1,64]{2,1,0:T(1,128)}), s32[32,1,64]{2,1,0:T(1,128)S(1)}, u32[]{:S(2)}, u32[]{:S(2)}) %all-to-all-start) | async-done | bytes 8224 | tf_op jit(solution)/shard_map/all_to_all | solution.py:157
  16.3 3.1 %mix_first.1 = (bf16[512,1024]{1,0:T(8,128)(2,1)}, bf16[512,1024]{1,0:T(8,128)(2,1)S(1)}) custom-call(s32[32,1,64]{2,1,0:T(1,128)S(1)} %all-to-all-done.route_ref, bf16[1024,1024]{1,0:T(8,128)(2,1)S(1)} %bitcast.72), custom_call_target="tpu_custom_call" | custom-call | tf_op jit(solution)/shard_map/mix_first/pallas_call | solution.py:49
  19.4 2.6 %all-to-all-start.1 = ((bf16[32,16,1024]{2,1,0:T(8,128)(2,1)}), bf16[32,16,1024]{2,1,0:T(8,128)(2,1)S(1)}, u32[]{:S(2)}, u32[]{:S(2)}) async-start(bf16[32,16,1024]{2,1,0:T(8,128)(2,1)} %bitcast.79), calls=%async_computation.1 | async-start | bytes 2097152 | tf_op jit(solution)/shard_map/all_to_all | solution.py:157
  22.1 3.8 %convolution_convert_fusion.2 = bf16[512,1024]{1,0:T(8,128)(2,1)} fusion(bf16[512,1024]{1,0:T(8,128)(2,1)S(1)} %get-tuple-element.18, bf16[1024,1024]{1,0:T(8,128)(2,1)} %bitcast.76), kind=kOutput, calls=%fused_computation.25 | convolution fusion | flops 1074266112 | bytes 4194304 | tf_op jit(solution)/shard_map/dot_general | solution.py:196
  25.9 22.4 %all-to-all-done.1 = bf16[32,16,1024]{2,1,0:T(8,128)(2,1)S(1)} async-done(((bf16[32,16,1024]{2,1,0:T(8,128)(2,1)}), bf16[32,16,1024]{2,1,0:T(8,128)(2,1)S(1)}, u32[]{:S(2)}, u32[]{:S(2)}) %all-to-all-start.1) | async-done | bytes 1048608 | tf_op jit(solution)/shard_map/all_to_all | solution.py:157
  48.3 0.0 copy-start
  48.3 3.7 %all-to-all-start.2 = ((bf16[32,16,1024]{2,1,0:T(8,128)(2,1)}), bf16[32,16,1024]{2,1,0:T(8,128)(2,1)}, u32[]{:S(2)}, u32[]{:S(2)}) async-start(bf16[32,16,1024]{2,1,0:T(8,128)(2,1)} %bitcast.7), calls=%async_computation.2 | async-start | bytes 2097152 | tf_op jit(solution)/shard_map/all_to_all | solution.py:157
  52.0 0.0 copy-start.2
  52.0 6.7 %fusion.11 = (bf16[2048,512]{0,1:T(8,128)(2,1)S(1)}, f32[512,2048]{1,0:T(8,128)}) fusion(bf16[512,1024]{1,0:T(8,128)(2,1)S(1)} %bitcast.77, bf16[1,2048,1024]{2,1,0:T(8,128)(2,1)} %param.7), kind=kOutput, calls=%fused_computation.14 | convolution fusion | flops 2152726528 | bytes 11534336 | tf_op jit(solution)/shard_map/dot_general | solution.py:198
  58.6 0.0 copy-done
  58.6 0.0 copy-start.4
  58.6 1.3 copy-done.4
  59.9 0.0 copy-done.2
  60.0 3.3 %fusion.23 = bf16[512,1024]{1,0:T(8,128)(2,1)} fusion(bf16[2048,512]{0,1:T(8,128)(2,1)S(1)} %get-tuple-element.19, bf16[1,2048,1024]{2,1,0:T(8,128)(2,1)S(1)} %copy-done.2), kind=kOutput, calls=%fused_computation.27 | convolution fusion | flops 2148007936 | bytes 7340032 | tf_op jit(solution)/shard_map/dot_general | solution.py:204
  63.3 14.8 %all-to-all-done.2 = bf16[32,16,1024]{2,1,0:T(8,128)(2,1)} async-done(((bf16[32,16,1024]{2,1,0:T(8,128)(2,1)}), bf16[32,16,1024]{2,1,0:T(8,128)(2,1)}, u32[]{:S(2)}, u32[]{:S(2)}) %all-to-all-start.2) | async-done | bytes 1048608 | tf_op jit(solution)/shard_map/all_to_all | solution.py:157
  78.1 3.6 %all-to-all-start.3 = ((bf16[32,16,1024]{2,1,0:T(8,128)(2,1)}), bf16[32,16,1024]{2,1,0:T(8,128)(2,1)S(1)}, u32[]{:S(2)}, u32[]{:S(2)}) async-start(bf16[32,16,1024]{2,1,0:T(8,128)(2,1)} %bitcast.13), calls=%async_computation.3 | async-start | bytes 2097152 | tf_op jit(solution)/shard_map/all_to_all | solution.py:157
  81.8 0.0 copy-start.3
  81.8 6.2 %fusion.5 = bf16[2048,512]{0,1:T(8,128)(2,1)S(1)} fusion(f32[512,2048]{1,0:T(8,128)} %get-tuple-element.29, bf16[512,1024]{1,0:T(8,128)(2,1)} %bitcast.8, bf16[1,2048,1024]{2,1,0:T(8,128)(2,1)} %param.8), kind=kOutput, calls=%fused_computation.6 | convolution fusion | flops 2157969408 | bytes 11534336 | tf_op jit(solution)/shard_map/dot_general | solution.py:206
  88.0 0.0 copy-start.6
  88.0 1.3 copy-done.6
  89.3 0.0 copy-done.3
  89.3 3.3 %fusion.20 = bf16[512,1024]{1,0:T(8,128)(2,1)} fusion(bf16[2048,512]{0,1:T(8,128)(2,1)S(1)} %fusion.5, bf16[1,2048,1024]{2,1,0:T(8,128)(2,1)S(1)} %copy-done.3), kind=kOutput, calls=%fused_computation.26 | convolution fusion | flops 2148007936 | bytes 7340032 | tf_op jit(solution)/shard_map/dot_general | solution.py:211
  92.6 15.4 %all-to-all-done.3 = bf16[32,16,1024]{2,1,0:T(8,128)(2,1)S(1)} async-done(((bf16[32,16,1024]{2,1,0:T(8,128)(2,1)}), bf16[32,16,1024]{2,1,0:T(8,128)(2,1)S(1)}, u32[]{:S(2)}, u32[]{:S(2)}) %all-to-all-start.3) | async-done | bytes 1048608 | tf_op jit(solution)/shard_map/all_to_all | solution.py:157
  108.0 3.9 %all-to-all-start.4 = ((bf16[32,16,1024]{2,1,0:T(8,128)(2,1)}), bf16[32,16,1024]{2,1,0:T(8,128)(2,1)}, u32[]{:S(2)}, u32[]{:S(2)}) async-start(bf16[32,16,1024]{2,1,0:T(8,128)(2,1)} %bitcast.19), calls=%async_computation.4 | async-start | bytes 2097152 | tf_op jit(solution)/shard_map/all_to_all | solution.py:157
  111.9 0.5 copy.13
  112.5 0.0 copy-start.5
  112.5 7.2 %subtract_convert_fusion = (bf16[64,16,1024]{2,1,0:T(8,128)(2,1)}, f32[64,16,1024]{2,1,0:T(8,128)}) fusion(bf16[64,16,1024]{2,1,0:T(8,128)(2,1)} %param.11, bf16[64,16,512]{2,1,0:T(8,128)(2,1)S(1)} %bitcast.70, bf16[512,1024,1]{1,0,2:T(8,128)(2,1)S(1)} %bitcast.74, f32[64,16,1024]{2,1,0:T(8,128)} %param.13), kind=kOutput, calls=%fused_computation.21 | convolution fusion | flops 1080033280 | bytes 14680064 | tf_op jit(solution)/shard_map/dot_general | solution.py:181
  119.6 0.0 copy-done.5
  119.6 0.0 copy-start.1
  119.6 0.0 copy-start.7
  119.6 5.8 %convolution_convert_fusion.1 = bf16[2048,1024]{1,0:T(8,128)(2,1)} fusion(bf16[2048,512]{0,1:T(8,128)(2,1)S(1)} %copy-done.5, bf16[512,1024]{1,0:T(8,128)(2,1)} %bitcast.8), kind=kOutput, calls=%fused_computation.24 | convolution fusion | flops 2149580800 | bytes 7340032 | tf_op jit(solution)/shard_map/dot_general | solution.py:217
  125.4 0.0 copy-done.1
  125.4 0.0 copy-done.7
  125.4 4.4 %convolution_convert_fusion = bf16[2048,1024]{1,0:T(8,128)(2,1)} fusion(bf16[2048,512]{0,1:T(8,128)(2,1)S(1)} %copy-done.7, bf16[512,1024]{1,0:T(8,128)(2,1)S(1)} %bitcast.78), kind=kOutput, calls=%fused_computation.23 | convolution fusion | flops 2149580800 | bytes 7340032 | tf_op jit(solution)/shard_map/dot_general | solution.py:218
  129.8 1.6 %fetch.3 = bf16[64,16,1024]{2,1,0:T(8,128)(2,1)S(1)} custom-call(bf16[64,16,1024]{2,1,0:T(8,128)(2,1)} %refs_0_.2), custom_call_target="tpu_custom_call" | custom-call | tf_op jit(solution)/shard_map/fetch/pallas_call | solution.py:83
  131.4 6.5 %all-to-all-done.4 = bf16[32,16,1024]{2,1,0:T(8,128)(2,1)} async-done(((bf16[32,16,1024]{2,1,0:T(8,128)(2,1)}), bf16[32,16,1024]{2,1,0:T(8,128)(2,1)}, u32[]{:S(2)}, u32[]{:S(2)}) %all-to-all-start.4) | async-done | bytes 1048608 | tf_op jit(solution)/shard_map/all_to_all | solution.py:157
  137.9 6.4 %update_last.1 = (f32[1024,1024]{1,0:T(8,128)}, bf16[1024,1024]{1,0:T(8,128)(2,1)}) custom-call(bf16[1024,512]{1,0:T(8,128)(2,1)S(1)} %bitcast.71, bf16[1024,1024]{1,0:T(8,128)(2,1)S(1)} %bitcast.73, bf16[512,1024]{1,0:T(8,128)(2,1)} %bitcast.20.grad_hbm, f32[1024,1024]{1,0:T(8,128)} %bitcast.75), custom_call_target="tpu_custom_call" | custom-call | tf_op jit(solution)/shard_map/update_last/pallas_call | solution.py:134
Async XLA Ops:
  1.9 14.4 %all-to-all-start = ((s32[32,1,64]{2,1,0:T(1,128)}), s32[32,1,64]{2,1,0:T(1,128)S(1)}, u32[]{:S(2)}, u32[]{:S(2)}) async-start(s32[32,1,64]{2,1,0:T(1,128)} %broadcast_in_dim.15), calls=%async_computation | async-start | bytes 32768 | tf_op jit(solution)/shard_map/all_to_all | solution.py:157
  19.4 28.8 %all-to-all-start.1 = ((bf16[32,16,1024]{2,1,0:T(8,128)(2,1)}), bf16[32,16,1024]{2,1,0:T(8,128)(2,1)S(1)}, u32[]{:S(2)}, u32[]{:S(2)}) async-start(bf16[32,16,1024]{2,1,0:T(8,128)(2,1)} %bitcast.79), calls=%async_computation.1 | async-start | bytes 2097152 | tf_op jit(solution)/shard_map/all_to_all | solution.py:157
  48.3 10.4 %copy-start = (bf16[32,16,1024]{2,1,0:T(8,128)(2,1)}, bf16[32,16,1024]{2,1,0:T(8,128)(2,1)S(1)}, u32[]{:S(2)}) copy-start(bf16[32,16,1024]{2,1,0:T(8,128)(2,1)S(1)} %all-to-all-done.1) | copy-start | bytes 3145732
  48.3 29.9 %all-to-all-start.2 = ((bf16[32,16,1024]{2,1,0:T(8,128)(2,1)}), bf16[32,16,1024]{2,1,0:T(8,128)(2,1)}, u32[]{:S(2)}, u32[]{:S(2)}) async-start(bf16[32,16,1024]{2,1,0:T(8,128)(2,1)} %bitcast.7), calls=%async_computation.2 | async-start | bytes 2097152 | tf_op jit(solution)/shard_map/all_to_all | solution.py:157
  52.0 8.0 %copy-start.2 = (bf16[1,2048,1024]{2,1,0:T(8,128)(2,1)S(1)}, bf16[1,2048,1024]{2,1,0:T(8,128)(2,1)}, u32[]{:S(2)}) copy-start(bf16[1,2048,1024]{2,1,0:T(8,128)(2,1)} %param.8) | copy-start | bytes 12582916
  58.6 1.3 copy-start.4
  78.1 29.8 %all-to-all-start.3 = ((bf16[32,16,1024]{2,1,0:T(8,128)(2,1)}), bf16[32,16,1024]{2,1,0:T(8,128)(2,1)S(1)}, u32[]{:S(2)}, u32[]{:S(2)}) async-start(bf16[32,16,1024]{2,1,0:T(8,128)(2,1)} %bitcast.13), calls=%async_computation.3 | async-start | bytes 2097152 | tf_op jit(solution)/shard_map/all_to_all | solution.py:157
  81.8 7.5 %copy-start.3 = (bf16[1,2048,1024]{2,1,0:T(8,128)(2,1)S(1)}, bf16[1,2048,1024]{2,1,0:T(8,128)(2,1)}, u32[]{:S(2)}) copy-start(bf16[1,2048,1024]{2,1,0:T(8,128)(2,1)} %param.7) | copy-start | bytes 12582916
  88.0 1.3 copy-start.6
  108.0 29.9 %all-to-all-start.4 = ((bf16[32,16,1024]{2,1,0:T(8,128)(2,1)}), bf16[32,16,1024]{2,1,0:T(8,128)(2,1)}, u32[]{:S(2)}, u32[]{:S(2)}) async-start(bf16[32,16,1024]{2,1,0:T(8,128)(2,1)} %bitcast.19), calls=%async_computation.4 | async-start | bytes 2097152 | tf_op jit(solution)/shard_map/all_to_all | solution.py:157
  112.5 7.2 %copy-start.5 = (bf16[2048,512]{0,1:T(8,128)(2,1)S(1)}, bf16[2048,512]{0,1:T(8,128)(2,1)}, u32[]{:S(2)}) copy-start(bf16[2048,512]{0,1:T(8,128)(2,1)} %copy-done.4) | copy-start | bytes 6291460
  119.6 5.8 %copy-start.1 = (bf16[32,16,1024]{2,1,0:T(8,128)(2,1)S(1)}, bf16[32,16,1024]{2,1,0:T(8,128)(2,1)}, u32[]{:S(2)}) copy-start(bf16[32,16,1024]{2,1,0:T(8,128)(2,1)} %copy-done) | copy-start | bytes 3145732
  119.6 5.8 %copy-start.7 = (bf16[2048,512]{0,1:T(8,128)(2,1)S(1)}, bf16[2048,512]{0,1:T(8,128)(2,1)}, u32[]{:S(2)}) copy-start(bf16[2048,512]{0,1:T(8,128)(2,1)} %copy-done.6) | copy-start | bytes 6291460

commit v3 on v2

--- a/solution.py
+++ b/solution.py
@@ -7,7 +7,9 @@
 from jax.experimental.pallas import tpu as pltpu
 from jax.sharding import PartitionSpec as P
 
+
 PIECES = 4
+TOP = 4
 
 
 def gelu_parts(pre):
@@ -19,51 +21,157 @@
     return (act, slope)
 
 
-def mix_kernel(rows, route_ref, weight_ref, sum_ref, mixer_ref):
+def mix_of(route_ref):
+    experts = route_ref.shape[2]
+    return (route_ref[:, 0, :].astype(jnp.float32) / (8.0 * experts)).astype(jnp.bfloat16)
+
+
+def spread(mix, rows, out_ref):
+    lines, columns = mix.shape[0], mix.shape[1] * rows
+    pick = lax.broadcasted_iota(jnp.int32, (mix.shape[1], columns), 1) // rows
+    pick = pick == lax.broadcasted_iota(jnp.int32, (mix.shape[1], columns), 0)
+    pick = jnp.where(pick, 1.0, 0.0).astype(jnp.bfloat16)
+    wide = jnp.dot(mix, pick, preferred_element_type=jnp.float32)
+    same = lax.broadcasted_iota(jnp.int32, (rows, columns), 0)
+    same = same == lax.broadcasted_iota(jnp.int32, (rows, columns), 1) % rows
+    for i in range(lines):
+        line = jnp.broadcast_to(wide[i : i + 1, :], (rows, columns))
+        out_ref[i * rows : (i + 1) * rows, :] = jnp.where(same, line, 0.0).astype(jnp.bfloat16)
+
+
+def mix_kernel(rows, top, resident, me_ref, route_ref, weight_ref, *refs):
+    sum_refs, mixer_ref = refs[:-1], refs[-1]
+
     @pl.when(pl.program_id(0) == 0)
     def _():
-        segs, _, experts = route_ref.shape
-        columns = experts * rows
-        mix = (route_ref[:, 0, :].astype(jnp.float32) / (8.0 * experts)).astype(jnp.bfloat16)
-        pick = lax.broadcasted_iota(jnp.int32, (experts, columns), 1) // rows
-        pick = pick == lax.broadcasted_iota(jnp.int32, (experts, columns), 0)
-        pick = jnp.where(pick, 1.0, 0.0).astype(jnp.bfloat16)
-        wide = jnp.dot(mix, pick, preferred_element_type=jnp.float32)
-        same = lax.broadcasted_iota(jnp.int32, (rows, columns), 0)
-        same = same == lax.broadcasted_iota(jnp.int32, (rows, columns), 1) % rows
-        for s in range(segs):
-            line = jnp.broadcast_to(wide[s : s + 1, :], (rows, columns))
-            mixer_ref[s * rows : (s + 1) * rows, :] = jnp.where(same, line, 0.0).astype(jnp.bfloat16)
-
-    tile = sum_ref.shape[1]
-    here = pl.ds(pl.multiple_of(pl.program_id(0) * tile, tile), tile)
-    sum_ref[...] = jnp.dot(
-        mixer_ref[...], weight_ref[:, here], preferred_element_type=jnp.float32
-    ).astype(jnp.bfloat16)
-
-
-def mix_first(routes, weights):
+        mix = mix_of(route_ref)
+        segs = mix.shape[0]
+        if top:
+            line = lax.broadcasted_iota(jnp.int32, (segs, segs), 0)
+            apart = (line % top) * (segs // top) + line // top
+            chosen = lax.broadcasted_iota(jnp.int32, (segs, segs), 1) == (apart ^ me_ref[0])
+            chosen = jnp.where(chosen, 1.0, 0.0).astype(jnp.bfloat16)
+            mix = jnp.dot(chosen, mix, preferred_element_type=jnp.float32).astype(jnp.bfloat16)
+        spread(mix, rows, mixer_ref)
+
+    lines, tile = sum_refs[0].shape
+    weight = weight_ref
+    if resident:
+        here = pl.ds(pl.multiple_of(pl.program_id(0) * tile, tile), tile)
+        weight = weight_ref.at[:, here]
+    sums = jnp.dot(mixer_ref[...], weight[...], preferred_element_type=jnp.float32)
+    for i, sum_ref in enumerate(sum_refs):
+        sum_ref[...] = sums[i * lines : (i + 1) * lines, :].astype(jnp.bfloat16)
+
+
+def mix_call(me, routes, weights, parts, top, resident):
     segs = routes.shape[0]
     experts, rows, width = weights.shape
     tile = width // 4
+    lines = segs * rows // parts
+    weights = weights.reshape(experts * rows, width)
+    whole = pl.BlockSpec(memory_space=pltpu.VMEM)
+    if not resident:
+        weights = pltpu.with_memory_space_constraint(weights, pltpu.HBM)
     return pl.pallas_call(
-        functools.partial(mix_kernel, rows),
+        functools.partial(mix_kernel, rows, top, resident),
         grid=(width // tile,),
         in_specs=[
+            pl.BlockSpec(memory_space=pltpu.SMEM),
             pl.BlockSpec(routes.shape, lambda i: (0, 0, 0)),
-            pl.BlockSpec(memory_space=pltpu.VMEM),
+            whole if resident else pl.BlockSpec((experts * rows, tile), lambda i: (0, i)),
         ],
-        out_specs=[
-            pl.BlockSpec((segs * rows, tile), lambda i: (0, i)),
-            pl.BlockSpec((segs * rows, experts * rows), lambda i: (0, 0)),
-        ],
-        out_shape=[
-            pltpu.HBM((segs * rows, width), jnp.bfloat16),
-            jax.ShapeDtypeStruct((segs * rows, experts * rows), jnp.bfloat16),
-        ],
+        out_specs=[pl.BlockSpec((lines, tile), lambda i: (0, i))] * parts,
+        out_shape=[pltpu.HBM((lines, width), jnp.bfloat16)] * parts,
+        scratch_shapes=[pltpu.VMEM((segs * rows, experts * rows), jnp.bfloat16)],
         compiler_params=pltpu.CompilerParams(vmem_limit_bytes=12 << 20),
-        name="mix_first",
-    )(routes, weights.reshape(experts * rows, width))
+        name="mix",
+    )(me, routes, weights)
+
+
+def turn_kernel(rows, route_ref, out_ref):
+    spread(mix_of(route_ref).astype(jnp.float32).T.astype(jnp.bfloat16), rows, out_ref)
+
+
+def turn(routes, rows):
+    segs, _, experts = routes.shape
+    return pl.pallas_call(
+        functools.partial(turn_kernel, rows),
+        out_shape=jax.ShapeDtypeStruct((experts * rows, segs * rows), jnp.bfloat16),
+        compiler_params=pltpu.CompilerParams(vmem_limit_bytes=8 << 20),
+        name="turn",
+    )(routes)
+
+
+def in_hbm(*arrays):
+    return [pltpu.with_memory_space_constraint(array, pltpu.HBM) for array in arrays]
+
+
+def copy_all(copies):
+    for copy in copies:
+        copy.start()
+    for copy in copies:
+        copy.wait()
+
+
+def regroup_kernel(low, top, rows, *refs):
+    plane, send, sems = refs[:low], refs[low : low + top - 1], refs[low + top - 1]
+    copy_all(
+        [
+            pltpu.make_async_copy(
+                plane[k].at[pl.ds(z * rows, rows), :],
+                send[z - 1].at[pl.ds(k * rows, rows), :],
+                sems.at[k, z - 1],
+            )
+            for z in range(1, top)
+            for k in range(low)
+        ]
+    )
+
+
+def settle_kernel(low, top, rows, me_ref, *refs):
+    plane, got, out_ref, sems = refs[:low], refs[low : low + top - 1], refs[-2], refs[-1]
+    copies = []
+    for z in range(top):
+        for k in range(low):
+            source = plane[k].at[pl.ds(0, rows), :]
+            if z:
+                source = got[z - 1].at[pl.ds(k * rows, rows), :]
+            place = pl.multiple_of((me_ref[0] ^ (z * low + k)) * rows, rows)
+            copies.append(
+                pltpu.make_async_copy(source, out_ref.at[pl.ds(place, rows), :], sems.at[k, z])
+            )
+    copy_all(copies)
+
+
+def by_permutes(me, parts, segs, rows, top):
+    low = segs // top
+    width = parts[0].shape[1]
+    hbm, free = pl.BlockSpec(memory_space=pltpu.HBM), pl.BlockSpec(memory_space=pl.ANY)
+
+    def swap(block, apart):
+        return lax.ppermute(block, "seg", [(i, i ^ apart) for i in range(segs)])
+
+    plane = [parts[0]] + [swap(parts[k], k) for k in range(1, low)]
+    send = pl.pallas_call(
+        functools.partial(regroup_kernel, low, top, rows),
+        in_specs=[hbm] + [free] * (low - 1),
+        out_specs=[hbm] * (top - 1),
+        out_shape=[pltpu.HBM((low * rows, width), jnp.bfloat16)] * (top - 1),
+        scratch_shapes=[pltpu.SemaphoreType.DMA((low, top - 1))],
+        compiler_params=pltpu.CompilerParams(vmem_limit_bytes=1 << 20),
+        name="regroup",
+    )(*in_hbm(plane[0]), *plane[1:])
+    got = [swap(send[z - 1], z * low) for z in range(1, top)]
+    return pl.pallas_call(
+        functools.partial(settle_kernel, low, top, rows),
+        in_specs=[pl.BlockSpec(memory_space=pltpu.SMEM), hbm] + [free] * (low + top - 2),
+        out_specs=hbm,
+        out_shape=pltpu.HBM((segs * rows, width), jnp.bfloat16),
+        scratch_shapes=[pltpu.SemaphoreType.DMA((low, top))],
+        compiler_params=pltpu.CompilerParams(vmem_limit_bytes=1 << 20),
+        name="settle",
+    )(me, *in_hbm(plane[0]), *plane[1:], *got)
 
 
 def fetch_kernel(count, *refs):
@@ -157,7 +265,7 @@
     return lax.all_to_all(blocks, "seg", split_axis=0, concat_axis=0, tiled=True)
 
 
-def body(tokens, cotangent, routing, w_up, w_down, momentum_up, momentum_down):
+def step(tokens, cotangent, routing, w_up, w_down, momentum_up, momentum_down):
     group_count = lax.axis_size("grp")
     seg_count = lax.axis_size("seg")
     group_index = lax.axis_index("grp")
@@ -166,8 +274,9 @@
     hidden = seg_count * slice_rows
 
     routes = exchange(jnp.broadcast_to(routing[:, None, :], (seg_count, 1, experts)))
+    me = lax.axis_index("seg").astype(jnp.int32)[None]
     (early_up,) = fetch(w_up)
-    first, mixer = mix_first(routes, early_up)
+    first = mix_call(me, routes, early_up, 1, 0, True)[0]
 
     def delivered(sums):
         return exchange(sums.reshape(seg_count, slice_rows, width)).reshape(hidden, width)
@@ -175,7 +284,7 @@
     def returned(grads):
         return delivered(grads.astype(jnp.bfloat16))
 
-    turned = mixer.T
+    turned = turn(routes, slice_rows)
 
     def updated(weights, momentum, grads):
         part = jnp.dot(turned, grads, preferred_element_type=jnp.float32)
@@ -192,23 +301,24 @@
     inputs = tokens[0]
     grads = cotangent[0]
     up = delivered(first)
-    flat_down = w_down.reshape(experts * slice_rows, width)
-    second = jnp.dot(mixer, flat_down, preferred_element_type=jnp.float32)
-    down = delivered(second.astype(jnp.bfloat16))
-    pre = lax.dot_general(
-        inputs, up, (((1,), (1,)), ((), ())), preferred_element_type=jnp.float32
-    )
+    top = TOP if seg_count % TOP == 0 and seg_count & (seg_count - 1) == 0 else 0
+    if top:
+        parts = mix_call(me, routes, w_down, seg_count // top, top, False)
+        down = by_permutes(me, parts, seg_count, slice_rows, top)
+    else:
+        down = delivered(mix_call(me, routes, w_down, 1, 0, False)[0])
+    pre = lax.dot_general(inputs, up, (((1,), (1,)), ((), ())), preferred_element_type=jnp.float32)
     act_full, slope = gelu_parts(pre)
     act = act_full.astype(jnp.bfloat16)
     grad_down = returned(
-        lax.dot_general(act, grads, (((0,), (0,)), ((), ())), preferred_element_type=jnp.float32)
+        lax.dot_general(act, grads, (((0,), (0,)), ((), ())), preferred_element_type=jnp.float32),
     )
     d_act = lax.dot_general(
         grads, down, (((1,), (1,)), ((), ())), preferred_element_type=jnp.float32
     )
     d_pre = (d_act * slope).astype(jnp.bfloat16)
     grad_up = returned(
-        lax.dot_general(d_pre, inputs, (((0,), (0,)), ((), ())), preferred_element_type=jnp.float32)
+        lax.dot_general(d_pre, inputs, (((0,), (0,)), ((), ())), preferred_element_type=jnp.float32),
     )
     new_momentum_down, new_down = updated(w_down, momentum_down, grad_down)
     act, d_pre, new_momentum_down, new_down = lax.optimization_barrier(
@@ -243,4 +353,4 @@
         P("grp", "seg", None),
         P("grp", "seg", None),
     )
-    return jax.shard_map(body, mesh=mesh, in_specs=in_specs, out_specs=out_specs, check_vma=False)
+    return jax.shard_map(step, mesh=mesh, in_specs=in_specs, out_specs=out_specs, check_vma=False)

time: 145 us -> 168 us (1.16)
  starting transfers between devices: 21.2 us -> 33.7 us
  matrix products: 40.7 us -> 29.6 us
  Pallas kernels: 12.7 us -> 23.2 us
  waiting for transfers between devices: 64.5 us -> 70.4 us
  other arithmetic: 0 us -> 4.07 us
    ppermute x0 -> x10, waiting for transfers between devices: none -> 37.3 us  [swap(): return lax.ppermute(block, 'seg', [(i, i ^ apart) for i in range(segs)])]
    all_to_all x5 -> x4, waiting for transfers between devices: 64.5 us -> 33.1 us  [exchange(): lax.all_to_all(blocks, 'seg', split_axis=0, concat_axis=0, tiled=True)]
    ppermute x0 -> x10, starting transfers between devices: none -> 12.2 us  [swap(): return lax.ppermute(block, 'seg', [(i, i ^ apart) for i in range(segs)])]
    pallas_call x1 -> x5, Pallas kernels: 3.09 us -> 14.9 us  [the longest x2 7.78 us: mix_call(): pl.pallas_call(functools.partial(mix_kernel, rows, top, resident), grid=(...]
    dot_general x1, matrix products: 7.17 us -> 1.26 us  [updated(): part = jnp.dot(turned, grads, preferred_element_type=jnp.float32)]
    dot_general x7 -> x6, matrix products: 33.5 us -> 28.3 us  [the longest x1 6.65 us: step(): lax.dot_general(inputs, up, (((1,), (1,)), ((), ())), preferred_element_t...]
    convert_element_type x0 -> x1, other arithmetic: none -> 4.07 us  [updated(): (weights.astype(jnp.float32) - 0.01 * new_momentum).astype(jnp.bfloat16)]
    unnamed x16 -> x32, local copies, waits for them, and re-layouts: 2.66 us -> 4.49 us
  transfers between devices with their start and end apart: 5 -> 14, of which waited for: 5 -> 8; matrix products, arithmetic and copies ran while one was open for 29% -> 20% of each run, Pallas kernels for 2% -> 9%
where the time goes in v3:
time: 168 us
  waiting for transfers between devices  70.4 us (42%)
  starting transfers between devices  33.7 us (20%)
  matrix products  29.6 us (18%)
  Pallas kernels  23.2 us (14%)
  local copies, waits for them, and re-layouts  5.76 us (3%)
  other arithmetic  4.07 us (2%)
    ppermute x10, waiting for transfers between devices, swap(): return lax.ppermute(block, 'seg', [(i, i ^ apart) for i in range(segs)])  37.3 us
    all_to_all x4, waiting for transfers between devices, exchange(): lax.all_to_all(blocks, 'seg', split_axis=0, concat_axis=0, tiled=True)  33.1 us
    all_to_all x4, starting transfers between devices, exchange(): lax.all_to_all(blocks, 'seg', split_axis=0, concat_axis=0, tiled=True)  21.5 us
    ppermute x10, starting transfers between devices, swap(): return lax.ppermute(block, 'seg', [(i, i ^ apart) for i in range(segs)])  12.2 us
    pallas_call x2, Pallas kernels, mix_call(): pl.pallas_call(functools.partial(mix_kernel, rows, top, resident), grid=(...  7.78 us
    dot_general x1, matrix products, step(): lax.dot_general(inputs, up, (((1,), (1,)), ((), ())), preferred_element_t...  6.65 us
    dot_general x1, matrix products, step(): lax.dot_general(grads, down, (((1,), (1,)), ((), ())), preferred_element_...  6.2 us
    pallas_call x1, Pallas kernels, update_last(): pl.pallas_call(functools.partial(update_kernel, count), in_specs=[vmem, v...  5.13 us
  transfers between devices with their start and end apart: 14, of which 8 were waited for; matrix products, arithmetic and copies ran while one was open for 20% of the time, Pallas kernels for 9%

profile of v3, /device:TPU:0, one launch (start us, length us, event | category | flops | bytes accessed | tf_op | source)
XLA Modules:
  0.0 167.8 jit_solution(11992627980710131606)
XLA Ops:
  0.6 1.3 broadcast_in_dim.19
  1.9 7.3 %all-to-all-start = ((s32[32,1,64]{2,1,0:T(1,128)}), s32[32,1,64]{2,1,0:T(1,128)S(1)}, u32[]{:S(2)}, u32[]{:S(2)}) async-start(s32[32,1,64]{2,1,0:T(1,128)} %broadcast_in_dim.19), calls=%async_computation | async-start | bytes 32768 | tf_op jit(solution)/shard_map/all_to_all | solution.py:265
  9.2 1.6 fetch.2
  10.8 5.5 %all-to-all-done.route_ref = s32[32,1,64]{2,1,0:T(1,128)S(1)} async-done(((s32[32,1,64]{2,1,0:T(1,128)}), s32[32,1,64]{2,1,0:T(1,128)S(1)}, u32[]{:S(2)}, u32[]{:S(2)}) %all-to-all-start) | async-done | bytes 8224 | tf_op jit(solution)/shard_map/all_to_all | solution.py:265
  16.3 3.1 %mix.2 = bf16[512,1024]{1,0:T(8,128)(2,1)} custom-call(s32[1]{0:T(128)} %bitcast.me_ref, s32[32,1,64]{2,1,0:T(1,128)S(1)} %all-to-all-done.route_ref, bf16[1024,1024]{1,0:T(8,128)(2,1)S(1)} %bitcast.65), custom_call_target="tpu_custom_call" | custom-call | tf_op jit(solution)/shard_map/mix/pallas_call | solution.py:76
  19.4 2.6 %all-to-all-start.1 = ((bf16[32,16,1024]{2,1,0:T(8,128)(2,1)}), bf16[32,16,1024]{2,1,0:T(8,128)(2,1)S(1)}, u32[]{:S(2)}, u32[]{:S(2)}) async-start(bf16[32,16,1024]{2,1,0:T(8,128)(2,1)} %bitcast.70), calls=%async_computation.1 | async-start | bytes 2097152 | tf_op jit(solution)/shard_map/all_to_all | solution.py:265
  22.1 4.7 %mix.3 = (bf16[64,1024]{1,0:T(8,128)(2,1)}, bf16[64,1024]{1,0:T(8,128)(2,1)}, bf16[64,1024]{1,0:T(8,128)(2,1)}, bf16[64,1024]{1,0:T(8,128)(2,1)}, bf16[64,1024]{...) custom-call(s32[1]{0:T(128)} %bitcast.me_ref, ...), custom_call_target="tpu_custom_call" | custom-call | tf_op jit(solution)/shard_map/mix/pallas_call | solution.py:76
  26.8 0.2 collective-permute-start
  26.9 1.6 collective-permute-start.1
  28.6 19.7 %all-to-all-done.1 = bf16[32,16,1024]{2,1,0:T(8,128)(2,1)S(1)} async-done(((bf16[32,16,1024]{2,1,0:T(8,128)(2,1)}), bf16[32,16,1024]{2,1,0:T(8,128)(2,1)S(1)}, u32[]{:S(2)}, u32[]{:S(2)}) %all-to-all-start.1) | async-done | bytes 1048608 | tf_op jit(solution)/shard_map/all_to_all | solution.py:265
  48.3 6.6 %fusion.11 = (bf16[2048,512]{0,1:T(8,128)(2,1)S(1)}, f32[512,2048]{1,0:T(8,128)}) fusion(bf16[512,1024]{1,0:T(8,128)(2,1)S(1)} %bitcast.72, bf16[1,2048,1024]{2,1,0:T(8,128)(2,1)} %param.7), kind=kOutput, calls=%fused_computation.14 | convolution fusion | flops 2152726528 | bytes 11534336 | tf_op jit(solution)/shard_map/dot_general | solution.py:310
  54.9 0.0 copy-done.5
  54.9 0.0 copy-start.9
  55.0 0.0 copy-start.8
  55.0 0.0 copy-start.7
  55.0 3.3 %fusion.23 = bf16[512,1024]{1,0:T(8,128)(2,1)} fusion(bf16[2048,512]{0,1:T(8,128)(2,1)S(1)} %get-tuple-element.37, bf16[1,2048,1024]{2,1,0:T(8,128)(2,1)S(1)} %copy-done.5), kind=kOutput, calls=%fused_computation.26 | convolution fusion | flops 2148007936 | bytes 7340032 | tf_op jit(solution)/shard_map/dot_general | solution.py:314
  58.3 0.0 copy-done.12
  58.3 3.5 %all-to-all-start.2 = ((bf16[32,16,1024]{2,1,0:T(8,128)(2,1)}), bf16[32,16,1024]{2,1,0:T(8,128)(2,1)S(1)}, u32[]{:S(2)}, u32[]{:S(2)}) async-start(bf16[32,16,1024]{2,1,0:T(8,128)(2,1)} %bitcast.75), calls=%async_computation.2 | async-start | bytes 2097152 | tf_op jit(solution)/shard_map/all_to_all | solution.py:265
  61.9 0.0 copy-done.11
  61.9 1.6 collective-permute-start.2
  63.4 0.0 copy-done.10
  63.4 1.5 collective-permute-start.3
  64.9 0.0 copy-done.9
  64.9 0.3 collective-permute-start.4
  65.2 0.0 collective-permute-done.refs_1_
  65.2 0.0 copy-done.8
  65.2 1.5 collective-permute-start.5
  66.6 0.0 collective-permute-done.1.refs_2_
  66.6 1.2 collective-permute-start.6
  67.8 6.2 %collective-permute-done.2.refs_3_ = bf16[64,1024]{1,0:T(8,128)(2,1)S(1)} collective-permute-done((bf16[64,1024]{1,0:T(8,128)(2,1)S(1)}, bf16[64,1024]{1,0:T(8,128)(2,1)S(1)}, u32[]{:S(2)}, u32[]{:S(2)}) %collective-permute-start.2) | collective-permute-done | bytes 131104 | tf_op jit(solution)/shard_map/ppermute | solution.py:153
  74.0 0.5 collective-permute-done.3.refs_4_
  74.5 12.0 %collective-permute-done.4.refs_5_ = bf16[64,1024]{1,0:T(8,128)(2,1)S(1)} collective-permute-done((bf16[64,1024]{1,0:T(8,128)(2,1)S(1)}, bf16[64,1024]{1,0:T(8,128)(2,1)S(1)}, u32[]{:S(2)}, u32[]{:S(2)}) %collective-permute-start.4) | collective-permute-done | bytes 131104 | tf_op jit(solution)/shard_map/ppermute | solution.py:153
  86.5 0.0 collective-permute-done.5.refs_6_
  86.5 0.0 collective-permute-done.6.refs_7_
  86.5 4.3 %regroup.1 = (bf16[128,1024]{1,0:T(8,128)(2,1)}, bf16[128,1024]{1,0:T(8,128)(2,1)}, bf16[128,1024]{1,0:T(8,128)(2,1)}) custom-call(bf16[64,1024]{1,0:T(8,128)(2,1)} %get-tuple-element.26.refs_0_, bf16[64,1024]{1,0:T(8,128)(2,1)S(1)} %collective-permute-done.refs_1_, bf16[64,1024]{1,0:T(8,128)(2,1)S(1)} %collective-permute-done.1.refs_2_, ...), custom_call_target="tpu_custom_call" | custom-call | tf_op jit(solution)/shard_map/regroup/pallas_call | solution.py:156
  90.9 1.5 collective-permute-start.7
  92.4 2.8 %collective-permute-start.8 = (bf16[128,1024]{1,0:T(8,128)(2,1)}, bf16[128,1024]{1,0:T(8,128)(2,1)S(1)}, u32[]{:S(2)}, u32[]{:S(2)}) collective-permute-start(bf16[128,1024]{1,0:T(8,128)(2,1)} %get-tuple-element.35), channel_id=1, source_target_pairs={{0,16},{1,17},{2,18},{3,19},{4,20},{5,21},{6,22},{7,23},{8,24},{9,... | collective-permute-start | bytes 786440 | tf_op jit(solution)/shard_map/ppermute | solution.py:153
  95.2 0.2 collective-permute-start.9
  95.3 9.3 %collective-permute-done.7.refs_8_ = bf16[128,1024]{1,0:T(8,128)(2,1)S(1)} collective-permute-done((bf16[128,1024]{1,0:T(8,128)(2,1)}, bf16[128,1024]{1,0:T(8,128)(2,1)S(1)}, u32[]{:S(2)}, u32[]{:S(2)}) %collective-permute-start.7) | collective-permute-done | bytes 262176 | tf_op jit(solution)/shard_map/ppermute | solution.py:153
  104.6 9.3 %collective-permute-done.8.refs_9_ = bf16[128,1024]{1,0:T(8,128)(2,1)S(1)} collective-permute-done((bf16[128,1024]{1,0:T(8,128)(2,1)}, bf16[128,1024]{1,0:T(8,128)(2,1)S(1)}, u32[]{:S(2)}, u32[]{:S(2)}) %collective-permute-start.8) | collective-permute-done | bytes 262176 | tf_op jit(solution)/shard_map/ppermute | solution.py:153
  113.9 0.0 collective-permute-done.9.refs_10_
  113.9 2.4 %settle.1 = bf16[512,1024]{1,0:T(8,128)(2,1)} custom-call(s32[1]{0:T(128)} %bitcast.me_ref, bf16[64,1024]{1,0:T(8,128)(2,1)} %get-tuple-element.26.refs_0_, bf16[64,1024]{1,0:T(8,128)(2,1)S(1)} %collective-permute-done.refs_1_, bf16[64,1024]{1,0:T(8,128)(2,1)S(1)} %collective-permute-done.1.refs_2_, bf16[64,1024]{1,0:T(8,128)(2,1)S(1)} %collective-permute-done.2.refs_3_, ...), custom_call_target="tpu_custom_call" | custom-call | tf_op jit(solution)/shard_map/settle/pallas_call | solution.py:166
  116.4 0.0 copy-start.6
  116.4 6.2 %fusion.5 = bf16[2048,512]{0,1:T(8,128)(2,1)S(1)} fusion(f32[512,2048]{1,0:T(8,128)} %get-tuple-element.49, bf16[512,1024]{1,0:T(8,128)(2,1)} %settle.1, bf16[1,2048,1024]{2,1,0:T(8,128)(2,1)} %param.8), kind=kOutput, calls=%fused_computation.6 | convolution fusion | flops 2157969408 | bytes 11534336 | tf_op jit(solution)/shard_map/dot_general | solution.py:316
  122.6 0.0 copy-start.14
  122.6 1.3 copy-done.14
  123.9 3.3 %fusion.20 = bf16[512,1024]{1,0:T(8,128)(2,1)} fusion(bf16[2048,512]{0,1:T(8,128)(2,1)S(1)} %fusion.5, bf16[1,2048,1024]{2,1,0:T(8,128)(2,1)S(1)} %copy-done.6), kind=kOutput, calls=%fused_computation.25 | convolution fusion | flops 2148007936 | bytes 7340032 | tf_op jit(solution)/shard_map/dot_general | solution.py:321
  127.2 0.0 all-to-all-done.2
  127.2 8.0 %all-to-all-start.3 = ((bf16[32,16,1024]{2,1,0:T(8,128)(2,1)}), bf16[32,16,1024]{2,1,0:T(8,128)(2,1)S(1)}, u32[]{:S(2)}, u32[]{:S(2)}) async-start(bf16[32,16,1024]{2,1,0:T(8,128)(2,1)} %bitcast.76), calls=%async_computation.3 | async-start | bytes 2097152 | tf_op jit(solution)/shard_map/all_to_all | solution.py:265
  135.2 0.4 turn.1.mixer_ref
  135.6 0.0 copy-start.2
  135.6 0.0 copy-start.3
  135.6 1.3 fusion.26
  136.9 0.0 copy-done
  136.9 0.7 copy-done.2
  137.6 1.2 copy-done.3
  138.8 4.1 %subtract_convert_fusion = (bf16[64,16,1024]{2,1,0:T(8,128)(2,1)}, f32[64,16,1024]{2,1,0:T(8,128)}) fusion(bf16[64,16,1024]{2,1,0:T(8,128)(2,1)S(1)} %copy-done.2, f32[64,16,1024]{2,1,0:T(8,128)S(1)} %bitcast.71, f32[64,16,1024]{2,1,0:T(8,128)S(1)} %copy-done.3), kind=kLoop, calls=%fused_computation.21 | loop fusion | flops 6291456 | bytes 16777216 | tf_op jit(solution)/shard_map/convert_element_type | solution.py:298
  142.9 0.0 copy-done.4
  142.9 4.4 %convolution_convert_fusion.1 = bf16[2048,1024]{1,0:T(8,128)(2,1)} fusion(bf16[2048,512]{0,1:T(8,128)(2,1)S(1)} %copy-done.13, bf16[512,1024]{1,0:T(8,128)(2,1)S(1)} %copy-done.4), kind=kOutput, calls=%fused_computation.24 | convolution fusion | flops 2149580800 | bytes 7340032 | tf_op jit(solution)/shard_map/dot_general | solution.py:327
  147.3 4.4 %convolution_convert_fusion = bf16[2048,1024]{1,0:T(8,128)(2,1)} fusion(bf16[2048,512]{0,1:T(8,128)(2,1)S(1)} %copy-done.15, bf16[512,1024]{1,0:T(8,128)(2,1)S(1)} %bitcast.73), kind=kOutput, calls=%fused_computation.23 | convolution fusion | flops 2149580800 | bytes 7340032 | tf_op jit(solution)/shard_map/dot_general | solution.py:328
  151.7 1.6 fetch.3
  153.3 7.9 %all-to-all-done.3 = bf16[32,16,1024]{2,1,0:T(8,128)(2,1)S(1)} async-done(((bf16[32,16,1024]{2,1,0:T(8,128)(2,1)}), bf16[32,16,1024]{2,1,0:T(8,128)(2,1)S(1)}, u32[]{:S(2)}, u32[]{:S(2)}) %all-to-all-start.3) | async-done | bytes 1048608 | tf_op jit(solution)/shard_map/all_to_all | solution.py:265
  161.2 1.2 copy-done.1
  162.5 5.1 %update_last.1 = (f32[1024,1024]{1,0:T(8,128)}, bf16[1024,1024]{1,0:T(8,128)(2,1)}) custom-call(bf16[1024,512]{1,0:T(8,128)(2,1)S(1)} %copy-done.1, bf16[1024,1024]{1,0:T(8,128)(2,1)S(1)} %bitcast.66, bf16[512,1024]{1,0:T(8,128)(2,1)S(1)} %bitcast.67, f32[1024,1024]{1,0:T(8,128)} %bitcast.69), custom_call_target="tpu_custom_call" | custom-call | tf_op jit(solution)/shard_map/update_last/pallas_call | solution.py:242
  (13 shorter events, 0.0 us)
Async XLA Ops:
  1.9 14.4 %all-to-all-start = ((s32[32,1,64]{2,1,0:T(1,128)}), s32[32,1,64]{2,1,0:T(1,128)S(1)}, u32[]{:S(2)}, u32[]{:S(2)}) async-start(s32[32,1,64]{2,1,0:T(1,128)} %broadcast_in_dim.19), calls=%async_computation | async-start | bytes 32768 | tf_op jit(solution)/shard_map/all_to_all | solution.py:265
  19.4 28.8 %all-to-all-start.1 = ((bf16[32,16,1024]{2,1,0:T(8,128)(2,1)}), bf16[32,16,1024]{2,1,0:T(8,128)(2,1)S(1)}, u32[]{:S(2)}, u32[]{:S(2)}) async-start(bf16[32,16,1024]{2,1,0:T(8,128)(2,1)} %bitcast.70), calls=%async_computation.1 | async-start | bytes 2097152 | tf_op jit(solution)/shard_map/all_to_all | solution.py:265
  26.8 38.4 %collective-permute-start = (bf16[64,1024]{1,0:T(8,128)(2,1)}, bf16[64,1024]{1,0:T(8,128)(2,1)S(1)}, u32[]{:S(2)}, u32[]{:S(2)}) collective-permute-start(bf16[64,1024]{1,0:T(8,128)(2,1)} %get-tuple-element.27), channel_id=1, source_target_pairs={{0,1},{1,0},{2,3},{3,2},{4,5},{5,4},{6,7},{7,6},{8,9},{9,8},{10,11... | collective-permute-start | bytes 393224 | tf_op jit(solution)/shard_map/ppermute | solution.py:153
  26.9 39.7 %collective-permute-start.1 = (bf16[64,1024]{1,0:T(8,128)(2,1)}, bf16[64,1024]{1,0:T(8,128)(2,1)S(1)}, u32[]{:S(2)}, u32[]{:S(2)}) collective-permute-start(bf16[64,1024]{1,0:T(8,128)(2,1)} %get-tuple-element.28), channel_id=1, source_target_pairs={{0,2},{1,3},{2,0},{3,1},{4,6},{5,7},{6,4},{7,5},{8,10},{9,11},{10,... | collective-permute-start | bytes 393224 | tf_op jit(solution)/shard_map/ppermute | solution.py:153
  48.3 6.7 %copy-start.5 = (bf16[1,2048,1024]{2,1,0:T(8,128)(2,1)S(1)}, bf16[1,2048,1024]{2,1,0:T(8,128)(2,1)}, u32[]{:S(2)}) copy-start(bf16[1,2048,1024]{2,1,0:T(8,128)(2,1)} %param.8) | copy-start | bytes 12582916
  54.9 3.4 %copy-start.12 = (bf16[2048,512]{0,1:T(8,128)(2,1)}, bf16[2048,512]{0,1:T(8,128)(2,1)S(1)}, u32[]{:S(2)}) copy-start(bf16[2048,512]{0,1:T(8,128)(2,1)S(1)} %get-tuple-element.37) | copy-start | bytes 6291460
  54.9 6.9 %copy-start.11 = (bf16[64,1024]{1,0:T(8,128)(2,1)S(1)}, bf16[64,1024]{1,0:T(8,128)(2,1)}, u32[]{:S(2)}) copy-start(bf16[64,1024]{1,0:T(8,128)(2,1)} %get-tuple-element.29) | copy-start | bytes 393220
  54.9 8.5 %copy-start.10 = (bf16[64,1024]{1,0:T(8,128)(2,1)S(1)}, bf16[64,1024]{1,0:T(8,128)(2,1)}, u32[]{:S(2)}) copy-start(bf16[64,1024]{1,0:T(8,128)(2,1)} %get-tuple-element.30) | copy-start | bytes 393220
  54.9 9.9 %copy-start.9 = (bf16[64,1024]{1,0:T(8,128)(2,1)S(1)}, bf16[64,1024]{1,0:T(8,128)(2,1)}, u32[]{:S(2)}) copy-start(bf16[64,1024]{1,0:T(8,128)(2,1)} %get-tuple-element.31) | copy-start | bytes 393220
  55.0 10.2 %copy-start.8 = (bf16[64,1024]{1,0:T(8,128)(2,1)S(1)}, bf16[64,1024]{1,0:T(8,128)(2,1)}, u32[]{:S(2)}) copy-start(bf16[64,1024]{1,0:T(8,128)(2,1)} %get-tuple-element.32) | copy-start | bytes 393220
  55.0 11.7 %copy-start.7 = (bf16[64,1024]{1,0:T(8,128)(2,1)S(1)}, bf16[64,1024]{1,0:T(8,128)(2,1)}, u32[]{:S(2)}) copy-start(bf16[64,1024]{1,0:T(8,128)(2,1)} %get-tuple-element.33) | copy-start | bytes 393220
  58.3 68.9 %all-to-all-start.2 = ((bf16[32,16,1024]{2,1,0:T(8,128)(2,1)}), bf16[32,16,1024]{2,1,0:T(8,128)(2,1)S(1)}, u32[]{:S(2)}, u32[]{:S(2)}) async-start(bf16[32,16,1024]{2,1,0:T(8,128)(2,1)} %bitcast.75), calls=%async_computation.2 | async-start | bytes 2097152 | tf_op jit(solution)/shard_map/all_to_all | solution.py:265
  61.9 12.2 %collective-permute-start.2 = (bf16[64,1024]{1,0:T(8,128)(2,1)S(1)}, bf16[64,1024]{1,0:T(8,128)(2,1)S(1)}, u32[]{:S(2)}, u32[]{:S(2)}) collective-permute-start(bf16[64,1024]{1,0:T(8,128)(2,1)S(1)} %copy-done.11), channel_id=1, source_target_pairs={{0,3},{1,2},{2,1},{3,0},{4,7},{5,6},{6,5},{7,4},{8,11},{9,10},{10,... | collective-permute-start | bytes 393224 | tf_op jit(solution)/shard_map/ppermute | solution.py:153
  63.4 11.1 %collective-permute-start.3 = (bf16[64,1024]{1,0:T(8,128)(2,1)S(1)}, bf16[64,1024]{1,0:T(8,128)(2,1)S(1)}, u32[]{:S(2)}, u32[]{:S(2)}) collective-permute-start(bf16[64,1024]{1,0:T(8,128)(2,1)S(1)} %copy-done.10), channel_id=1, source_target_pairs={{0,4},{1,5},{2,6},{3,7},{4,0},{5,1},{6,2},{7,3},{8,12},{9,13},{10,... | collective-permute-start | bytes 393224 | tf_op jit(solution)/shard_map/ppermute | solution.py:153
  64.9 21.7 %collective-permute-start.4 = (bf16[64,1024]{1,0:T(8,128)(2,1)S(1)}, bf16[64,1024]{1,0:T(8,128)(2,1)S(1)}, u32[]{:S(2)}, u32[]{:S(2)}) collective-permute-start(bf16[64,1024]{1,0:T(8,128)(2,1)S(1)} %copy-done.9), channel_id=1, source_target_pairs={{0,5},{1,4},{2,7},{3,6},{4,1},{5,0},{6,3},{7,2},{8,13},{9,12},{10,... | collective-permute-start | bytes 393224 | tf_op jit(solution)/shard_map/ppermute | solution.py:153
  65.2 21.4 %collective-permute-start.5 = (bf16[64,1024]{1,0:T(8,128)(2,1)S(1)}, bf16[64,1024]{1,0:T(8,128)(2,1)S(1)}, u32[]{:S(2)}, u32[]{:S(2)}) collective-permute-start(bf16[64,1024]{1,0:T(8,128)(2,1)S(1)} %copy-done.8), channel_id=1, source_target_pairs={{0,6},{1,7},{2,4},{3,5},{4,2},{5,3},{6,0},{7,1},{8,14},{9,15},{10,... | collective-permute-start | bytes 393224 | tf_op jit(solution)/shard_map/ppermute | solution.py:153
  66.6 19.9 %collective-permute-start.6 = (bf16[64,1024]{1,0:T(8,128)(2,1)S(1)}, bf16[64,1024]{1,0:T(8,128)(2,1)S(1)}, u32[]{:S(2)}, u32[]{:S(2)}) collective-permute-start(bf16[64,1024]{1,0:T(8,128)(2,1)S(1)} %copy-done.7), channel_id=1, source_target_pairs={{0,7},{1,6},{2,5},{3,4},{4,3},{5,2},{6,1},{7,0},{8,15},{9,14},{10,... | collective-permute-start | bytes 393224 | tf_op jit(solution)/shard_map/ppermute | solution.py:153
  90.9 13.7 %collective-permute-start.7 = (bf16[128,1024]{1,0:T(8,128)(2,1)}, bf16[128,1024]{1,0:T(8,128)(2,1)S(1)}, u32[]{:S(2)}, u32[]{:S(2)}) collective-permute-start(bf16[128,1024]{1,0:T(8,128)(2,1)} %get-tuple-element.34), channel_id=1, source_target_pairs={{0,8},{1,9},{2,10},{3,11},{4,12},{5,13},{6,14},{7,15},{8,0},{9,1},... | collective-permute-start | bytes 786440 | tf_op jit(solution)/shard_map/ppermute | solution.py:153
  92.4 21.5 %collective-permute-start.8 = (bf16[128,1024]{1,0:T(8,128)(2,1)}, bf16[128,1024]{1,0:T(8,128)(2,1)S(1)}, u32[]{:S(2)}, u32[]{:S(2)}) collective-permute-start(bf16[128,1024]{1,0:T(8,128)(2,1)} %get-tuple-element.35), channel_id=1, source_target_pairs={{0,16},{1,17},{2,18},{3,19},{4,20},{5,21},{6,22},{7,23},{8,24},{9,... | collective-permute-start | bytes 786440 | tf_op jit(solution)/shard_map/ppermute | solution.py:153
  95.2 18.8 %collective-permute-start.9 = (bf16[128,1024]{1,0:T(8,128)(2,1)}, bf16[128,1024]{1,0:T(8,128)(2,1)S(1)}, u32[]{:S(2)}, u32[]{:S(2)}) collective-permute-start(bf16[128,1024]{1,0:T(8,128)(2,1)} %get-tuple-element.36), channel_id=1, source_target_pairs={{0,24},{1,25},{2,26},{3,27},{4,28},{5,29},{6,30},{7,31},{8,16},{9,... | collective-permute-start | bytes 786440 | tf_op jit(solution)/shard_map/ppermute | solution.py:153
  116.4 7.5 %copy-start.6 = (bf16[1,2048,1024]{2,1,0:T(8,128)(2,1)S(1)}, bf16[1,2048,1024]{2,1,0:T(8,128)(2,1)}, u32[]{:S(2)}) copy-start(bf16[1,2048,1024]{2,1,0:T(8,128)(2,1)} %param.7) | copy-start | bytes 12582916
  122.6 1.3 copy-start.14
  127.2 34.0 %all-to-all-start.3 = ((bf16[32,16,1024]{2,1,0:T(8,128)(2,1)}), bf16[32,16,1024]{2,1,0:T(8,128)(2,1)S(1)}, u32[]{:S(2)}, u32[]{:S(2)}) async-start(bf16[32,16,1024]{2,1,0:T(8,128)(2,1)} %bitcast.76), calls=%async_computation.3 | async-start | bytes 2097152 | tf_op jit(solution)/shard_map/all_to_all | solution.py:265
  135.6 1.3 copy-start
  135.6 2.0 %copy-start.2 = (bf16[64,16,1024]{2,1,0:T(8,128)(2,1)S(1)}, bf16[64,16,1024]{2,1,0:T(8,128)(2,1)}, u32[]{:S(2)}) copy-start(bf16[64,16,1024]{2,1,0:T(8,128)(2,1)} %param.11) | copy-start | bytes 6291460
  135.6 3.2 %copy-start.3 = (f32[64,16,1024]{2,1,0:T(8,128)S(1)}, f32[64,16,1024]{2,1,0:T(8,128)}, u32[]{:S(2)}) copy-start(f32[64,16,1024]{2,1,0:T(8,128)} %param.13) | copy-start | bytes 12582916
  138.8 4.1 %copy-start.4 = (bf16[512,1024]{1,0:T(8,128)(2,1)S(1)}, bf16[512,1024]{1,0:T(8,128)(2,1)}, u32[]{:S(2)}) copy-start(bf16[512,1024]{1,0:T(8,128)(2,1)} %settle.1) | copy-start | bytes 3145732
  138.8 4.1 %copy-start.13 = (bf16[2048,512]{0,1:T(8,128)(2,1)S(1)}, bf16[2048,512]{0,1:T(8,128)(2,1)}, u32[]{:S(2)}) copy-start(bf16[2048,512]{0,1:T(8,128)(2,1)} %copy-done.12) | copy-start | bytes 6291460
  142.9 4.4 %copy-start.15 = (bf16[2048,512]{0,1:T(8,128)(2,1)S(1)}, bf16[2048,512]{0,1:T(8,128)(2,1)}, u32[]{:S(2)}) copy-start(bf16[2048,512]{0,1:T(8,128)(2,1)} %copy-done.14) | copy-start | bytes 6291460
  161.2 1.2 copy-start.1

commit v4 on v3

--- a/solution.py
+++ b/solution.py
@@ -9,7 +9,7 @@
 
 
 PIECES = 4
-TOP = 4
+TOP = 8
 
 
 def gelu_parts(pre):
@@ -115,18 +115,10 @@
 
 
 def regroup_kernel(low, top, rows, *refs):
-    plane, send, sems = refs[:low], refs[low : low + top - 1], refs[low + top - 1]
-    copy_all(
-        [
-            pltpu.make_async_copy(
-                plane[k].at[pl.ds(z * rows, rows), :],
-                send[z - 1].at[pl.ds(k * rows, rows), :],
-                sems.at[k, z - 1],
-            )
-            for z in range(1, top)
-            for k in range(low)
-        ]
-    )
+    plane, send = refs[:low], refs[low:]
+    for z in range(1, top):
+        for k in range(low):
+            send[z - 1][k * rows : (k + 1) * rows, :] = plane[k][z * rows : (z + 1) * rows, :]
 
 
 def settle_kernel(low, top, rows, me_ref, *refs):
@@ -148,6 +140,7 @@
     low = segs // top
     width = parts[0].shape[1]
     hbm, free = pl.BlockSpec(memory_space=pltpu.HBM), pl.BlockSpec(memory_space=pl.ANY)
+    near = pl.BlockSpec(memory_space=pltpu.VMEM)
 
     def swap(block, apart):
         return lax.ppermute(block, "seg", [(i, i ^ apart) for i in range(segs)])
@@ -155,14 +148,13 @@
     plane = [parts[0]] + [swap(parts[k], k) for k in range(1, low)]
     send = pl.pallas_call(
         functools.partial(regroup_kernel, low, top, rows),
-        in_specs=[hbm] + [free] * (low - 1),
-        out_specs=[hbm] * (top - 1),
-        out_shape=[pltpu.HBM((low * rows, width), jnp.bfloat16)] * (top - 1),
-        scratch_shapes=[pltpu.SemaphoreType.DMA((low, top - 1))],
-        compiler_params=pltpu.CompilerParams(vmem_limit_bytes=1 << 20),
+        in_specs=[near] * low,
+        out_specs=[near] * (top - 1),
+        out_shape=[pltpu.VMEM((low * rows, width), jnp.bfloat16)] * (top - 1),
+        compiler_params=pltpu.CompilerParams(vmem_limit_bytes=4 << 20),
         name="regroup",
-    )(*in_hbm(plane[0]), *plane[1:])
-    got = [swap(send[z - 1], z * low) for z in range(1, top)]
+    )(*plane)
+    got = [swap(send[z - 1], z * low) for z in reversed(range(1, top))][::-1]
     return pl.pallas_call(
         functools.partial(settle_kernel, low, top, rows),
         in_specs=[pl.BlockSpec(memory_space=pltpu.SMEM), hbm] + [free] * (low + top - 2),
@@ -200,20 +192,18 @@
 
 
 def update_kernel(
-    count, mixer_ref, weight_ref, grad_hbm, momentum_hbm, new_momentum_hbm, new_hbm,
-    grad_ref, momentum_ref, new_ref, grad_sem, in_sems, out_sems,
+    count, rows, route_ref, grad_ref, weight_ref, momentum_hbm, new_momentum_hbm, new_hbm,
+    mixer_ref, momentum_ref, new_ref, in_sems, out_sems,
 ):
     lines = momentum_ref.shape[0] // count
     parts = [slice(i * lines, (i + 1) * lines) for i in range(count)]
-    first = pltpu.make_async_copy(grad_hbm, grad_ref, grad_sem)
-    first.start()
     reads = [
         pltpu.make_async_copy(momentum_hbm.at[here, :], momentum_ref.at[here, :], in_sems.at[i])
         for i, here in enumerate(parts)
     ]
     for read in reads:
         read.start()
-    first.wait()
+    turn_kernel(rows, route_ref, mixer_ref)
     writes = []
     for i, here in enumerate(parts):
         part = jnp.dot(mixer_ref[here, :], grad_ref[...], preferred_element_type=jnp.float32)
@@ -231,33 +221,32 @@
         write.wait()
 
 
-def update_last(mixer, grads, weights, momentum):
+def update_last(routes, grads, weights, momentum):
     experts, rows, width = weights.shape
     lines = experts * rows
     count = PIECES if experts % PIECES == 0 else 1
-    mixer = pltpu.with_memory_space_constraint(mixer, pltpu.VMEM)
     weights = pltpu.with_memory_space_constraint(weights.reshape(lines, width), pltpu.VMEM)
+    grads = pltpu.with_memory_space_constraint(grads, pltpu.VMEM)
     momentum = pltpu.with_memory_space_constraint(momentum.reshape(lines, width), pltpu.HBM)
     vmem, hbm = pl.BlockSpec(memory_space=pltpu.VMEM), pl.BlockSpec(memory_space=pltpu.HBM)
     new_momentum, new = pl.pallas_call(
-        functools.partial(update_kernel, count),
-        in_specs=[vmem, vmem, pl.BlockSpec(memory_space=pl.ANY), hbm],
+        functools.partial(update_kernel, count, rows),
+        in_specs=[vmem, vmem, vmem, hbm],
         out_specs=[hbm, hbm],
         out_shape=[
             jax.ShapeDtypeStruct((lines, width), jnp.float32),
             jax.ShapeDtypeStruct((lines, width), jnp.bfloat16),
         ],
         scratch_shapes=[
-            pltpu.VMEM(grads.shape, grads.dtype),
+            pltpu.VMEM((lines, grads.shape[0]), jnp.bfloat16),
             pltpu.VMEM((lines, width), jnp.float32),
             pltpu.VMEM((lines, width), jnp.bfloat16),
-            pltpu.SemaphoreType.DMA,
             pltpu.SemaphoreType.DMA((count,)),
             pltpu.SemaphoreType.DMA((count, 2)),
         ],
-        compiler_params=pltpu.CompilerParams(vmem_limit_bytes=12 << 20),
+        compiler_params=pltpu.CompilerParams(vmem_limit_bytes=14 << 20),
         name="update_last",
-    )(mixer, weights, grads, momentum)
+    )(routes, grads, weights, momentum)
     return new_momentum.reshape(experts, rows, width), new.reshape(experts, rows, width)
 
 
@@ -329,7 +318,7 @@
     layer_out, token_grad, late_up = lax.optimization_barrier((layer_out, token_grad, w_up))
     if group_count == 1:
         (late_up,) = fetch(late_up)
-        new_momentum_up, new_up = update_last(turned, grad_up, late_up, momentum_up)
+        new_momentum_up, new_up = update_last(routes, grad_up, late_up, momentum_up)
     else:
         new_momentum_up, new_up = updated(late_up, momentum_up, grad_up)
     return (layer_out[None], token_grad[None], new_momentum_up, new_momentum_down, new_up, new_down)

time: 168 us -> 159 us (0.946)
  waiting for transfers between devices: 70.4 us -> 61.1 us
  starting transfers between devices: 33.7 us -> 39.2 us
  Pallas kernels: 23.2 us -> 18.9 us
    ppermute x10, waiting for transfers between devices: 37.3 us -> 27.7 us  [swap(): return lax.ppermute(block, 'seg', [(i, i ^ apart) for i in range(segs)])]
    ppermute x10, starting transfers between devices: 12.2 us -> 18.6 us  [swap(): return lax.ppermute(block, 'seg', [(i, i ^ apart) for i in range(segs)])]
    pallas_call x1, Pallas kernels: 4.3 us -> 0.06 us  [by_permutes(): pl.pallas_call(functools.partial(regroup_kernel, low, top, rows), in_spec...]
    unnamed x32 -> x20, local copies, waits for them, and re-layouts: 4.49 us -> 2.89 us
  transfers between devices with their start and end apart: 14 -> 14, of which waited for: 8 -> 8; matrix products, arithmetic and copies ran while one was open for 20% -> 21% of each run, Pallas kernels for 9% -> 7%
where the time goes in v4:
time: 159 us; the launch traced here: 158 us
  waiting for transfers between devices  61.1 us (38%)
  starting transfers between devices  39.2 us (25%)
  matrix products  29.6 us (19%)
  Pallas kernels  18.9 us (12%)
  local copies, waits for them, and re-layouts  4.16 us (3%)
  other arithmetic  4.07 us (3%)
    all_to_all x4, waiting for transfers between devices, exchange(): lax.all_to_all(blocks, 'seg', split_axis=0, concat_axis=0, tiled=True)  33.4 us
    ppermute x10, waiting for transfers between devices, swap(): return lax.ppermute(block, 'seg', [(i, i ^ apart) for i in range(segs)])  27.7 us
    all_to_all x4, starting transfers between devices, exchange(): lax.all_to_all(blocks, 'seg', split_axis=0, concat_axis=0, tiled=True)  20.6 us
    ppermute x10, starting transfers between devices, swap(): return lax.ppermute(block, 'seg', [(i, i ^ apart) for i in range(segs)])  18.6 us
    pallas_call x2, Pallas kernels, mix_call(): pl.pallas_call(functools.partial(mix_kernel, rows, top, resident), grid=(...  7.81 us
    dot_general x1, matrix products, step(): lax.dot_general(inputs, up, (((1,), (1,)), ((), ())), preferred_element_t...  6.65 us
    dot_general x1, matrix products, step(): lax.dot_general(grads, down, (((1,), (1,)), ((), ())), preferred_element_...  6.19 us
    pallas_call x1, Pallas kernels, update_last(): pl.pallas_call(functools.partial(update_kernel, count, rows), in_specs=[v...  5.06 us
  transfers between devices with their start and end apart: 14, of which 8 were waited for; matrix products, arithmetic and copies ran while one was open for 21% of the time, Pallas kernels for 7%

profile of v4, /device:TPU:0, one launch (start us, length us, event | category | flops | bytes accessed | tf_op | source)
XLA Modules:
  0.0 158.0 jit_solution(16099850490896853176)
XLA Ops:
  0.6 1.3 broadcast_in_dim.19
  1.9 7.3 %all-to-all-start = ((s32[32,1,64]{2,1,0:T(1,128)}), s32[32,1,64]{2,1,0:T(1,128)S(1)}, u32[]{:S(2)}, u32[]{:S(2)}) async-start(s32[32,1,64]{2,1,0:T(1,128)} %broadcast_in_dim.19), calls=%async_computation | async-start | bytes 32768 | tf_op jit(solution)/shard_map/all_to_all | solution.py:254
  9.2 1.6 %fetch.2 = bf16[64,16,1024]{2,1,0:T(8,128)(2,1)S(1)} custom-call(bf16[64,16,1024]{2,1,0:T(8,128)(2,1)} %refs_0_.2), custom_call_target="tpu_custom_call" | custom-call | tf_op jit(solution)/shard_map/fetch/pallas_call | solution.py:183
  10.8 5.5 %all-to-all-done.route_ref = s32[32,1,64]{2,1,0:T(1,128)S(1)} async-done(((s32[32,1,64]{2,1,0:T(1,128)}), s32[32,1,64]{2,1,0:T(1,128)S(1)}, u32[]{:S(2)}, u32[]{:S(2)}) %all-to-all-start) | async-done | bytes 8224 | tf_op jit(solution)/shard_map/all_to_all | solution.py:254
  16.3 3.1 %mix.2 = bf16[512,1024]{1,0:T(8,128)(2,1)} custom-call(s32[1]{0:T(128)} %bitcast.me_ref, s32[32,1,64]{2,1,0:T(1,128)S(1)} %all-to-all-done.route_ref, bf16[1024,1024]{1,0:T(8,128)(2,1)S(1)} %bitcast.66), custom_call_target="tpu_custom_call" | custom-call | tf_op jit(solution)/shard_map/mix/pallas_call | solution.py:76
  19.4 2.6 %all-to-all-start.1 = ((bf16[32,16,1024]{2,1,0:T(8,128)(2,1)}), bf16[32,16,1024]{2,1,0:T(8,128)(2,1)S(1)}, u32[]{:S(2)}, u32[]{:S(2)}) async-start(bf16[32,16,1024]{2,1,0:T(8,128)(2,1)} %bitcast.70), calls=%async_computation.1 | async-start | bytes 2097152 | tf_op jit(solution)/shard_map/all_to_all | solution.py:254
  22.1 4.7 %mix.3 = (bf16[128,1024]{1,0:T(8,128)(2,1)}, bf16[128,1024]{1,0:T(8,128)(2,1)}, bf16[128,1024]{1,0:T(8,128)(2,1)}, bf16[128,1024]{1,0:T(8,128)(2,1)}) custom-call(s32[1]{0:T(128)} %bitcast.me_ref, s32[32,1,64]{2,1,0:T(1,128)S(1)} %all-to-all-done.route_ref, bf16[1024,1024]{1,0:T(8,128)(2,1)} %bitcast.68), custom_call_target="tpu_custom_call" | custom-call | tf_op jit(solution)/shard_map/mix/pallas_call | solution.py:76
  26.8 0.1 collective-permute-start
  26.9 1.6 %collective-permute-start.1 = (bf16[128,1024]{1,0:T(8,128)(2,1)}, bf16[128,1024]{1,0:T(8,128)(2,1)S(1)}, u32[]{:S(2)}, u32[]{:S(2)}) collective-permute-start(bf16[128,1024]{1,0:T(8,128)(2,1)} %get-tuple-element.28), channel_id=1, source_target_pairs={{0,2},{1,3},{2,0},{3,1},{4,6},{5,7},{6,4},{7,5},{8,10},{9,11},{10,... | collective-permute-start | bytes 786440 | tf_op jit(solution)/shard_map/ppermute | solution.py:146
  28.6 0.1 collective-permute-start.2
  28.7 19.6 %all-to-all-done.1 = bf16[32,16,1024]{2,1,0:T(8,128)(2,1)S(1)} async-done(((bf16[32,16,1024]{2,1,0:T(8,128)(2,1)}), bf16[32,16,1024]{2,1,0:T(8,128)(2,1)S(1)}, u32[]{:S(2)}, u32[]{:S(2)}) %all-to-all-start.1) | async-done | bytes 1048608 | tf_op jit(solution)/shard_map/all_to_all | solution.py:254
  48.3 0.0 copy-start.4
  48.3 6.6 %fusion.11 = (bf16[2048,512]{0,1:T(8,128)(2,1)S(1)}, f32[512,2048]{1,0:T(8,128)}) fusion(bf16[512,1024]{1,0:T(8,128)(2,1)S(1)} %bitcast.72, bf16[1,2048,1024]{2,1,0:T(8,128)(2,1)} %param.7), kind=kOutput, calls=%fused_computation.14 | convolution fusion | flops 2152726528 | bytes 11534336 | tf_op jit(solution)/shard_map/dot_general | solution.py:299
  54.9 0.0 copy-start.6
  54.9 0.0 copy-done.4
  54.9 0.0 copy-start
  54.9 3.3 %fusion.23 = bf16[512,1024]{1,0:T(8,128)(2,1)} fusion(bf16[2048,512]{0,1:T(8,128)(2,1)S(1)} %get-tuple-element.37, bf16[1,2048,1024]{2,1,0:T(8,128)(2,1)S(1)} %copy-done.4), kind=kOutput, calls=%fused_computation.26 | convolution fusion | flops 2148007936 | bytes 7340032 | tf_op jit(solution)/shard_map/dot_general | solution.py:303
  58.3 0.0 copy-done.6
  58.3 3.5 %all-to-all-start.2 = ((bf16[32,16,1024]{2,1,0:T(8,128)(2,1)}), bf16[32,16,1024]{2,1,0:T(8,128)(2,1)S(1)}, u32[]{:S(2)}, u32[]{:S(2)}) async-start(bf16[32,16,1024]{2,1,0:T(8,128)(2,1)} %bitcast.75), calls=%async_computation.2 | async-start | bytes 2097152 | tf_op jit(solution)/shard_map/all_to_all | solution.py:254
  61.8 0.0 collective-permute-done.refs_1_
  61.8 0.0 collective-permute-done.1.refs_2_
  61.8 0.0 collective-permute-done.2.refs_3_
  61.8 0.0 copy-done
  61.9 0.1 regroup.1
  61.9 1.8 %collective-permute-start.3 = (bf16[64,1024]{1,0:T(8,128)(2,1)S(1)}, bf16[64,1024]{1,0:T(8,128)(2,1)S(1)}, u32[]{:S(2)}, u32[]{:S(2)}) collective-permute-start(bf16[64,1024]{1,0:T(8,128)(2,1)S(1)} %get-tuple-element.30), channel_id=1, source_target_pairs={{0,4},{1,5},{2,6},{3,7},{4,0},{5,1},{6,2},{7,3},{8,12},{9,13},{10,... | collective-permute-start | bytes 393224 | tf_op jit(solution)/shard_map/ppermute | solution.py:146
  63.8 1.5 collective-permute-start.4
  65.2 0.3 collective-permute-start.5
  65.5 2.7 %collective-permute-start.6 = (bf16[64,1024]{1,0:T(8,128)(2,1)S(1)}, bf16[64,1024]{1,0:T(8,128)(2,1)S(1)}, u32[]{:S(2)}, u32[]{:S(2)}) collective-permute-start(bf16[64,1024]{1,0:T(8,128)(2,1)S(1)} %get-tuple-element.33), channel_id=1, source_target_pairs={{0,16},{1,17},{2,18},{3,19},{4,20},{5,21},{6,22},{7,23},{8,24},{9,... | collective-permute-start | bytes 393224 | tf_op jit(solution)/shard_map/ppermute | solution.py:146
  68.2 1.5 collective-permute-start.7
  69.6 4.8 %collective-permute-done.3.refs_4_ = bf16[64,1024]{1,0:T(8,128)(2,1)S(1)} collective-permute-done((bf16[64,1024]{1,0:T(8,128)(2,1)S(1)}, bf16[64,1024]{1,0:T(8,128)(2,1)S(1)}, u32[]{:S(2)}, u32[]{:S(2)}) %collective-permute-start.3) | collective-permute-done | bytes 131104 | tf_op jit(solution)/shard_map/ppermute | solution.py:146
  74.4 4.4 %collective-permute-start.8 = (bf16[64,1024]{1,0:T(8,128)(2,1)S(1)}, bf16[64,1024]{1,0:T(8,128)(2,1)S(1)}, u32[]{:S(2)}, u32[]{:S(2)}) collective-permute-start(bf16[64,1024]{1,0:T(8,128)(2,1)S(1)} %get-tuple-element.35), channel_id=1, source_target_pairs={{0,24},{1,25},{2,26},{3,27},{4,28},{5,29},{6,30},{7,31},{8,16},{9,... | collective-permute-start | bytes 393224 | tf_op jit(solution)/shard_map/ppermute | solution.py:146
  78.8 3.8 %collective-permute-done.4.refs_5_ = bf16[64,1024]{1,0:T(8,128)(2,1)S(1)} collective-permute-done((bf16[64,1024]{1,0:T(8,128)(2,1)S(1)}, bf16[64,1024]{1,0:T(8,128)(2,1)S(1)}, u32[]{:S(2)}, u32[]{:S(2)}) %collective-permute-start.4) | collective-permute-done | bytes 131104 | tf_op jit(solution)/shard_map/ppermute | solution.py:146
  82.6 4.6 %collective-permute-start.9 = (bf16[64,1024]{1,0:T(8,128)(2,1)S(1)}, bf16[64,1024]{1,0:T(8,128)(2,1)S(1)}, u32[]{:S(2)}, u32[]{:S(2)}) collective-permute-start(bf16[64,1024]{1,0:T(8,128)(2,1)S(1)} %get-tuple-element.36), channel_id=1, source_target_pairs={{0,28},{1,29},{2,30},{3,31},{4,24},{5,25},{6,26},{7,27},{8,20},{9,... | collective-permute-start | bytes 393224 | tf_op jit(solution)/shard_map/ppermute | solution.py:146
  87.2 0.2 collective-permute-done.5.refs_6_
  87.4 15.2 %collective-permute-done.6.refs_7_ = bf16[64,1024]{1,0:T(8,128)(2,1)S(1)} collective-permute-done((bf16[64,1024]{1,0:T(8,128)(2,1)S(1)}, bf16[64,1024]{1,0:T(8,128)(2,1)S(1)}, u32[]{:S(2)}, u32[]{:S(2)}) %collective-permute-start.6) | collective-permute-done | bytes 131104 | tf_op jit(solution)/shard_map/ppermute | solution.py:146
  102.6 3.7 %collective-permute-done.7.refs_8_ = bf16[64,1024]{1,0:T(8,128)(2,1)S(1)} collective-permute-done((bf16[64,1024]{1,0:T(8,128)(2,1)S(1)}, bf16[64,1024]{1,0:T(8,128)(2,1)S(1)}, u32[]{:S(2)}, u32[]{:S(2)}) %collective-permute-start.7) | collective-permute-done | bytes 131104 | tf_op jit(solution)/shard_map/ppermute | solution.py:146
  106.4 0.0 collective-permute-done.8.refs_9_
  106.4 0.0 collective-permute-done.9.refs_10_
  106.4 2.4 %settle.1 = bf16[512,1024]{1,0:T(8,128)(2,1)} custom-call(s32[1]{0:T(128)} %bitcast.me_ref, bf16[128,1024]{1,0:T(8,128)(2,1)} %get-tuple-element.26.refs_0_, bf16[128,1024]{1,0:T(8,128)(2,1)S(1)} %collective-permute-done.refs_1_, bf16[128,1024]{1,0:T(8,128)(2,1)S(1)} %collective-permute-done.1.refs_2_, bf16[128,1024]{1,0:T(8,128)(2,1)S(1)} %collective-permute-done.2.refs_3_, ...), custom_call_target="tpu_custom_call" | custom-call | tf_op jit(solution)/shard_map/settle/pallas_call | solution.py:158
  108.8 0.0 copy-start.5
  108.8 6.2 %fusion.5 = bf16[2048,512]{0,1:T(8,128)(2,1)S(1)} fusion(f32[512,2048]{1,0:T(8,128)} %get-tuple-element.49, bf16[512,1024]{1,0:T(8,128)(2,1)} %settle.1, bf16[1,2048,1024]{2,1,0:T(8,128)(2,1)} %param.8), kind=kOutput, calls=%fused_computation.6 | convolution fusion | flops 2157969408 | bytes 11534336 | tf_op jit(solution)/shard_map/dot_general | solution.py:305
  115.0 0.0 copy-start.8
  115.0 1.3 copy-done.8
  116.3 0.0 copy-done.5
  116.3 3.3 %fusion.20 = bf16[512,1024]{1,0:T(8,128)(2,1)} fusion(bf16[2048,512]{0,1:T(8,128)(2,1)S(1)} %fusion.5, bf16[1,2048,1024]{2,1,0:T(8,128)(2,1)S(1)} %copy-done.5), kind=kOutput, calls=%fused_computation.25 | convolution fusion | flops 2148007936 | bytes 7340032 | tf_op jit(solution)/shard_map/dot_general | solution.py:310
  119.6 0.0 all-to-all-done.2
  119.7 7.1 %all-to-all-start.3 = ((bf16[32,16,1024]{2,1,0:T(8,128)(2,1)}), bf16[32,16,1024]{2,1,0:T(8,128)(2,1)S(1)}, u32[]{:S(2)}, u32[]{:S(2)}) async-start(bf16[32,16,1024]{2,1,0:T(8,128)(2,1)} %bitcast.76), calls=%async_computation.3 | async-start | bytes 2097152 | tf_op jit(solution)/shard_map/all_to_all | solution.py:254
  126.7 0.4 turn.1
  127.1 0.0 copy-start.1
  127.1 0.0 copy-start.2
  127.1 1.3 fusion.26
  128.4 0.3 copy-done.1
  128.7 1.2 copy-done.2
  129.9 0.0 copy-start.3
  129.9 0.0 copy-start.7
  129.9 4.1 %subtract_convert_fusion = (bf16[64,16,1024]{2,1,0:T(8,128)(2,1)}, f32[64,16,1024]{2,1,0:T(8,128)}) fusion(bf16[64,16,1024]{2,1,0:T(8,128)(2,1)S(1)} %copy-done.1, f32[64,16,1024]{2,1,0:T(8,128)S(1)} %bitcast.71, f32[64,16,1024]{2,1,0:T(8,128)S(1)} %copy-done.2), kind=kLoop, calls=%fused_computation.21 | loop fusion | flops 6291456 | bytes 16777216 | tf_op jit(solution)/shard_map/convert_element_type | solution.py:287
  134.0 0.0 copy-done.3
  134.0 0.0 copy-done.7
  134.0 4.4 %convolution_convert_fusion.1 = bf16[2048,1024]{1,0:T(8,128)(2,1)} fusion(bf16[2048,512]{0,1:T(8,128)(2,1)S(1)} %copy-done.7, bf16[512,1024]{1,0:T(8,128)(2,1)S(1)} %copy-done.3), kind=kOutput, calls=%fused_computation.24 | convolution fusion | flops 2149580800 | bytes 7340032 | tf_op jit(solution)/shard_map/dot_general | solution.py:316
  138.4 0.0 copy-done.9
  138.4 4.4 %convolution_convert_fusion = bf16[2048,1024]{1,0:T(8,128)(2,1)} fusion(bf16[2048,512]{0,1:T(8,128)(2,1)S(1)} %copy-done.9, bf16[512,1024]{1,0:T(8,128)(2,1)S(1)} %bitcast.73), kind=kOutput, calls=%fused_computation.23 | convolution fusion | flops 2149580800 | bytes 7340032 | tf_op jit(solution)/shard_map/dot_general | solution.py:317
  142.8 1.6 %fetch.3 = bf16[64,16,1024]{2,1,0:T(8,128)(2,1)S(1)} custom-call(bf16[64,16,1024]{2,1,0:T(8,128)(2,1)} %refs_0_.2), custom_call_target="tpu_custom_call" | custom-call | tf_op jit(solution)/shard_map/fetch/pallas_call | solution.py:183
  144.4 8.3 %all-to-all-done.3 = bf16[32,16,1024]{2,1,0:T(8,128)(2,1)S(1)} async-done(((bf16[32,16,1024]{2,1,0:T(8,128)(2,1)}), bf16[32,16,1024]{2,1,0:T(8,128)(2,1)S(1)}, u32[]{:S(2)}, u32[]{:S(2)}) %all-to-all-start.3) | async-done | bytes 1048608 | tf_op jit(solution)/shard_map/all_to_all | solution.py:254
  152.8 5.1 %update_last.1 = (f32[1024,1024]{1,0:T(8,128)}, bf16[1024,1024]{1,0:T(8,128)(2,1)}) custom-call(s32[32,1,64]{2,1,0:T(1,128)S(1)} %all-to-all-done.route_ref, bf16[512,1024]{1,0:T(8,128)(2,1)S(1)} %bitcast.67, bf16[1024,1024]{1,0:T(8,128)(2,1)S(1)} %bitcast.65, f32[1024,1024]{1,0:T(8,128)} %bitcast.69), custom_call_target="tpu_custom_call" | custom-call | tf_op jit(solution)/shard_map/update_last/pallas_call | solution.py:232
  (1 shorter events, 0.0 us)
Async XLA Ops:
  1.9 14.4 %all-to-all-start = ((s32[32,1,64]{2,1,0:T(1,128)}), s32[32,1,64]{2,1,0:T(1,128)S(1)}, u32[]{:S(2)}, u32[]{:S(2)}) async-start(s32[32,1,64]{2,1,0:T(1,128)} %broadcast_in_dim.19), calls=%async_computation | async-start | bytes 32768 | tf_op jit(solution)/shard_map/all_to_all | solution.py:254
  19.4 28.8 %all-to-all-start.1 = ((bf16[32,16,1024]{2,1,0:T(8,128)(2,1)}), bf16[32,16,1024]{2,1,0:T(8,128)(2,1)S(1)}, u32[]{:S(2)}, u32[]{:S(2)}) async-start(bf16[32,16,1024]{2,1,0:T(8,128)(2,1)} %bitcast.70), calls=%async_computation.1 | async-start | bytes 2097152 | tf_op jit(solution)/shard_map/all_to_all | solution.py:254
  26.8 35.0 %collective-permute-start = (bf16[128,1024]{1,0:T(8,128)(2,1)}, bf16[128,1024]{1,0:T(8,128)(2,1)S(1)}, u32[]{:S(2)}, u32[]{:S(2)}) collective-permute-start(bf16[128,1024]{1,0:T(8,128)(2,1)} %get-tuple-element.27), channel_id=1, source_target_pairs={{0,1},{1,0},{2,3},{3,2},{4,5},{5,4},{6,7},{7,6},{8,9},{9,8},{10,11... | collective-permute-start | bytes 786440 | tf_op jit(solution)/shard_map/ppermute | solution.py:146
  26.9 34.9 %collective-permute-start.1 = (bf16[128,1024]{1,0:T(8,128)(2,1)}, bf16[128,1024]{1,0:T(8,128)(2,1)S(1)}, u32[]{:S(2)}, u32[]{:S(2)}) collective-permute-start(bf16[128,1024]{1,0:T(8,128)(2,1)} %get-tuple-element.28), channel_id=1, source_target_pairs={{0,2},{1,3},{2,0},{3,1},{4,6},{5,7},{6,4},{7,5},{8,10},{9,11},{10,... | collective-permute-start | bytes 786440 | tf_op jit(solution)/shard_map/ppermute | solution.py:146
  28.6 33.3 %collective-permute-start.2 = (bf16[128,1024]{1,0:T(8,128)(2,1)}, bf16[128,1024]{1,0:T(8,128)(2,1)S(1)}, u32[]{:S(2)}, u32[]{:S(2)}) collective-permute-start(bf16[128,1024]{1,0:T(8,128)(2,1)} %get-tuple-element.29), channel_id=1, source_target_pairs={{0,3},{1,2},{2,1},{3,0},{4,7},{5,6},{6,5},{7,4},{8,11},{9,10},{10,... | collective-permute-start | bytes 786440 | tf_op jit(solution)/shard_map/ppermute | solution.py:146
  48.3 6.7 %copy-start.4 = (bf16[1,2048,1024]{2,1,0:T(8,128)(2,1)S(1)}, bf16[1,2048,1024]{2,1,0:T(8,128)(2,1)}, u32[]{:S(2)}) copy-start(bf16[1,2048,1024]{2,1,0:T(8,128)(2,1)} %param.8) | copy-start | bytes 12582916
  54.9 3.3 %copy-start.6 = (bf16[2048,512]{0,1:T(8,128)(2,1)}, bf16[2048,512]{0,1:T(8,128)(2,1)S(1)}, u32[]{:S(2)}) copy-start(bf16[2048,512]{0,1:T(8,128)(2,1)S(1)} %get-tuple-element.37) | copy-start | bytes 6291460
  54.9 6.9 %copy-start = (bf16[128,1024]{1,0:T(8,128)(2,1)S(1)}, bf16[128,1024]{1,0:T(8,128)(2,1)}, u32[]{:S(2)}) copy-start(bf16[128,1024]{1,0:T(8,128)(2,1)} %get-tuple-element.26.refs_0_) | copy-start | bytes 786436
  58.3 61.4 %all-to-all-start.2 = ((bf16[32,16,1024]{2,1,0:T(8,128)(2,1)}), bf16[32,16,1024]{2,1,0:T(8,128)(2,1)S(1)}, u32[]{:S(2)}, u32[]{:S(2)}) async-start(bf16[32,16,1024]{2,1,0:T(8,128)(2,1)} %bitcast.75), calls=%async_computation.2 | async-start | bytes 2097152 | tf_op jit(solution)/shard_map/all_to_all | solution.py:254
  61.9 12.5 %collective-permute-start.3 = (bf16[64,1024]{1,0:T(8,128)(2,1)S(1)}, bf16[64,1024]{1,0:T(8,128)(2,1)S(1)}, u32[]{:S(2)}, u32[]{:S(2)}) collective-permute-start(bf16[64,1024]{1,0:T(8,128)(2,1)S(1)} %get-tuple-element.30), channel_id=1, source_target_pairs={{0,4},{1,5},{2,6},{3,7},{4,0},{5,1},{6,2},{7,3},{8,12},{9,13},{10,... | collective-permute-start | bytes 393224 | tf_op jit(solution)/shard_map/ppermute | solution.py:146
  63.8 18.8 %collective-permute-start.4 = (bf16[64,1024]{1,0:T(8,128)(2,1)S(1)}, bf16[64,1024]{1,0:T(8,128)(2,1)S(1)}, u32[]{:S(2)}, u32[]{:S(2)}) collective-permute-start(bf16[64,1024]{1,0:T(8,128)(2,1)S(1)} %get-tuple-element.31), channel_id=1, source_target_pairs={{0,8},{1,9},{2,10},{3,11},{4,12},{5,13},{6,14},{7,15},{8,0},{9,1},... | collective-permute-start | bytes 393224 | tf_op jit(solution)/shard_map/ppermute | solution.py:146
  65.2 22.2 %collective-permute-start.5 = (bf16[64,1024]{1,0:T(8,128)(2,1)S(1)}, bf16[64,1024]{1,0:T(8,128)(2,1)S(1)}, u32[]{:S(2)}, u32[]{:S(2)}) collective-permute-start(bf16[64,1024]{1,0:T(8,128)(2,1)S(1)} %get-tuple-element.32), channel_id=1, source_target_pairs={{0,12},{1,13},{2,14},{3,15},{4,8},{5,9},{6,10},{7,11},{8,4},{9,5},... | collective-permute-start | bytes 393224 | tf_op jit(solution)/shard_map/ppermute | solution.py:146
  65.5 37.2 %collective-permute-start.6 = (bf16[64,1024]{1,0:T(8,128)(2,1)S(1)}, bf16[64,1024]{1,0:T(8,128)(2,1)S(1)}, u32[]{:S(2)}, u32[]{:S(2)}) collective-permute-start(bf16[64,1024]{1,0:T(8,128)(2,1)S(1)} %get-tuple-element.33), channel_id=1, source_target_pairs={{0,16},{1,17},{2,18},{3,19},{4,20},{5,21},{6,22},{7,23},{8,24},{9,... | collective-permute-start | bytes 393224 | tf_op jit(solution)/shard_map/ppermute | solution.py:146
  68.2 38.2 %collective-permute-start.7 = (bf16[64,1024]{1,0:T(8,128)(2,1)S(1)}, bf16[64,1024]{1,0:T(8,128)(2,1)S(1)}, u32[]{:S(2)}, u32[]{:S(2)}) collective-permute-start(bf16[64,1024]{1,0:T(8,128)(2,1)S(1)} %get-tuple-element.34), channel_id=1, source_target_pairs={{0,20},{1,21},{2,22},{3,23},{4,16},{5,17},{6,18},{7,19},{8,28},{9,... | collective-permute-start | bytes 393224 | tf_op jit(solution)/shard_map/ppermute | solution.py:146
  74.4 31.9 %collective-permute-start.8 = (bf16[64,1024]{1,0:T(8,128)(2,1)S(1)}, bf16[64,1024]{1,0:T(8,128)(2,1)S(1)}, u32[]{:S(2)}, u32[]{:S(2)}) collective-permute-start(bf16[64,1024]{1,0:T(8,128)(2,1)S(1)} %get-tuple-element.35), channel_id=1, source_target_pairs={{0,24},{1,25},{2,26},{3,27},{4,28},{5,29},{6,30},{7,31},{8,16},{9,... | collective-permute-start | bytes 393224 | tf_op jit(solution)/shard_map/ppermute | solution.py:146
  82.6 23.8 %collective-permute-start.9 = (bf16[64,1024]{1,0:T(8,128)(2,1)S(1)}, bf16[64,1024]{1,0:T(8,128)(2,1)S(1)}, u32[]{:S(2)}, u32[]{:S(2)}) collective-permute-start(bf16[64,1024]{1,0:T(8,128)(2,1)S(1)} %get-tuple-element.36), channel_id=1, source_target_pairs={{0,28},{1,29},{2,30},{3,31},{4,24},{5,25},{6,26},{7,27},{8,20},{9,... | collective-permute-start | bytes 393224 | tf_op jit(solution)/shard_map/ppermute | solution.py:146
  108.8 7.5 %copy-start.5 = (bf16[1,2048,1024]{2,1,0:T(8,128)(2,1)S(1)}, bf16[1,2048,1024]{2,1,0:T(8,128)(2,1)}, u32[]{:S(2)}) copy-start(bf16[1,2048,1024]{2,1,0:T(8,128)(2,1)} %param.7) | copy-start | bytes 12582916
  115.0 1.3 copy-start.8
  119.7 33.1 %all-to-all-start.3 = ((bf16[32,16,1024]{2,1,0:T(8,128)(2,1)}), bf16[32,16,1024]{2,1,0:T(8,128)(2,1)S(1)}, u32[]{:S(2)}, u32[]{:S(2)}) async-start(bf16[32,16,1024]{2,1,0:T(8,128)(2,1)} %bitcast.76), calls=%async_computation.3 | async-start | bytes 2097152 | tf_op jit(solution)/shard_map/all_to_all | solution.py:254
  127.1 1.6 %copy-start.1 = (bf16[64,16,1024]{2,1,0:T(8,128)(2,1)S(1)}, bf16[64,16,1024]{2,1,0:T(8,128)(2,1)}, u32[]{:S(2)}) copy-start(bf16[64,16,1024]{2,1,0:T(8,128)(2,1)} %param.11) | copy-start | bytes 6291460
  127.1 2.8 %copy-start.2 = (f32[64,16,1024]{2,1,0:T(8,128)S(1)}, f32[64,16,1024]{2,1,0:T(8,128)}, u32[]{:S(2)}) copy-start(f32[64,16,1024]{2,1,0:T(8,128)} %param.13) | copy-start | bytes 12582916
  129.9 4.1 %copy-start.3 = (bf16[512,1024]{1,0:T(8,128)(2,1)S(1)}, bf16[512,1024]{1,0:T(8,128)(2,1)}, u32[]{:S(2)}) copy-start(bf16[512,1024]{1,0:T(8,128)(2,1)} %settle.1) | copy-start | bytes 3145732
  129.9 4.1 %copy-start.7 = (bf16[2048,512]{0,1:T(8,128)(2,1)S(1)}, bf16[2048,512]{0,1:T(8,128)(2,1)}, u32[]{:S(2)}) copy-start(bf16[2048,512]{0,1:T(8,128)(2,1)} %copy-done.6) | copy-start | bytes 6291460
  134.0 4.4 %copy-start.9 = (bf16[2048,512]{0,1:T(8,128)(2,1)S(1)}, bf16[2048,512]{0,1:T(8,128)(2,1)}, u32[]{:S(2)}) copy-start(bf16[2048,512]{0,1:T(8,128)(2,1)} %copy-done.8) | copy-start | bytes 6291460

commit v5 on v4

--- a/solution.py
+++ b/solution.py
@@ -9,7 +9,7 @@
 
 
 PIECES = 4
-TOP = 8
+TOP = 16
 
 
 def gelu_parts(pre):
@@ -40,51 +40,64 @@
 
 
 def mix_kernel(rows, top, resident, me_ref, route_ref, weight_ref, *refs):
-    sum_refs, mixer_ref = refs[:-1], refs[-1]
-
-    @pl.when(pl.program_id(0) == 0)
-    def _():
-        mix = mix_of(route_ref)
-        segs = mix.shape[0]
-        if top:
-            line = lax.broadcasted_iota(jnp.int32, (segs, segs), 0)
-            apart = (line % top) * (segs // top) + line // top
-            chosen = lax.broadcasted_iota(jnp.int32, (segs, segs), 1) == (apart ^ me_ref[0])
-            chosen = jnp.where(chosen, 1.0, 0.0).astype(jnp.bfloat16)
-            mix = jnp.dot(chosen, mix, preferred_element_type=jnp.float32).astype(jnp.bfloat16)
-        spread(mix, rows, mixer_ref)
-
-    lines, tile = sum_refs[0].shape
-    weight = weight_ref
-    if resident:
-        here = pl.ds(pl.multiple_of(pl.program_id(0) * tile, tile), tile)
-        weight = weight_ref.at[:, here]
-    sums = jnp.dot(mixer_ref[...], weight[...], preferred_element_type=jnp.float32)
-    for i, sum_ref in enumerate(sum_refs):
-        sum_ref[...] = sums[i * lines : (i + 1) * lines, :].astype(jnp.bfloat16)
+    outs, (mixer_ref, sum_ref, held_ref, in_sem, sems) = refs[:-5], refs[-5:]
+    if not resident:
+        fetched = pltpu.make_async_copy(weight_ref, held_ref, in_sem)
+        fetched.start()
+    mix = mix_of(route_ref)
+    segs = mix.shape[0]
+    if top:
+        line = lax.broadcasted_iota(jnp.int32, (segs, segs), 0)
+        apart = (line % top) * (segs // top) + line // top
+        chosen = lax.broadcasted_iota(jnp.int32, (segs, segs), 1) == (apart ^ me_ref[0])
+        chosen = jnp.where(chosen, 1.0, 0.0).astype(jnp.bfloat16)
+        mix = jnp.dot(chosen, mix, preferred_element_type=jnp.float32).astype(jnp.bfloat16)
+    spread(mix, rows, mixer_ref)
+    if not resident:
+        fetched.wait()
+        weight_ref = held_ref
+    size = sum_ref.shape[0] // sems.shape[0]
+    lines = outs[0].shape[0]
+    copies = []
+    for i in range(sems.shape[0]):
+        here = slice(i * size, (i + 1) * size)
+        sums = jnp.dot(mixer_ref[here, :], weight_ref[...], preferred_element_type=jnp.float32)
+        sum_ref[here, :] = sums.astype(jnp.bfloat16)
+        place = pl.ds(i * size % lines, size)
+        copy = pltpu.make_async_copy(
+            sum_ref.at[here, :], outs[i * size // lines].at[place, :], sems.at[i]
+        )
+        copy.start()
+        copies.append(copy)
+    for copy in copies:
+        copy.wait()
 
 
 def mix_call(me, routes, weights, parts, top, resident):
     segs = routes.shape[0]
     experts, rows, width = weights.shape
-    tile = width // 4
     lines = segs * rows // parts
+    steps = max(4, parts)
     weights = weights.reshape(experts * rows, width)
-    whole = pl.BlockSpec(memory_space=pltpu.VMEM)
+    whole, free = pl.BlockSpec(memory_space=pltpu.VMEM), pl.BlockSpec(memory_space=pl.ANY)
     if not resident:
         weights = pltpu.with_memory_space_constraint(weights, pltpu.HBM)
     return pl.pallas_call(
         functools.partial(mix_kernel, rows, top, resident),
-        grid=(width // tile,),
-        in_specs=[
-            pl.BlockSpec(memory_space=pltpu.SMEM),
-            pl.BlockSpec(routes.shape, lambda i: (0, 0, 0)),
-            whole if resident else pl.BlockSpec((experts * rows, tile), lambda i: (0, i)),
+        in_specs=[pl.BlockSpec(memory_space=pltpu.SMEM), whole, whole if resident else free],
+        out_specs=[free] * parts,
+        out_shape=[
+            (pltpu.VMEM if top and i == 0 else pltpu.HBM)((lines, width), jnp.bfloat16)
+            for i in range(parts)
         ],
-        out_specs=[pl.BlockSpec((lines, tile), lambda i: (0, i))] * parts,
-        out_shape=[pltpu.HBM((lines, width), jnp.bfloat16)] * parts,
-        scratch_shapes=[pltpu.VMEM((segs * rows, experts * rows), jnp.bfloat16)],
-        compiler_params=pltpu.CompilerParams(vmem_limit_bytes=12 << 20),
+        scratch_shapes=[
+            pltpu.VMEM((segs * rows, experts * rows), jnp.bfloat16),
+            pltpu.VMEM((segs * rows, width), jnp.bfloat16),
+            pltpu.VMEM((8, 128) if resident else (experts * rows, width), jnp.bfloat16),
+            pltpu.SemaphoreType.DMA,
+            pltpu.SemaphoreType.DMA((steps,)),
+        ],
+        compiler_params=pltpu.CompilerParams(vmem_limit_bytes=10 << 20),
         name="mix",
     )(me, routes, weights)
 
@@ -101,10 +114,6 @@
         compiler_params=pltpu.CompilerParams(vmem_limit_bytes=8 << 20),
         name="turn",
     )(routes)
-
-
-def in_hbm(*arrays):
-    return [pltpu.with_memory_space_constraint(array, pltpu.HBM) for array in arrays]
 
 
 def copy_all(copies):
@@ -157,13 +166,13 @@
     got = [swap(send[z - 1], z * low) for z in reversed(range(1, top))][::-1]
     return pl.pallas_call(
         functools.partial(settle_kernel, low, top, rows),
-        in_specs=[pl.BlockSpec(memory_space=pltpu.SMEM), hbm] + [free] * (low + top - 2),
+        in_specs=[pl.BlockSpec(memory_space=pltpu.SMEM)] + [free] * (low + top - 1),
         out_specs=hbm,
         out_shape=pltpu.HBM((segs * rows, width), jnp.bfloat16),
         scratch_shapes=[pltpu.SemaphoreType.DMA((low, top))],
         compiler_params=pltpu.CompilerParams(vmem_limit_bytes=1 << 20),
         name="settle",
-    )(me, *in_hbm(plane[0]), *plane[1:], *got)
+    )(me, *plane, *got)
 
 
 def fetch_kernel(count, *refs):

time: 159 us -> 156 us (0.981)
  starting transfers between devices: 39.2 us -> 46.1 us
  waiting for transfers between devices: 61.1 us -> 55 us
  Pallas kernels: 18.9 us -> 16.1 us
    ppermute x10 -> x16, starting transfers between devices: 18.6 us -> 29.7 us  [swap(): return lax.ppermute(block, 'seg', [(i, i ^ apart) for i in range(segs)])]
    ppermute x10 -> x16, waiting for transfers between devices: 27.7 us -> 19.2 us  [swap(): return lax.ppermute(block, 'seg', [(i, i ^ apart) for i in range(segs)])]
    all_to_all x4, starting transfers between devices: 20.6 us -> 16.4 us  [exchange(): lax.all_to_all(blocks, 'seg', split_axis=0, concat_axis=0, tiled=True)]
    all_to_all x4, waiting for transfers between devices: 33.4 us -> 35.8 us  [exchange(): lax.all_to_all(blocks, 'seg', split_axis=0, concat_axis=0, tiled=True)]
    pallas_call x2, Pallas kernels: 7.81 us -> 6.16 us  [mix_call(): pl.pallas_call(functools.partial(mix_kernel, rows, top, resident), in_spe...]
  transfers between devices with their start and end apart: 14 -> 20, of which waited for: 8 -> 10; matrix products, arithmetic and copies ran while one was open for 21% -> 22% of each run, Pallas kernels for 7% -> 6%
where the time goes in v5:
time: 156 us
  waiting for transfers between devices  55 us (35%)
  starting transfers between devices  46.1 us (30%)
  matrix products  29.6 us (19%)
  Pallas kernels  16.1 us (10%)
  local copies, waits for them, and re-layouts  4.16 us (3%)
  other arithmetic  4.07 us (3%)
    all_to_all x4, waiting for transfers between devices, exchange(): lax.all_to_all(blocks, 'seg', split_axis=0, concat_axis=0, tiled=True)  35.8 us
    ppermute x16, starting transfers between devices, swap(): return lax.ppermute(block, 'seg', [(i, i ^ apart) for i in range(segs)])  29.7 us
    ppermute x16, waiting for transfers between devices, swap(): return lax.ppermute(block, 'seg', [(i, i ^ apart) for i in range(segs)])  19.2 us
    all_to_all x4, starting transfers between devices, exchange(): lax.all_to_all(blocks, 'seg', split_axis=0, concat_axis=0, tiled=True)  16.4 us
    dot_general x1, matrix products, step(): lax.dot_general(inputs, up, (((1,), (1,)), ((), ())), preferred_element_t...  6.64 us
    dot_general x1, matrix products, step(): lax.dot_general(grads, down, (((1,), (1,)), ((), ())), preferred_element_...  6.19 us
    pallas_call x2, Pallas kernels, mix_call(): pl.pallas_call(functools.partial(mix_kernel, rows, top, resident), in_spe...  6.16 us
    pallas_call x1, Pallas kernels, update_last(): pl.pallas_call(functools.partial(update_kernel, count, rows), in_specs=[v...  5.06 us
  transfers between devices with their start and end apart: 20, of which 10 were waited for; matrix products, arithmetic and copies ran while one was open for 22% of the time, Pallas kernels for 6%

profile of v5, /device:TPU:0, one launch (start us, length us, event | category | flops | bytes accessed | tf_op | source)
XLA Modules:
  0.0 155.9 jit_solution(11822651069440492888)
XLA Ops:
  0.6 1.3 broadcast_in_dim.19
  1.9 7.3 %all-to-all-start = ((s32[32,1,64]{2,1,0:T(1,128)}), s32[32,1,64]{2,1,0:T(1,128)S(1)}, u32[]{:S(2)}, u32[]{:S(2)}) async-start(s32[32,1,64]{2,1,0:T(1,128)} %broadcast_in_dim.19), calls=%async_computation | async-start | bytes 32768 | tf_op jit(solution)/shard_map/all_to_all | solution.py:263
  9.2 1.6 %fetch.2 = bf16[64,16,1024]{2,1,0:T(8,128)(2,1)S(1)} custom-call(bf16[64,16,1024]{2,1,0:T(8,128)(2,1)} %refs_0_.2), custom_call_target="tpu_custom_call" | custom-call | tf_op jit(solution)/shard_map/fetch/pallas_call | solution.py:192
  10.8 5.5 %all-to-all-done.route_ref = s32[32,1,64]{2,1,0:T(1,128)S(1)} async-done(((s32[32,1,64]{2,1,0:T(1,128)}), s32[32,1,64]{2,1,0:T(1,128)S(1)}, u32[]{:S(2)}, u32[]{:S(2)}) %all-to-all-start) | async-done | bytes 8224 | tf_op jit(solution)/shard_map/all_to_all | solution.py:263
  16.3 2.1 %mix.2 = bf16[512,1024]{1,0:T(8,128)(2,1)} custom-call(s32[1]{0:T(128)} %bitcast.me_ref, s32[32,1,64]{2,1,0:T(1,128)S(1)} %all-to-all-done.route_ref, bf16[1024,1024]{1,0:T(8,128)(2,1)S(1)} %bitcast.66), custom_call_target="tpu_custom_call" | custom-call | tf_op jit(solution)/shard_map/mix/pallas_call | solution.py:85
  18.5 2.7 %all-to-all-start.1 = ((bf16[32,16,1024]{2,1,0:T(8,128)(2,1)}), bf16[32,16,1024]{2,1,0:T(8,128)(2,1)S(1)}, u32[]{:S(2)}, u32[]{:S(2)}) async-start(bf16[32,16,1024]{2,1,0:T(8,128)(2,1)} %bitcast.70), calls=%async_computation.1 | async-start | bytes 2097152 | tf_op jit(solution)/shard_map/all_to_all | solution.py:263
  21.1 4.0 %mix.3 = (bf16[256,1024]{1,0:T(8,128)(2,1)S(1)}, bf16[256,1024]{1,0:T(8,128)(2,1)}) custom-call(s32[1]{0:T(128)} %bitcast.me_ref, s32[32,1,64]{2,1,0:T(1,128)S(1)} %all-to-all-done.route_ref, bf16[1024,1024]{1,0:T(8,128)(2,1)} %bitcast.68), custom_call_target="tpu_custom_call" | custom-call | tf_op jit(solution)/shard_map/mix/pallas_call | solution.py:85
  25.2 0.2 collective-permute-start
  25.4 22.0 %all-to-all-done.1 = bf16[32,16,1024]{2,1,0:T(8,128)(2,1)S(1)} async-done(((bf16[32,16,1024]{2,1,0:T(8,128)(2,1)}), bf16[32,16,1024]{2,1,0:T(8,128)(2,1)S(1)}, u32[]{:S(2)}, u32[]{:S(2)}) %all-to-all-start.1) | async-done | bytes 1048608 | tf_op jit(solution)/shard_map/all_to_all | solution.py:263
  47.3 6.6 %fusion.11 = (bf16[2048,512]{0,1:T(8,128)(2,1)S(1)}, f32[512,2048]{1,0:T(8,128)}) fusion(bf16[512,1024]{1,0:T(8,128)(2,1)S(1)} %bitcast.72, bf16[1,2048,1024]{2,1,0:T(8,128)(2,1)} %param.7), kind=kOutput, calls=%fused_computation.14 | convolution fusion | flops 2152726528 | bytes 11534336 | tf_op jit(solution)/shard_map/dot_general | solution.py:308
  54.0 3.3 %fusion.23 = bf16[512,1024]{1,0:T(8,128)(2,1)} fusion(bf16[2048,512]{0,1:T(8,128)(2,1)S(1)} %get-tuple-element.49, bf16[1,2048,1024]{2,1,0:T(8,128)(2,1)S(1)} %copy-done.3), kind=kOutput, calls=%fused_computation.26 | convolution fusion | flops 2148007936 | bytes 7340032 | tf_op jit(solution)/shard_map/dot_general | solution.py:312
  57.3 3.5 %all-to-all-start.2 = ((bf16[32,16,1024]{2,1,0:T(8,128)(2,1)}), bf16[32,16,1024]{2,1,0:T(8,128)(2,1)S(1)}, u32[]{:S(2)}, u32[]{:S(2)}) async-start(bf16[32,16,1024]{2,1,0:T(8,128)(2,1)} %bitcast.75), calls=%async_computation.2 | async-start | bytes 2097152 | tf_op jit(solution)/shard_map/all_to_all | solution.py:263
  60.9 0.0 collective-permute-done.refs_1_
  60.9 0.1 regroup.1
  61.0 1.8 %collective-permute-start.1 = (bf16[32,1024]{1,0:T(8,128)(2,1)S(1)}, bf16[32,1024]{1,0:T(8,128)(2,1)S(1)}, u32[]{:S(2)}, u32[]{:S(2)}) collective-permute-start(bf16[32,1024]{1,0:T(8,128)(2,1)S(1)} %get-tuple-element.34), channel_id=1, source_target_pairs={{0,2},{1,3},{2,0},{3,1},{4,6},{5,7},{6,4},{7,5},{8,10},{9,11},{10,... | collective-permute-start | bytes 196616 | tf_op jit(solution)/shard_map/ppermute | solution.py:155
  62.8 1.5 collective-permute-start.2
  64.3 0.3 collective-permute-start.3
  64.5 1.8 %collective-permute-start.4 = (bf16[32,1024]{1,0:T(8,128)(2,1)S(1)}, bf16[32,1024]{1,0:T(8,128)(2,1)S(1)}, u32[]{:S(2)}, u32[]{:S(2)}) collective-permute-start(bf16[32,1024]{1,0:T(8,128)(2,1)S(1)} %get-tuple-element.37), channel_id=1, source_target_pairs={{0,8},{1,9},{2,10},{3,11},{4,12},{5,13},{6,14},{7,15},{8,0},{9,1},... | collective-permute-start | bytes 196616 | tf_op jit(solution)/shard_map/ppermute | solution.py:155
  66.3 1.5 collective-permute-start.5
  67.7 4.9 %collective-permute-done.1.refs_2_ = bf16[32,1024]{1,0:T(8,128)(2,1)S(1)} collective-permute-done((bf16[32,1024]{1,0:T(8,128)(2,1)S(1)}, bf16[32,1024]{1,0:T(8,128)(2,1)S(1)}, u32[]{:S(2)}, u32[]{:S(2)}) %collective-permute-start.1) | collective-permute-done | bytes 65568 | tf_op jit(solution)/shard_map/ppermute | solution.py:155
  72.7 1.1 collective-permute-start.6
  73.7 0.0 collective-permute-done.2.refs_3_
  73.7 2.8 %collective-permute-start.7 = (bf16[32,1024]{1,0:T(8,128)(2,1)S(1)}, bf16[32,1024]{1,0:T(8,128)(2,1)S(1)}, u32[]{:S(2)}, u32[]{:S(2)}) collective-permute-start(bf16[32,1024]{1,0:T(8,128)(2,1)S(1)} %get-tuple-element.40), channel_id=1, source_target_pairs={{0,14},{1,15},{2,12},{3,13},{4,10},{5,11},{6,8},{7,9},{8,6},{9,7},... | collective-permute-start | bytes 196616 | tf_op jit(solution)/shard_map/ppermute | solution.py:155
  76.6 0.0 collective-permute-done.3.refs_4_
  76.6 1.8 %collective-permute-start.8 = (bf16[32,1024]{1,0:T(8,128)(2,1)S(1)}, bf16[32,1024]{1,0:T(8,128)(2,1)S(1)}, u32[]{:S(2)}, u32[]{:S(2)}) collective-permute-start(bf16[32,1024]{1,0:T(8,128)(2,1)S(1)} %get-tuple-element.41), channel_id=1, source_target_pairs={{0,16},{1,17},{2,18},{3,19},{4,20},{5,21},{6,22},{7,23},{8,24},{9,... | collective-permute-start | bytes 196616 | tf_op jit(solution)/shard_map/ppermute | solution.py:155
  78.3 1.9 %collective-permute-done.4.refs_5_ = bf16[32,1024]{1,0:T(8,128)(2,1)S(1)} collective-permute-done((bf16[32,1024]{1,0:T(8,128)(2,1)S(1)}, bf16[32,1024]{1,0:T(8,128)(2,1)S(1)}, u32[]{:S(2)}, u32[]{:S(2)}) %collective-permute-start.4) | collective-permute-done | bytes 65568 | tf_op jit(solution)/shard_map/ppermute | solution.py:155
  80.2 5.6 %collective-permute-start.9 = (bf16[32,1024]{1,0:T(8,128)(2,1)S(1)}, bf16[32,1024]{1,0:T(8,128)(2,1)S(1)}, u32[]{:S(2)}, u32[]{:S(2)}) collective-permute-start(bf16[32,1024]{1,0:T(8,128)(2,1)S(1)} %get-tuple-element.42), channel_id=1, source_target_pairs={{0,18},{1,19},{2,16},{3,17},{4,22},{5,23},{6,20},{7,21},{8,26},{9,... | collective-permute-start | bytes 196616 | tf_op jit(solution)/shard_map/ppermute | solution.py:155
  85.9 0.0 collective-permute-done.5.refs_6_
  85.9 2.3 %collective-permute-start.10 = (bf16[32,1024]{1,0:T(8,128)(2,1)S(1)}, bf16[32,1024]{1,0:T(8,128)(2,1)S(1)}, u32[]{:S(2)}, u32[]{:S(2)}) collective-permute-start(bf16[32,1024]{1,0:T(8,128)(2,1)S(1)} %get-tuple-element.43), channel_id=1, source_target_pairs={{0,20},{1,21},{2,22},{3,23},{4,16},{5,17},{6,18},{7,19},{8,28},{9,... | collective-permute-start | bytes 196616 | tf_op jit(solution)/shard_map/ppermute | solution.py:155
  88.2 0.0 collective-permute-done.6.refs_7_
  88.2 1.5 collective-permute-start.11
  89.7 0.0 collective-permute-done.7.refs_8_
  89.7 0.7 collective-permute-start.12
  90.3 5.7 %collective-permute-done.8.refs_9_ = bf16[32,1024]{1,0:T(8,128)(2,1)S(1)} collective-permute-done((bf16[32,1024]{1,0:T(8,128)(2,1)S(1)}, bf16[32,1024]{1,0:T(8,128)(2,1)S(1)}, u32[]{:S(2)}, u32[]{:S(2)}) %collective-permute-start.8) | collective-permute-done | bytes 65568 | tf_op jit(solution)/shard_map/ppermute | solution.py:155
  96.1 2.2 %collective-permute-start.13 = (bf16[32,1024]{1,0:T(8,128)(2,1)S(1)}, bf16[32,1024]{1,0:T(8,128)(2,1)S(1)}, u32[]{:S(2)}, u32[]{:S(2)}) collective-permute-start(bf16[32,1024]{1,0:T(8,128)(2,1)S(1)} %get-tuple-element.46), channel_id=1, source_target_pairs={{0,26},{1,27},{2,24},{3,25},{4,30},{5,31},{6,28},{7,29},{8,18},{9,... | collective-permute-start | bytes 196616 | tf_op jit(solution)/shard_map/ppermute | solution.py:155
  98.3 0.1 collective-permute-done.9.refs_10_
  98.4 3.4 %collective-permute-start.14 = (bf16[32,1024]{1,0:T(8,128)(2,1)S(1)}, bf16[32,1024]{1,0:T(8,128)(2,1)S(1)}, u32[]{:S(2)}, u32[]{:S(2)}) collective-permute-start(bf16[32,1024]{1,0:T(8,128)(2,1)S(1)} %get-tuple-element.47), channel_id=1, source_target_pairs={{0,28},{1,29},{2,30},{3,31},{4,24},{5,25},{6,26},{7,27},{8,20},{9,... | collective-permute-start | bytes 196616 | tf_op jit(solution)/shard_map/ppermute | solution.py:155
  101.7 0.0 collective-permute-done.10.refs_11_
  101.7 1.4 collective-permute-start.15
  103.1 1.1 collective-permute-done.11.refs_12_
  104.2 0.0 collective-permute-done.12.refs_13_
  104.2 0.0 collective-permute-done.13.refs_14_
  104.2 1.3 collective-permute-done.14.refs_15_
  105.5 4.2 %collective-permute-done.15.refs_16_ = bf16[32,1024]{1,0:T(8,128)(2,1)S(1)} collective-permute-done((bf16[32,1024]{1,0:T(8,128)(2,1)S(1)}, bf16[32,1024]{1,0:T(8,128)(2,1)S(1)}, u32[]{:S(2)}, u32[]{:S(2)}) %collective-permute-start.15) | collective-permute-done | bytes 65568 | tf_op jit(solution)/shard_map/ppermute | solution.py:155
  109.7 1.2 settle.1
  110.9 0.0 copy-start.4
  110.9 6.2 %fusion.5 = bf16[2048,512]{0,1:T(8,128)(2,1)S(1)} fusion(f32[512,2048]{1,0:T(8,128)} %get-tuple-element.61, bf16[512,1024]{1,0:T(8,128)(2,1)} %settle.1, bf16[1,2048,1024]{2,1,0:T(8,128)(2,1)} %param.8), kind=kOutput, calls=%fused_computation.6 | convolution fusion | flops 2157969408 | bytes 11534336 | tf_op jit(solution)/shard_map/dot_general | solution.py:314
  117.1 0.0 copy-start.7
  117.2 1.3 copy-done.7
  118.5 3.3 %fusion.20 = bf16[512,1024]{1,0:T(8,128)(2,1)} fusion(bf16[2048,512]{0,1:T(8,128)(2,1)S(1)} %fusion.5, bf16[1,2048,1024]{2,1,0:T(8,128)(2,1)S(1)} %copy-done.4), kind=kOutput, calls=%fused_computation.25 | convolution fusion | flops 2148007936 | bytes 7340032 | tf_op jit(solution)/shard_map/dot_general | solution.py:319
  121.8 0.0 all-to-all-done.2
  121.8 2.8 %all-to-all-start.3 = ((bf16[32,16,1024]{2,1,0:T(8,128)(2,1)}), bf16[32,16,1024]{2,1,0:T(8,128)(2,1)S(1)}, u32[]{:S(2)}, u32[]{:S(2)}) async-start(bf16[32,16,1024]{2,1,0:T(8,128)(2,1)} %bitcast.76), calls=%async_computation.3 | async-start | bytes 2097152 | tf_op jit(solution)/shard_map/all_to_all | solution.py:263
  124.6 0.4 turn.1
  125.0 0.0 copy-start
  125.0 0.0 copy-start.1
  125.0 1.3 fusion.26
  126.3 0.3 copy-done
  126.6 1.2 copy-done.1
  127.8 4.1 %subtract_convert_fusion = (bf16[64,16,1024]{2,1,0:T(8,128)(2,1)}, f32[64,16,1024]{2,1,0:T(8,128)}) fusion(bf16[64,16,1024]{2,1,0:T(8,128)(2,1)S(1)} %copy-done, f32[64,16,1024]{2,1,0:T(8,128)S(1)} %bitcast.71, f32[64,16,1024]{2,1,0:T(8,128)S(1)} %copy-done.1), kind=kLoop, calls=%fused_computation.21 | loop fusion | flops 6291456 | bytes 16777216 | tf_op jit(solution)/shard_map/convert_element_type | solution.py:296
  131.9 4.4 %convolution_convert_fusion.1 = bf16[2048,1024]{1,0:T(8,128)(2,1)} fusion(bf16[2048,512]{0,1:T(8,128)(2,1)S(1)} %copy-done.6, bf16[512,1024]{1,0:T(8,128)(2,1)S(1)} %copy-done.2), kind=kOutput, calls=%fused_computation.24 | convolution fusion | flops 2149580800 | bytes 7340032 | tf_op jit(solution)/shard_map/dot_general | solution.py:325
  136.3 4.4 %convolution_convert_fusion = bf16[2048,1024]{1,0:T(8,128)(2,1)} fusion(bf16[2048,512]{0,1:T(8,128)(2,1)S(1)} %copy-done.8, bf16[512,1024]{1,0:T(8,128)(2,1)S(1)} %bitcast.73), kind=kOutput, calls=%fused_computation.23 | convolution fusion | flops 2149580800 | bytes 7340032 | tf_op jit(solution)/shard_map/dot_general | solution.py:326
  140.7 1.6 %fetch.3 = bf16[64,16,1024]{2,1,0:T(8,128)(2,1)S(1)} custom-call(bf16[64,16,1024]{2,1,0:T(8,128)(2,1)} %refs_0_.2), custom_call_target="tpu_custom_call" | custom-call | tf_op jit(solution)/shard_map/fetch/pallas_call | solution.py:192
  142.3 8.3 %all-to-all-done.3 = bf16[32,16,1024]{2,1,0:T(8,128)(2,1)S(1)} async-done(((bf16[32,16,1024]{2,1,0:T(8,128)(2,1)}), bf16[32,16,1024]{2,1,0:T(8,128)(2,1)S(1)}, u32[]{:S(2)}, u32[]{:S(2)}) %all-to-all-start.3) | async-done | bytes 1048608 | tf_op jit(solution)/shard_map/all_to_all | solution.py:263
  150.6 5.1 %update_last.1 = (f32[1024,1024]{1,0:T(8,128)}, bf16[1024,1024]{1,0:T(8,128)(2,1)}) custom-call(s32[32,1,64]{2,1,0:T(1,128)S(1)} %all-to-all-done.route_ref, bf16[512,1024]{1,0:T(8,128)(2,1)S(1)} %bitcast.67, bf16[1024,1024]{1,0:T(8,128)(2,1)S(1)} %bitcast.65, f32[1024,1024]{1,0:T(8,128)} %bitcast.69), custom_call_target="tpu_custom_call" | custom-call | tf_op jit(solution)/shard_map/update_last/pallas_call | solution.py:241
  (11 shorter events, 0.0 us)
Async XLA Ops:
  1.9 14.4 %all-to-all-start = ((s32[32,1,64]{2,1,0:T(1,128)}), s32[32,1,64]{2,1,0:T(1,128)S(1)}, u32[]{:S(2)}, u32[]{:S(2)}) async-start(s32[32,1,64]{2,1,0:T(1,128)} %broadcast_in_dim.19), calls=%async_computation | async-start | bytes 32768 | tf_op jit(solution)/shard_map/all_to_all | solution.py:263
  18.5 28.9 %all-to-all-start.1 = ((bf16[32,16,1024]{2,1,0:T(8,128)(2,1)}), bf16[32,16,1024]{2,1,0:T(8,128)(2,1)S(1)}, u32[]{:S(2)}, u32[]{:S(2)}) async-start(bf16[32,16,1024]{2,1,0:T(8,128)(2,1)} %bitcast.70), calls=%async_computation.1 | async-start | bytes 2097152 | tf_op jit(solution)/shard_map/all_to_all | solution.py:263
  25.2 35.7 %collective-permute-start = (bf16[256,1024]{1,0:T(8,128)(2,1)}, bf16[256,1024]{1,0:T(8,128)(2,1)S(1)}, u32[]{:S(2)}, u32[]{:S(2)}) collective-permute-start(bf16[256,1024]{1,0:T(8,128)(2,1)} %get-tuple-element.33), channel_id=1, source_target_pairs={{0,1},{1,0},{2,3},{3,2},{4,5},{5,4},{6,7},{7,6},{8,9},{9,8},{10,11... | collective-permute-start | bytes 1572872 | tf_op jit(solution)/shard_map/ppermute | solution.py:155
  47.3 6.6 %copy-start.3 = (bf16[1,2048,1024]{2,1,0:T(8,128)(2,1)S(1)}, bf16[1,2048,1024]{2,1,0:T(8,128)(2,1)}, u32[]{:S(2)}) copy-start(bf16[1,2048,1024]{2,1,0:T(8,128)(2,1)} %param.8) | copy-start | bytes 12582916
  54.0 3.3 %copy-start.5 = (bf16[2048,512]{0,1:T(8,128)(2,1)}, bf16[2048,512]{0,1:T(8,128)(2,1)S(1)}, u32[]{:S(2)}) copy-start(bf16[2048,512]{0,1:T(8,128)(2,1)S(1)} %get-tuple-element.49) | copy-start | bytes 6291460
  57.3 64.5 %all-to-all-start.2 = ((bf16[32,16,1024]{2,1,0:T(8,128)(2,1)}), bf16[32,16,1024]{2,1,0:T(8,128)(2,1)S(1)}, u32[]{:S(2)}, u32[]{:S(2)}) async-start(bf16[32,16,1024]{2,1,0:T(8,128)(2,1)} %bitcast.75), calls=%async_computation.2 | async-start | bytes 2097152 | tf_op jit(solution)/shard_map/all_to_all | solution.py:263
  61.0 11.7 %collective-permute-start.1 = (bf16[32,1024]{1,0:T(8,128)(2,1)S(1)}, bf16[32,1024]{1,0:T(8,128)(2,1)S(1)}, u32[]{:S(2)}, u32[]{:S(2)}) collective-permute-start(bf16[32,1024]{1,0:T(8,128)(2,1)S(1)} %get-tuple-element.34), channel_id=1, source_target_pairs={{0,2},{1,3},{2,0},{3,1},{4,6},{5,7},{6,4},{7,5},{8,10},{9,11},{10,... | collective-permute-start | bytes 196616 | tf_op jit(solution)/shard_map/ppermute | solution.py:155
  62.8 10.9 %collective-permute-start.2 = (bf16[32,1024]{1,0:T(8,128)(2,1)S(1)}, bf16[32,1024]{1,0:T(8,128)(2,1)S(1)}, u32[]{:S(2)}, u32[]{:S(2)}) collective-permute-start(bf16[32,1024]{1,0:T(8,128)(2,1)S(1)} %get-tuple-element.35), channel_id=1, source_target_pairs={{0,4},{1,5},{2,6},{3,7},{4,0},{5,1},{6,2},{7,3},{8,12},{9,13},{10,... | collective-permute-start | bytes 196616 | tf_op jit(solution)/shard_map/ppermute | solution.py:155
  64.3 12.3 %collective-permute-start.3 = (bf16[32,1024]{1,0:T(8,128)(2,1)S(1)}, bf16[32,1024]{1,0:T(8,128)(2,1)S(1)}, u32[]{:S(2)}, u32[]{:S(2)}) collective-permute-start(bf16[32,1024]{1,0:T(8,128)(2,1)S(1)} %get-tuple-element.36), channel_id=1, source_target_pairs={{0,6},{1,7},{2,4},{3,5},{4,2},{5,3},{6,0},{7,1},{8,14},{9,15},{10,... | collective-permute-start | bytes 196616 | tf_op jit(solution)/shard_map/ppermute | solution.py:155
  64.5 15.7 %collective-permute-start.4 = (bf16[32,1024]{1,0:T(8,128)(2,1)S(1)}, bf16[32,1024]{1,0:T(8,128)(2,1)S(1)}, u32[]{:S(2)}, u32[]{:S(2)}) collective-permute-start(bf16[32,1024]{1,0:T(8,128)(2,1)S(1)} %get-tuple-element.37), channel_id=1, source_target_pairs={{0,8},{1,9},{2,10},{3,11},{4,12},{5,13},{6,14},{7,15},{8,0},{9,1},... | collective-permute-start | bytes 196616 | tf_op jit(solution)/shard_map/ppermute | solution.py:155
  66.3 19.6 %collective-permute-start.5 = (bf16[32,1024]{1,0:T(8,128)(2,1)S(1)}, bf16[32,1024]{1,0:T(8,128)(2,1)S(1)}, u32[]{:S(2)}, u32[]{:S(2)}) collective-permute-start(bf16[32,1024]{1,0:T(8,128)(2,1)S(1)} %get-tuple-element.38), channel_id=1, source_target_pairs={{0,10},{1,11},{2,8},{3,9},{4,14},{5,15},{6,12},{7,13},{8,2},{9,3},... | collective-permute-start | bytes 196616 | tf_op jit(solution)/shard_map/ppermute | solution.py:155
  72.7 15.5 %collective-permute-start.6 = (bf16[32,1024]{1,0:T(8,128)(2,1)S(1)}, bf16[32,1024]{1,0:T(8,128)(2,1)S(1)}, u32[]{:S(2)}, u32[]{:S(2)}) collective-permute-start(bf16[32,1024]{1,0:T(8,128)(2,1)S(1)} %get-tuple-element.39), channel_id=1, source_target_pairs={{0,12},{1,13},{2,14},{3,15},{4,8},{5,9},{6,10},{7,11},{8,4},{9,5},... | collective-permute-start | bytes 196616 | tf_op jit(solution)/shard_map/ppermute | solution.py:155
  73.7 15.9 %collective-permute-start.7 = (bf16[32,1024]{1,0:T(8,128)(2,1)S(1)}, bf16[32,1024]{1,0:T(8,128)(2,1)S(1)}, u32[]{:S(2)}, u32[]{:S(2)}) collective-permute-start(bf16[32,1024]{1,0:T(8,128)(2,1)S(1)} %get-tuple-element.40), channel_id=1, source_target_pairs={{0,14},{1,15},{2,12},{3,13},{4,10},{5,11},{6,8},{7,9},{8,6},{9,7},... | collective-permute-start | bytes 196616 | tf_op jit(solution)/shard_map/ppermute | solution.py:155
  76.6 19.5 %collective-permute-start.8 = (bf16[32,1024]{1,0:T(8,128)(2,1)S(1)}, bf16[32,1024]{1,0:T(8,128)(2,1)S(1)}, u32[]{:S(2)}, u32[]{:S(2)}) collective-permute-start(bf16[32,1024]{1,0:T(8,128)(2,1)S(1)} %get-tuple-element.41), channel_id=1, source_target_pairs={{0,16},{1,17},{2,18},{3,19},{4,20},{5,21},{6,22},{7,23},{8,24},{9,... | collective-permute-start | bytes 196616 | tf_op jit(solution)/shard_map/ppermute | solution.py:155
  80.2 18.2 %collective-permute-start.9 = (bf16[32,1024]{1,0:T(8,128)(2,1)S(1)}, bf16[32,1024]{1,0:T(8,128)(2,1)S(1)}, u32[]{:S(2)}, u32[]{:S(2)}) collective-permute-start(bf16[32,1024]{1,0:T(8,128)(2,1)S(1)} %get-tuple-element.42), channel_id=1, source_target_pairs={{0,18},{1,19},{2,16},{3,17},{4,22},{5,23},{6,20},{7,21},{8,26},{9,... | collective-permute-start | bytes 196616 | tf_op jit(solution)/shard_map/ppermute | solution.py:155
  85.9 15.9 %collective-permute-start.10 = (bf16[32,1024]{1,0:T(8,128)(2,1)S(1)}, bf16[32,1024]{1,0:T(8,128)(2,1)S(1)}, u32[]{:S(2)}, u32[]{:S(2)}) collective-permute-start(bf16[32,1024]{1,0:T(8,128)(2,1)S(1)} %get-tuple-element.43), channel_id=1, source_target_pairs={{0,20},{1,21},{2,22},{3,23},{4,16},{5,17},{6,18},{7,19},{8,28},{9,... | collective-permute-start | bytes 196616 | tf_op jit(solution)/shard_map/ppermute | solution.py:155
  88.2 16.0 %collective-permute-start.11 = (bf16[32,1024]{1,0:T(8,128)(2,1)S(1)}, bf16[32,1024]{1,0:T(8,128)(2,1)S(1)}, u32[]{:S(2)}, u32[]{:S(2)}) collective-permute-start(bf16[32,1024]{1,0:T(8,128)(2,1)S(1)} %get-tuple-element.44), channel_id=1, source_target_pairs={{0,22},{1,23},{2,20},{3,21},{4,18},{5,19},{6,16},{7,17},{8,30},{9,... | collective-permute-start | bytes 196616 | tf_op jit(solution)/shard_map/ppermute | solution.py:155
  89.7 14.5 %collective-permute-start.12 = (bf16[32,1024]{1,0:T(8,128)(2,1)S(1)}, bf16[32,1024]{1,0:T(8,128)(2,1)S(1)}, u32[]{:S(2)}, u32[]{:S(2)}) collective-permute-start(bf16[32,1024]{1,0:T(8,128)(2,1)S(1)} %get-tuple-element.45), channel_id=1, source_target_pairs={{0,24},{1,25},{2,26},{3,27},{4,28},{5,29},{6,30},{7,31},{8,16},{9,... | collective-permute-start | bytes 196616 | tf_op jit(solution)/shard_map/ppermute | solution.py:155
  96.1 8.2 %collective-permute-start.13 = (bf16[32,1024]{1,0:T(8,128)(2,1)S(1)}, bf16[32,1024]{1,0:T(8,128)(2,1)S(1)}, u32[]{:S(2)}, u32[]{:S(2)}) collective-permute-start(bf16[32,1024]{1,0:T(8,128)(2,1)S(1)} %get-tuple-element.46), channel_id=1, source_target_pairs={{0,26},{1,27},{2,24},{3,25},{4,30},{5,31},{6,28},{7,29},{8,18},{9,... | collective-permute-start | bytes 196616 | tf_op jit(solution)/shard_map/ppermute | solution.py:155
  98.4 7.2 %collective-permute-start.14 = (bf16[32,1024]{1,0:T(8,128)(2,1)S(1)}, bf16[32,1024]{1,0:T(8,128)(2,1)S(1)}, u32[]{:S(2)}, u32[]{:S(2)}) collective-permute-start(bf16[32,1024]{1,0:T(8,128)(2,1)S(1)} %get-tuple-element.47), channel_id=1, source_target_pairs={{0,28},{1,29},{2,30},{3,31},{4,24},{5,25},{6,26},{7,27},{8,20},{9,... | collective-permute-start | bytes 196616 | tf_op jit(solution)/shard_map/ppermute | solution.py:155
  101.7 8.0 %collective-permute-start.15 = (bf16[32,1024]{1,0:T(8,128)(2,1)S(1)}, bf16[32,1024]{1,0:T(8,128)(2,1)S(1)}, u32[]{:S(2)}, u32[]{:S(2)}) collective-permute-start(bf16[32,1024]{1,0:T(8,128)(2,1)S(1)} %get-tuple-element.48), channel_id=1, source_target_pairs={{0,30},{1,31},{2,28},{3,29},{4,26},{5,27},{6,24},{7,25},{8,22},{9,... | collective-permute-start | bytes 196616 | tf_op jit(solution)/shard_map/ppermute | solution.py:155
  110.9 7.5 %copy-start.4 = (bf16[1,2048,1024]{2,1,0:T(8,128)(2,1)S(1)}, bf16[1,2048,1024]{2,1,0:T(8,128)(2,1)}, u32[]{:S(2)}) copy-start(bf16[1,2048,1024]{2,1,0:T(8,128)(2,1)} %param.7) | copy-start | bytes 12582916
  117.1 1.3 copy-start.7
  121.8 28.9 %all-to-all-start.3 = ((bf16[32,16,1024]{2,1,0:T(8,128)(2,1)}), bf16[32,16,1024]{2,1,0:T(8,128)(2,1)S(1)}, u32[]{:S(2)}, u32[]{:S(2)}) async-start(bf16[32,16,1024]{2,1,0:T(8,128)(2,1)} %bitcast.76), calls=%async_computation.3 | async-start | bytes 2097152 | tf_op jit(solution)/shard_map/all_to_all | solution.py:263
  125.0 1.6 %copy-start = (bf16[64,16,1024]{2,1,0:T(8,128)(2,1)S(1)}, bf16[64,16,1024]{2,1,0:T(8,128)(2,1)}, u32[]{:S(2)}) copy-start(bf16[64,16,1024]{2,1,0:T(8,128)(2,1)} %param.11) | copy-start | bytes 6291460
  125.0 2.8 %copy-start.1 = (f32[64,16,1024]{2,1,0:T(8,128)S(1)}, f32[64,16,1024]{2,1,0:T(8,128)}, u32[]{:S(2)}) copy-start(f32[64,16,1024]{2,1,0:T(8,128)} %param.13) | copy-start | bytes 12582916
  127.8 4.1 %copy-start.2 = (bf16[512,1024]{1,0:T(8,128)(2,1)S(1)}, bf16[512,1024]{1,0:T(8,128)(2,1)}, u32[]{:S(2)}) copy-start(bf16[512,1024]{1,0:T(8,128)(2,1)} %settle.1) | copy-start | bytes 3145732
  127.8 4.1 %copy-start.6 = (bf16[2048,512]{0,1:T(8,128)(2,1)S(1)}, bf16[2048,512]{0,1:T(8,128)(2,1)}, u32[]{:S(2)}) copy-start(bf16[2048,512]{0,1:T(8,128)(2,1)} %copy-done.5) | copy-start | bytes 6291460
  131.9 4.4 %copy-start.8 = (bf16[2048,512]{0,1:T(8,128)(2,1)S(1)}, bf16[2048,512]{0,1:T(8,128)(2,1)}, u32[]{:S(2)}) copy-start(bf16[2048,512]{0,1:T(8,128)(2,1)} %copy-done.7) | copy-start | bytes 6291460

commit v6 on v5

--- a/solution.py
+++ b/solution.py
@@ -8,7 +8,8 @@
 from jax.sharding import PartitionSpec as P
 
 
-PIECES = 4
+PIECES = 8
+STRIDE = 4
 TOP = 16
 
 
@@ -202,7 +203,7 @@
 
 def update_kernel(
     count, rows, route_ref, grad_ref, weight_ref, momentum_hbm, new_momentum_hbm, new_hbm,
-    mixer_ref, momentum_ref, new_ref, in_sems, out_sems,
+    mixer_ref, part_ref, momentum_ref, new_ref, in_sems, out_sems,
 ):
     lines = momentum_ref.shape[0] // count
     parts = [slice(i * lines, (i + 1) * lines) for i in range(count)]
@@ -214,10 +215,15 @@
         read.start()
     turn_kernel(rows, route_ref, mixer_ref)
     writes = []
+    stride = min(STRIDE, count)
     for i, here in enumerate(parts):
-        part = jnp.dot(mixer_ref[here, :], grad_ref[...], preferred_element_type=jnp.float32)
+        if i % stride == 0:
+            ahead = slice(i * lines, (i + stride) * lines)
+            part_ref[ahead, :] = jnp.dot(
+                mixer_ref[ahead, :], grad_ref[...], preferred_element_type=jnp.float32
+            )
         reads[i].wait()
-        moved = 0.9 * momentum_ref[here, :] + part
+        moved = 0.9 * momentum_ref[here, :] + part_ref[here, :]
         momentum_ref[here, :] = moved
         rounded = weight_ref[here, :].astype(jnp.float32) - 0.01 * moved
         new_ref[here, :] = rounded.astype(jnp.bfloat16)
@@ -249,11 +255,12 @@
         scratch_shapes=[
             pltpu.VMEM((lines, grads.shape[0]), jnp.bfloat16),
             pltpu.VMEM((lines, width), jnp.float32),
+            pltpu.VMEM((lines, width), jnp.float32),
             pltpu.VMEM((lines, width), jnp.bfloat16),
             pltpu.SemaphoreType.DMA((count,)),
             pltpu.SemaphoreType.DMA((count, 2)),
         ],
-        compiler_params=pltpu.CompilerParams(vmem_limit_bytes=14 << 20),
+        compiler_params=pltpu.CompilerParams(vmem_limit_bytes=20 << 20),
         name="update_last",
     )(routes, grads, weights, momentum)
     return new_momentum.reshape(experts, rows, width), new.reshape(experts, rows, width)

time: 156 us -> 156 us (level)
  no operation moved by 1% of the time
where the time goes in v6:
time: 156 us; the launch traced here: 155 us
  waiting for transfers between devices  55 us (35%)
  starting transfers between devices  46.1 us (30%)
  matrix products  29.6 us (19%)
  Pallas kernels  15.3 us (10%)
  local copies, waits for them, and re-layouts  4.16 us (3%)
  other arithmetic  4.07 us (3%)
    all_to_all x4, waiting for transfers between devices, exchange(): lax.all_to_all(blocks, 'seg', split_axis=0, concat_axis=0, tiled=True)  35.8 us
    ppermute x16, starting transfers between devices, swap(): return lax.ppermute(block, 'seg', [(i, i ^ apart) for i in range(segs)])  29.7 us
    ppermute x16, waiting for transfers between devices, swap(): return lax.ppermute(block, 'seg', [(i, i ^ apart) for i in range(segs)])  19.2 us
    all_to_all x4, starting transfers between devices, exchange(): lax.all_to_all(blocks, 'seg', split_axis=0, concat_axis=0, tiled=True)  16.4 us
    dot_general x1, matrix products, step(): lax.dot_general(inputs, up, (((1,), (1,)), ((), ())), preferred_element_t...  6.64 us
    dot_general x1, matrix products, step(): lax.dot_general(grads, down, (((1,), (1,)), ((), ())), preferred_element_...  6.19 us
    pallas_call x2, Pallas kernels, mix_call(): pl.pallas_call(functools.partial(mix_kernel, rows, top, resident), in_spe...  6.16 us
    dot_general x1, matrix products, step(): jnp.dot(act, down, preferred_element_type=jnp.float32).astype(jnp.bfloat16)  4.41 us
  transfers between devices with their start and end apart: 20, of which 10 were waited for; matrix products, arithmetic and copies ran while one was open for 22% of the time, Pallas kernels for 6%

profile of v6, /device:TPU:0, one launch (start us, length us, event | category | flops | bytes accessed | tf_op | source)
XLA Modules:
  0.0 155.1 jit_solution(9829096779466521917)
XLA Ops:
  0.6 1.3 broadcast_in_dim.19
  1.9 7.3 %all-to-all-start = ((s32[32,1,64]{2,1,0:T(1,128)}), s32[32,1,64]{2,1,0:T(1,128)S(1)}, u32[]{:S(2)}, u32[]{:S(2)}) async-start(s32[32,1,64]{2,1,0:T(1,128)} %broadcast_in_dim.19), calls=%async_computation | async-start | bytes 32768 | tf_op jit(solution)/shard_map/all_to_all | solution.py:270
  9.2 1.6 %fetch.2 = bf16[64,16,1024]{2,1,0:T(8,128)(2,1)S(1)} custom-call(bf16[64,16,1024]{2,1,0:T(8,128)(2,1)} %refs_0_.2), custom_call_target="tpu_custom_call" | custom-call | tf_op jit(solution)/shard_map/fetch/pallas_call | solution.py:193
  10.8 5.5 %all-to-all-done.route_ref = s32[32,1,64]{2,1,0:T(1,128)S(1)} async-done(((s32[32,1,64]{2,1,0:T(1,128)}), s32[32,1,64]{2,1,0:T(1,128)S(1)}, u32[]{:S(2)}, u32[]{:S(2)}) %all-to-all-start) | async-done | bytes 8224 | tf_op jit(solution)/shard_map/all_to_all | solution.py:270
  16.3 2.1 %mix.2 = bf16[512,1024]{1,0:T(8,128)(2,1)} custom-call(s32[1]{0:T(128)} %bitcast.me_ref, s32[32,1,64]{2,1,0:T(1,128)S(1)} %all-to-all-done.route_ref, bf16[1024,1024]{1,0:T(8,128)(2,1)S(1)} %bitcast.66), custom_call_target="tpu_custom_call" | custom-call | tf_op jit(solution)/shard_map/mix/pallas_call | solution.py:86
  18.5 2.7 %all-to-all-start.1 = ((bf16[32,16,1024]{2,1,0:T(8,128)(2,1)}), bf16[32,16,1024]{2,1,0:T(8,128)(2,1)S(1)}, u32[]{:S(2)}, u32[]{:S(2)}) async-start(bf16[32,16,1024]{2,1,0:T(8,128)(2,1)} %bitcast.70), calls=%async_computation.1 | async-start | bytes 2097152 | tf_op jit(solution)/shard_map/all_to_all | solution.py:270
  21.1 4.0 %mix.3 = (bf16[256,1024]{1,0:T(8,128)(2,1)S(1)}, bf16[256,1024]{1,0:T(8,128)(2,1)}) custom-call(s32[1]{0:T(128)} %bitcast.me_ref, s32[32,1,64]{2,1,0:T(1,128)S(1)} %all-to-all-done.route_ref, bf16[1024,1024]{1,0:T(8,128)(2,1)} %bitcast.68), custom_call_target="tpu_custom_call" | custom-call | tf_op jit(solution)/shard_map/mix/pallas_call | solution.py:86
  25.2 0.2 collective-permute-start
  25.4 22.0 %all-to-all-done.1 = bf16[32,16,1024]{2,1,0:T(8,128)(2,1)S(1)} async-done(((bf16[32,16,1024]{2,1,0:T(8,128)(2,1)}), bf16[32,16,1024]{2,1,0:T(8,128)(2,1)S(1)}, u32[]{:S(2)}, u32[]{:S(2)}) %all-to-all-start.1) | async-done | bytes 1048608 | tf_op jit(solution)/shard_map/all_to_all | solution.py:270
  47.3 6.6 %fusion.11 = (bf16[2048,512]{0,1:T(8,128)(2,1)S(1)}, f32[512,2048]{1,0:T(8,128)}) fusion(bf16[512,1024]{1,0:T(8,128)(2,1)S(1)} %bitcast.72, bf16[1,2048,1024]{2,1,0:T(8,128)(2,1)} %param.7), kind=kOutput, calls=%fused_computation.14 | convolution fusion | flops 2152726528 | bytes 11534336 | tf_op jit(solution)/shard_map/dot_general | solution.py:315
  54.0 3.3 %fusion.23 = bf16[512,1024]{1,0:T(8,128)(2,1)} fusion(bf16[2048,512]{0,1:T(8,128)(2,1)S(1)} %get-tuple-element.49, bf16[1,2048,1024]{2,1,0:T(8,128)(2,1)S(1)} %copy-done.3), kind=kOutput, calls=%fused_computation.26 | convolution fusion | flops 2148007936 | bytes 7340032 | tf_op jit(solution)/shard_map/dot_general | solution.py:319
  57.3 3.5 %all-to-all-start.2 = ((bf16[32,16,1024]{2,1,0:T(8,128)(2,1)}), bf16[32,16,1024]{2,1,0:T(8,128)(2,1)S(1)}, u32[]{:S(2)}, u32[]{:S(2)}) async-start(bf16[32,16,1024]{2,1,0:T(8,128)(2,1)} %bitcast.75), calls=%async_computation.2 | async-start | bytes 2097152 | tf_op jit(solution)/shard_map/all_to_all | solution.py:270
  60.9 0.0 collective-permute-done.refs_1_
  60.9 0.1 regroup.1
  61.0 1.8 %collective-permute-start.1 = (bf16[32,1024]{1,0:T(8,128)(2,1)S(1)}, bf16[32,1024]{1,0:T(8,128)(2,1)S(1)}, u32[]{:S(2)}, u32[]{:S(2)}) collective-permute-start(bf16[32,1024]{1,0:T(8,128)(2,1)S(1)} %get-tuple-element.34), channel_id=1, source_target_pairs={{0,2},{1,3},{2,0},{3,1},{4,6},{5,7},{6,4},{7,5},{8,10},{9,11},{10,... | collective-permute-start | bytes 196616 | tf_op jit(solution)/shard_map/ppermute | solution.py:156
  62.8 1.5 collective-permute-start.2
  64.3 0.3 collective-permute-start.3
  64.5 1.8 %collective-permute-start.4 = (bf16[32,1024]{1,0:T(8,128)(2,1)S(1)}, bf16[32,1024]{1,0:T(8,128)(2,1)S(1)}, u32[]{:S(2)}, u32[]{:S(2)}) collective-permute-start(bf16[32,1024]{1,0:T(8,128)(2,1)S(1)} %get-tuple-element.37), channel_id=1, source_target_pairs={{0,8},{1,9},{2,10},{3,11},{4,12},{5,13},{6,14},{7,15},{8,0},{9,1},... | collective-permute-start | bytes 196616 | tf_op jit(solution)/shard_map/ppermute | solution.py:156
  66.3 1.5 collective-permute-start.5
  67.7 4.9 %collective-permute-done.1.refs_2_ = bf16[32,1024]{1,0:T(8,128)(2,1)S(1)} collective-permute-done((bf16[32,1024]{1,0:T(8,128)(2,1)S(1)}, bf16[32,1024]{1,0:T(8,128)(2,1)S(1)}, u32[]{:S(2)}, u32[]{:S(2)}) %collective-permute-start.1) | collective-permute-done | bytes 65568 | tf_op jit(solution)/shard_map/ppermute | solution.py:156
  72.7 1.1 collective-permute-start.6
  73.7 0.0 collective-permute-done.2.refs_3_
  73.7 2.8 %collective-permute-start.7 = (bf16[32,1024]{1,0:T(8,128)(2,1)S(1)}, bf16[32,1024]{1,0:T(8,128)(2,1)S(1)}, u32[]{:S(2)}, u32[]{:S(2)}) collective-permute-start(bf16[32,1024]{1,0:T(8,128)(2,1)S(1)} %get-tuple-element.40), channel_id=1, source_target_pairs={{0,14},{1,15},{2,12},{3,13},{4,10},{5,11},{6,8},{7,9},{8,6},{9,7},... | collective-permute-start | bytes 196616 | tf_op jit(solution)/shard_map/ppermute | solution.py:156
  76.6 0.0 collective-permute-done.3.refs_4_
  76.6 1.8 %collective-permute-start.8 = (bf16[32,1024]{1,0:T(8,128)(2,1)S(1)}, bf16[32,1024]{1,0:T(8,128)(2,1)S(1)}, u32[]{:S(2)}, u32[]{:S(2)}) collective-permute-start(bf16[32,1024]{1,0:T(8,128)(2,1)S(1)} %get-tuple-element.41), channel_id=1, source_target_pairs={{0,16},{1,17},{2,18},{3,19},{4,20},{5,21},{6,22},{7,23},{8,24},{9,... | collective-permute-start | bytes 196616 | tf_op jit(solution)/shard_map/ppermute | solution.py:156
  78.3 1.9 %collective-permute-done.4.refs_5_ = bf16[32,1024]{1,0:T(8,128)(2,1)S(1)} collective-permute-done((bf16[32,1024]{1,0:T(8,128)(2,1)S(1)}, bf16[32,1024]{1,0:T(8,128)(2,1)S(1)}, u32[]{:S(2)}, u32[]{:S(2)}) %collective-permute-start.4) | collective-permute-done | bytes 65568 | tf_op jit(solution)/shard_map/ppermute | solution.py:156
  80.2 5.6 %collective-permute-start.9 = (bf16[32,1024]{1,0:T(8,128)(2,1)S(1)}, bf16[32,1024]{1,0:T(8,128)(2,1)S(1)}, u32[]{:S(2)}, u32[]{:S(2)}) collective-permute-start(bf16[32,1024]{1,0:T(8,128)(2,1)S(1)} %get-tuple-element.42), channel_id=1, source_target_pairs={{0,18},{1,19},{2,16},{3,17},{4,22},{5,23},{6,20},{7,21},{8,26},{9,... | collective-permute-start | bytes 196616 | tf_op jit(solution)/shard_map/ppermute | solution.py:156
  85.9 0.0 collective-permute-done.5.refs_6_
  85.9 2.3 %collective-permute-start.10 = (bf16[32,1024]{1,0:T(8,128)(2,1)S(1)}, bf16[32,1024]{1,0:T(8,128)(2,1)S(1)}, u32[]{:S(2)}, u32[]{:S(2)}) collective-permute-start(bf16[32,1024]{1,0:T(8,128)(2,1)S(1)} %get-tuple-element.43), channel_id=1, source_target_pairs={{0,20},{1,21},{2,22},{3,23},{4,16},{5,17},{6,18},{7,19},{8,28},{9,... | collective-permute-start | bytes 196616 | tf_op jit(solution)/shard_map/ppermute | solution.py:156
  88.2 0.0 collective-permute-done.6.refs_7_
  88.2 1.5 collective-permute-start.11
  89.7 0.0 collective-permute-done.7.refs_8_
  89.7 0.7 collective-permute-start.12
  90.3 5.7 %collective-permute-done.8.refs_9_ = bf16[32,1024]{1,0:T(8,128)(2,1)S(1)} collective-permute-done((bf16[32,1024]{1,0:T(8,128)(2,1)S(1)}, bf16[32,1024]{1,0:T(8,128)(2,1)S(1)}, u32[]{:S(2)}, u32[]{:S(2)}) %collective-permute-start.8) | collective-permute-done | bytes 65568 | tf_op jit(solution)/shard_map/ppermute | solution.py:156
  96.1 2.2 %collective-permute-start.13 = (bf16[32,1024]{1,0:T(8,128)(2,1)S(1)}, bf16[32,1024]{1,0:T(8,128)(2,1)S(1)}, u32[]{:S(2)}, u32[]{:S(2)}) collective-permute-start(bf16[32,1024]{1,0:T(8,128)(2,1)S(1)} %get-tuple-element.46), channel_id=1, source_target_pairs={{0,26},{1,27},{2,24},{3,25},{4,30},{5,31},{6,28},{7,29},{8,18},{9,... | collective-permute-start | bytes 196616 | tf_op jit(solution)/shard_map/ppermute | solution.py:156
  98.3 0.1 collective-permute-done.9.refs_10_
  98.4 3.4 %collective-permute-start.14 = (bf16[32,1024]{1,0:T(8,128)(2,1)S(1)}, bf16[32,1024]{1,0:T(8,128)(2,1)S(1)}, u32[]{:S(2)}, u32[]{:S(2)}) collective-permute-start(bf16[32,1024]{1,0:T(8,128)(2,1)S(1)} %get-tuple-element.47), channel_id=1, source_target_pairs={{0,28},{1,29},{2,30},{3,31},{4,24},{5,25},{6,26},{7,27},{8,20},{9,... | collective-permute-start | bytes 196616 | tf_op jit(solution)/shard_map/ppermute | solution.py:156
  101.7 0.0 collective-permute-done.10.refs_11_
  101.7 1.4 collective-permute-start.15
  103.1 1.1 collective-permute-done.11.refs_12_
  104.2 0.0 collective-permute-done.12.refs_13_
  104.2 0.0 collective-permute-done.13.refs_14_
  104.2 1.3 collective-permute-done.14.refs_15_
  105.5 4.2 %collective-permute-done.15.refs_16_ = bf16[32,1024]{1,0:T(8,128)(2,1)S(1)} collective-permute-done((bf16[32,1024]{1,0:T(8,128)(2,1)S(1)}, bf16[32,1024]{1,0:T(8,128)(2,1)S(1)}, u32[]{:S(2)}, u32[]{:S(2)}) %collective-permute-start.15) | collective-permute-done | bytes 65568 | tf_op jit(solution)/shard_map/ppermute | solution.py:156
  109.7 1.2 settle.1
  110.9 0.0 copy-start.4
  110.9 6.2 %fusion.5 = bf16[2048,512]{0,1:T(8,128)(2,1)S(1)} fusion(f32[512,2048]{1,0:T(8,128)} %get-tuple-element.61, bf16[512,1024]{1,0:T(8,128)(2,1)} %settle.1, bf16[1,2048,1024]{2,1,0:T(8,128)(2,1)} %param.8), kind=kOutput, calls=%fused_computation.6 | convolution fusion | flops 2157969408 | bytes 11534336 | tf_op jit(solution)/shard_map/dot_general | solution.py:321
  117.1 0.0 copy-start.7
  117.2 1.3 copy-done.7
  118.5 3.3 %fusion.20 = bf16[512,1024]{1,0:T(8,128)(2,1)} fusion(bf16[2048,512]{0,1:T(8,128)(2,1)S(1)} %fusion.5, bf16[1,2048,1024]{2,1,0:T(8,128)(2,1)S(1)} %copy-done.4), kind=kOutput, calls=%fused_computation.25 | convolution fusion | flops 2148007936 | bytes 7340032 | tf_op jit(solution)/shard_map/dot_general | solution.py:326
  121.8 0.0 all-to-all-done.2
  121.8 2.8 %all-to-all-start.3 = ((bf16[32,16,1024]{2,1,0:T(8,128)(2,1)}), bf16[32,16,1024]{2,1,0:T(8,128)(2,1)S(1)}, u32[]{:S(2)}, u32[]{:S(2)}) async-start(bf16[32,16,1024]{2,1,0:T(8,128)(2,1)} %bitcast.76), calls=%async_computation.3 | async-start | bytes 2097152 | tf_op jit(solution)/shard_map/all_to_all | solution.py:270
  124.6 0.4 turn.1
  125.0 0.0 copy-start
  125.0 0.0 copy-start.1
  125.0 1.3 fusion.26
  126.3 0.3 copy-done
  126.6 1.2 copy-done.1
  127.8 4.1 %subtract_convert_fusion = (bf16[64,16,1024]{2,1,0:T(8,128)(2,1)}, f32[64,16,1024]{2,1,0:T(8,128)}) fusion(bf16[64,16,1024]{2,1,0:T(8,128)(2,1)S(1)} %copy-done, f32[64,16,1024]{2,1,0:T(8,128)S(1)} %bitcast.71, f32[64,16,1024]{2,1,0:T(8,128)S(1)} %copy-done.1), kind=kLoop, calls=%fused_computation.21 | loop fusion | flops 6291456 | bytes 16777216 | tf_op jit(solution)/shard_map/convert_element_type | solution.py:303
  131.9 4.4 %convolution_convert_fusion.1 = bf16[2048,1024]{1,0:T(8,128)(2,1)} fusion(bf16[2048,512]{0,1:T(8,128)(2,1)S(1)} %copy-done.6, bf16[512,1024]{1,0:T(8,128)(2,1)S(1)} %copy-done.2), kind=kOutput, calls=%fused_computation.24 | convolution fusion | flops 2149580800 | bytes 7340032 | tf_op jit(solution)/shard_map/dot_general | solution.py:332
  136.3 4.4 %convolution_convert_fusion = bf16[2048,1024]{1,0:T(8,128)(2,1)} fusion(bf16[2048,512]{0,1:T(8,128)(2,1)S(1)} %copy-done.8, bf16[512,1024]{1,0:T(8,128)(2,1)S(1)} %bitcast.73), kind=kOutput, calls=%fused_computation.23 | convolution fusion | flops 2149580800 | bytes 7340032 | tf_op jit(solution)/shard_map/dot_general | solution.py:333
  140.7 1.6 %fetch.3 = bf16[64,16,1024]{2,1,0:T(8,128)(2,1)S(1)} custom-call(bf16[64,16,1024]{2,1,0:T(8,128)(2,1)} %refs_0_.2), custom_call_target="tpu_custom_call" | custom-call | tf_op jit(solution)/shard_map/fetch/pallas_call | solution.py:193
  142.3 8.3 %all-to-all-done.3 = bf16[32,16,1024]{2,1,0:T(8,128)(2,1)S(1)} async-done(((bf16[32,16,1024]{2,1,0:T(8,128)(2,1)}), bf16[32,16,1024]{2,1,0:T(8,128)(2,1)S(1)}, u32[]{:S(2)}, u32[]{:S(2)}) %all-to-all-start.3) | async-done | bytes 1048608 | tf_op jit(solution)/shard_map/all_to_all | solution.py:270
  150.6 4.3 %update_last.1 = (f32[1024,1024]{1,0:T(8,128)}, bf16[1024,1024]{1,0:T(8,128)(2,1)}) custom-call(s32[32,1,64]{2,1,0:T(1,128)S(1)} %all-to-all-done.route_ref, bf16[512,1024]{1,0:T(8,128)(2,1)S(1)} %bitcast.67, bf16[1024,1024]{1,0:T(8,128)(2,1)S(1)} %bitcast.65, f32[1024,1024]{1,0:T(8,128)} %bitcast.69), custom_call_target="tpu_custom_call" | custom-call | tf_op jit(solution)/shard_map/update_last/pallas_call | solution.py:247
  (11 shorter events, 0.0 us)
Async XLA Ops:
  1.9 14.4 %all-to-all-start = ((s32[32,1,64]{2,1,0:T(1,128)}), s32[32,1,64]{2,1,0:T(1,128)S(1)}, u32[]{:S(2)}, u32[]{:S(2)}) async-start(s32[32,1,64]{2,1,0:T(1,128)} %broadcast_in_dim.19), calls=%async_computation | async-start | bytes 32768 | tf_op jit(solution)/shard_map/all_to_all | solution.py:270
  18.5 28.9 %all-to-all-start.1 = ((bf16[32,16,1024]{2,1,0:T(8,128)(2,1)}), bf16[32,16,1024]{2,1,0:T(8,128)(2,1)S(1)}, u32[]{:S(2)}, u32[]{:S(2)}) async-start(bf16[32,16,1024]{2,1,0:T(8,128)(2,1)} %bitcast.70), calls=%async_computation.1 | async-start | bytes 2097152 | tf_op jit(solution)/shard_map/all_to_all | solution.py:270
  25.2 35.7 %collective-permute-start = (bf16[256,1024]{1,0:T(8,128)(2,1)}, bf16[256,1024]{1,0:T(8,128)(2,1)S(1)}, u32[]{:S(2)}, u32[]{:S(2)}) collective-permute-start(bf16[256,1024]{1,0:T(8,128)(2,1)} %get-tuple-element.33), channel_id=1, source_target_pairs={{0,1},{1,0},{2,3},{3,2},{4,5},{5,4},{6,7},{7,6},{8,9},{9,8},{10,11... | collective-permute-start | bytes 1572872 | tf_op jit(solution)/shard_map/ppermute | solution.py:156
  47.3 6.6 %copy-start.3 = (bf16[1,2048,1024]{2,1,0:T(8,128)(2,1)S(1)}, bf16[1,2048,1024]{2,1,0:T(8,128)(2,1)}, u32[]{:S(2)}) copy-start(bf16[1,2048,1024]{2,1,0:T(8,128)(2,1)} %param.8) | copy-start | bytes 12582916
  54.0 3.3 %copy-start.5 = (bf16[2048,512]{0,1:T(8,128)(2,1)}, bf16[2048,512]{0,1:T(8,128)(2,1)S(1)}, u32[]{:S(2)}) copy-start(bf16[2048,512]{0,1:T(8,128)(2,1)S(1)} %get-tuple-element.49) | copy-start | bytes 6291460
  57.3 64.5 %all-to-all-start.2 = ((bf16[32,16,1024]{2,1,0:T(8,128)(2,1)}), bf16[32,16,1024]{2,1,0:T(8,128)(2,1)S(1)}, u32[]{:S(2)}, u32[]{:S(2)}) async-start(bf16[32,16,1024]{2,1,0:T(8,128)(2,1)} %bitcast.75), calls=%async_computation.2 | async-start | bytes 2097152 | tf_op jit(solution)/shard_map/all_to_all | solution.py:270
  61.0 11.7 %collective-permute-start.1 = (bf16[32,1024]{1,0:T(8,128)(2,1)S(1)}, bf16[32,1024]{1,0:T(8,128)(2,1)S(1)}, u32[]{:S(2)}, u32[]{:S(2)}) collective-permute-start(bf16[32,1024]{1,0:T(8,128)(2,1)S(1)} %get-tuple-element.34), channel_id=1, source_target_pairs={{0,2},{1,3},{2,0},{3,1},{4,6},{5,7},{6,4},{7,5},{8,10},{9,11},{10,... | collective-permute-start | bytes 196616 | tf_op jit(solution)/shard_map/ppermute | solution.py:156
  62.8 10.9 %collective-permute-start.2 = (bf16[32,1024]{1,0:T(8,128)(2,1)S(1)}, bf16[32,1024]{1,0:T(8,128)(2,1)S(1)}, u32[]{:S(2)}, u32[]{:S(2)}) collective-permute-start(bf16[32,1024]{1,0:T(8,128)(2,1)S(1)} %get-tuple-element.35), channel_id=1, source_target_pairs={{0,4},{1,5},{2,6},{3,7},{4,0},{5,1},{6,2},{7,3},{8,12},{9,13},{10,... | collective-permute-start | bytes 196616 | tf_op jit(solution)/shard_map/ppermute | solution.py:156
  64.3 12.3 %collective-permute-start.3 = (bf16[32,1024]{1,0:T(8,128)(2,1)S(1)}, bf16[32,1024]{1,0:T(8,128)(2,1)S(1)}, u32[]{:S(2)}, u32[]{:S(2)}) collective-permute-start(bf16[32,1024]{1,0:T(8,128)(2,1)S(1)} %get-tuple-element.36), channel_id=1, source_target_pairs={{0,6},{1,7},{2,4},{3,5},{4,2},{5,3},{6,0},{7,1},{8,14},{9,15},{10,... | collective-permute-start | bytes 196616 | tf_op jit(solution)/shard_map/ppermute | solution.py:156
  64.5 15.7 %collective-permute-start.4 = (bf16[32,1024]{1,0:T(8,128)(2,1)S(1)}, bf16[32,1024]{1,0:T(8,128)(2,1)S(1)}, u32[]{:S(2)}, u32[]{:S(2)}) collective-permute-start(bf16[32,1024]{1,0:T(8,128)(2,1)S(1)} %get-tuple-element.37), channel_id=1, source_target_pairs={{0,8},{1,9},{2,10},{3,11},{4,12},{5,13},{6,14},{7,15},{8,0},{9,1},... | collective-permute-start | bytes 196616 | tf_op jit(solution)/shard_map/ppermute | solution.py:156
  66.3 19.6 %collective-permute-start.5 = (bf16[32,1024]{1,0:T(8,128)(2,1)S(1)}, bf16[32,1024]{1,0:T(8,128)(2,1)S(1)}, u32[]{:S(2)}, u32[]{:S(2)}) collective-permute-start(bf16[32,1024]{1,0:T(8,128)(2,1)S(1)} %get-tuple-element.38), channel_id=1, source_target_pairs={{0,10},{1,11},{2,8},{3,9},{4,14},{5,15},{6,12},{7,13},{8,2},{9,3},... | collective-permute-start | bytes 196616 | tf_op jit(solution)/shard_map/ppermute | solution.py:156
  72.7 15.5 %collective-permute-start.6 = (bf16[32,1024]{1,0:T(8,128)(2,1)S(1)}, bf16[32,1024]{1,0:T(8,128)(2,1)S(1)}, u32[]{:S(2)}, u32[]{:S(2)}) collective-permute-start(bf16[32,1024]{1,0:T(8,128)(2,1)S(1)} %get-tuple-element.39), channel_id=1, source_target_pairs={{0,12},{1,13},{2,14},{3,15},{4,8},{5,9},{6,10},{7,11},{8,4},{9,5},... | collective-permute-start | bytes 196616 | tf_op jit(solution)/shard_map/ppermute | solution.py:156
  73.7 15.9 %collective-permute-start.7 = (bf16[32,1024]{1,0:T(8,128)(2,1)S(1)}, bf16[32,1024]{1,0:T(8,128)(2,1)S(1)}, u32[]{:S(2)}, u32[]{:S(2)}) collective-permute-start(bf16[32,1024]{1,0:T(8,128)(2,1)S(1)} %get-tuple-element.40), channel_id=1, source_target_pairs={{0,14},{1,15},{2,12},{3,13},{4,10},{5,11},{6,8},{7,9},{8,6},{9,7},... | collective-permute-start | bytes 196616 | tf_op jit(solution)/shard_map/ppermute | solution.py:156
  76.6 19.5 %collective-permute-start.8 = (bf16[32,1024]{1,0:T(8,128)(2,1)S(1)}, bf16[32,1024]{1,0:T(8,128)(2,1)S(1)}, u32[]{:S(2)}, u32[]{:S(2)}) collective-permute-start(bf16[32,1024]{1,0:T(8,128)(2,1)S(1)} %get-tuple-element.41), channel_id=1, source_target_pairs={{0,16},{1,17},{2,18},{3,19},{4,20},{5,21},{6,22},{7,23},{8,24},{9,... | collective-permute-start | bytes 196616 | tf_op jit(solution)/shard_map/ppermute | solution.py:156
  80.2 18.2 %collective-permute-start.9 = (bf16[32,1024]{1,0:T(8,128)(2,1)S(1)}, bf16[32,1024]{1,0:T(8,128)(2,1)S(1)}, u32[]{:S(2)}, u32[]{:S(2)}) collective-permute-start(bf16[32,1024]{1,0:T(8,128)(2,1)S(1)} %get-tuple-element.42), channel_id=1, source_target_pairs={{0,18},{1,19},{2,16},{3,17},{4,22},{5,23},{6,20},{7,21},{8,26},{9,... | collective-permute-start | bytes 196616 | tf_op jit(solution)/shard_map/ppermute | solution.py:156
  85.9 15.9 %collective-permute-start.10 = (bf16[32,1024]{1,0:T(8,128)(2,1)S(1)}, bf16[32,1024]{1,0:T(8,128)(2,1)S(1)}, u32[]{:S(2)}, u32[]{:S(2)}) collective-permute-start(bf16[32,1024]{1,0:T(8,128)(2,1)S(1)} %get-tuple-element.43), channel_id=1, source_target_pairs={{0,20},{1,21},{2,22},{3,23},{4,16},{5,17},{6,18},{7,19},{8,28},{9,... | collective-permute-start | bytes 196616 | tf_op jit(solution)/shard_map/ppermute | solution.py:156
  88.2 16.0 %collective-permute-start.11 = (bf16[32,1024]{1,0:T(8,128)(2,1)S(1)}, bf16[32,1024]{1,0:T(8,128)(2,1)S(1)}, u32[]{:S(2)}, u32[]{:S(2)}) collective-permute-start(bf16[32,1024]{1,0:T(8,128)(2,1)S(1)} %get-tuple-element.44), channel_id=1, source_target_pairs={{0,22},{1,23},{2,20},{3,21},{4,18},{5,19},{6,16},{7,17},{8,30},{9,... | collective-permute-start | bytes 196616 | tf_op jit(solution)/shard_map/ppermute | solution.py:156
  89.7 14.5 %collective-permute-start.12 = (bf16[32,1024]{1,0:T(8,128)(2,1)S(1)}, bf16[32,1024]{1,0:T(8,128)(2,1)S(1)}, u32[]{:S(2)}, u32[]{:S(2)}) collective-permute-start(bf16[32,1024]{1,0:T(8,128)(2,1)S(1)} %get-tuple-element.45), channel_id=1, source_target_pairs={{0,24},{1,25},{2,26},{3,27},{4,28},{5,29},{6,30},{7,31},{8,16},{9,... | collective-permute-start | bytes 196616 | tf_op jit(solution)/shard_map/ppermute | solution.py:156
  96.1 8.2 %collective-permute-start.13 = (bf16[32,1024]{1,0:T(8,128)(2,1)S(1)}, bf16[32,1024]{1,0:T(8,128)(2,1)S(1)}, u32[]{:S(2)}, u32[]{:S(2)}) collective-permute-start(bf16[32,1024]{1,0:T(8,128)(2,1)S(1)} %get-tuple-element.46), channel_id=1, source_target_pairs={{0,26},{1,27},{2,24},{3,25},{4,30},{5,31},{6,28},{7,29},{8,18},{9,... | collective-permute-start | bytes 196616 | tf_op jit(solution)/shard_map/ppermute | solution.py:156
  98.4 7.2 %collective-permute-start.14 = (bf16[32,1024]{1,0:T(8,128)(2,1)S(1)}, bf16[32,1024]{1,0:T(8,128)(2,1)S(1)}, u32[]{:S(2)}, u32[]{:S(2)}) collective-permute-start(bf16[32,1024]{1,0:T(8,128)(2,1)S(1)} %get-tuple-element.47), channel_id=1, source_target_pairs={{0,28},{1,29},{2,30},{3,31},{4,24},{5,25},{6,26},{7,27},{8,20},{9,... | collective-permute-start | bytes 196616 | tf_op jit(solution)/shard_map/ppermute | solution.py:156
  101.7 8.0 %collective-permute-start.15 = (bf16[32,1024]{1,0:T(8,128)(2,1)S(1)}, bf16[32,1024]{1,0:T(8,128)(2,1)S(1)}, u32[]{:S(2)}, u32[]{:S(2)}) collective-permute-start(bf16[32,1024]{1,0:T(8,128)(2,1)S(1)} %get-tuple-element.48), channel_id=1, source_target_pairs={{0,30},{1,31},{2,28},{3,29},{4,26},{5,27},{6,24},{7,25},{8,22},{9,... | collective-permute-start | bytes 196616 | tf_op jit(solution)/shard_map/ppermute | solution.py:156
  110.9 7.5 %copy-start.4 = (bf16[1,2048,1024]{2,1,0:T(8,128)(2,1)S(1)}, bf16[1,2048,1024]{2,1,0:T(8,128)(2,1)}, u32[]{:S(2)}) copy-start(bf16[1,2048,1024]{2,1,0:T(8,128)(2,1)} %param.7) | copy-start | bytes 12582916
  117.1 1.3 copy-start.7
  121.8 28.9 %all-to-all-start.3 = ((bf16[32,16,1024]{2,1,0:T(8,128)(2,1)}), bf16[32,16,1024]{2,1,0:T(8,128)(2,1)S(1)}, u32[]{:S(2)}, u32[]{:S(2)}) async-start(bf16[32,16,1024]{2,1,0:T(8,128)(2,1)} %bitcast.76), calls=%async_computation.3 | async-start | bytes 2097152 | tf_op jit(solution)/shard_map/all_to_all | solution.py:270
  125.0 1.6 %copy-start = (bf16[64,16,1024]{2,1,0:T(8,128)(2,1)S(1)}, bf16[64,16,1024]{2,1,0:T(8,128)(2,1)}, u32[]{:S(2)}) copy-start(bf16[64,16,1024]{2,1,0:T(8,128)(2,1)} %param.11) | copy-start | bytes 6291460
  125.0 2.8 %copy-start.1 = (f32[64,16,1024]{2,1,0:T(8,128)S(1)}, f32[64,16,1024]{2,1,0:T(8,128)}, u32[]{:S(2)}) copy-start(f32[64,16,1024]{2,1,0:T(8,128)} %param.13) | copy-start | bytes 12582916
  127.8 4.1 %copy-start.2 = (bf16[512,1024]{1,0:T(8,128)(2,1)S(1)}, bf16[512,1024]{1,0:T(8,128)(2,1)}, u32[]{:S(2)}) copy-start(bf16[512,1024]{1,0:T(8,128)(2,1)} %settle.1) | copy-start | bytes 3145732
  127.8 4.1 %copy-start.6 = (bf16[2048,512]{0,1:T(8,128)(2,1)S(1)}, bf16[2048,512]{0,1:T(8,128)(2,1)}, u32[]{:S(2)}) copy-start(bf16[2048,512]{0,1:T(8,128)(2,1)} %copy-done.5) | copy-start | bytes 6291460
  131.9 4.4 %copy-start.8 = (bf16[2048,512]{0,1:T(8,128)(2,1)S(1)}, bf16[2048,512]{0,1:T(8,128)(2,1)}, u32[]{:S(2)}) copy-start(bf16[2048,512]{0,1:T(8,128)(2,1)} %copy-done.7) | copy-start | bytes 6291460

commit v7 on v6

--- a/solution.py
+++ b/solution.py
@@ -13,13 +13,15 @@
 TOP = 16
 
 
-def gelu_parts(pre):
-    act = 0.5 * pre * (1.0 + lax.erf(pre * 0.7071067811865476))
-    slope = (
+def gelu(pre):
+    return 0.5 * pre * (1.0 + lax.erf(pre * 0.7071067811865476))
+
+
+def gelu_slope(pre):
+    return (
         0.5 * (1.0 + lax.erf(pre * 0.7071067811865476))
         + pre * jnp.exp(-0.5 * pre * pre) * 0.3989422804014327
     )
-    return (act, slope)
 
 
 def mix_of(route_ref):
@@ -313,15 +315,16 @@
     else:
         down = delivered(mix_call(me, routes, w_down, 1, 0, False)[0])
     pre = lax.dot_general(inputs, up, (((1,), (1,)), ((), ())), preferred_element_type=jnp.float32)
-    act_full, slope = gelu_parts(pre)
-    act = act_full.astype(jnp.bfloat16)
+    act = gelu(pre).astype(jnp.bfloat16)
+    kept = pre.astype(jnp.bfloat16)
+    act, kept = lax.optimization_barrier((act, kept))
     grad_down = returned(
         lax.dot_general(act, grads, (((0,), (0,)), ((), ())), preferred_element_type=jnp.float32),
     )
     d_act = lax.dot_general(
         grads, down, (((1,), (1,)), ((), ())), preferred_element_type=jnp.float32
     )
-    d_pre = (d_act * slope).astype(jnp.bfloat16)
+    d_pre = (d_act * gelu_slope(kept.astype(jnp.float32))).astype(jnp.bfloat16)
     grad_up = returned(
         lax.dot_general(d_pre, inputs, (((0,), (0,)), ((), ())), preferred_element_type=jnp.float32),
     )

time: 156 us -> 155 us (level)
  transfers between devices with their start and end apart: 20 -> 20, of which waited for: 10 -> 10; matrix products, arithmetic and copies ran while one was open for 22% -> 21% of each run, Pallas kernels for 6% -> 6%
where the time goes in v7:
time: 155 us
  waiting for transfers between devices  54.9 us (35%)
  starting transfers between devices  46 us (30%)
  matrix products  29.1 us (19%)
  Pallas kernels  15.3 us (10%)
  local copies, waits for them, and re-layouts  4.15 us (3%)
  other arithmetic  4.07 us (3%)
    all_to_all x4, waiting for transfers between devices, exchange(): lax.all_to_all(blocks, 'seg', split_axis=0, concat_axis=0, tiled=True)  35.8 us
    ppermute x16, starting transfers between devices, swap(): return lax.ppermute(block, 'seg', [(i, i ^ apart) for i in range(segs)])  29.7 us
    ppermute x16, waiting for transfers between devices, swap(): return lax.ppermute(block, 'seg', [(i, i ^ apart) for i in range(segs)])  19.2 us
    all_to_all x4, starting transfers between devices, exchange(): lax.all_to_all(blocks, 'seg', split_axis=0, concat_axis=0, tiled=True)  16.3 us
    dot_general x1, matrix products, step(): lax.dot_general(inputs, up, (((1,), (1,)), ((), ())), preferred_element_t...  6.4 us
    pallas_call x2, Pallas kernels, mix_call(): pl.pallas_call(functools.partial(mix_kernel, rows, top, resident), in_spe...  6.16 us
    dot_general x1, matrix products, step(): lax.dot_general(grads, down, (((1,), (1,)), ((), ())), preferred_element_...  6.02 us
    dot_general x1, matrix products, step(): jnp.dot(act, down, preferred_element_type=jnp.float32).astype(jnp.bfloat16)  4.42 us
  transfers between devices with their start and end apart: 20, of which 10 were waited for; matrix products, arithmetic and copies ran while one was open for 21% of the time, Pallas kernels for 6%

profile of v7, /device:TPU:0, one launch (start us, length us, event | category | flops | bytes accessed | tf_op | source)
XLA Modules:
  0.0 154.7 jit_solution(3407087390900386044)
XLA Ops:
  0.6 1.3 broadcast_in_dim.19
  1.9 7.3 %all-to-all-start = ((s32[32,1,64]{2,1,0:T(1,128)}), s32[32,1,64]{2,1,0:T(1,128)S(1)}, u32[]{:S(2)}, u32[]{:S(2)}) async-start(s32[32,1,64]{2,1,0:T(1,128)} %broadcast_in_dim.19), calls=%async_computation | async-start | bytes 32768 | tf_op jit(solution)/shard_map/all_to_all | solution.py:272
  9.2 1.6 %fetch.2 = bf16[64,16,1024]{2,1,0:T(8,128)(2,1)S(1)} custom-call(bf16[64,16,1024]{2,1,0:T(8,128)(2,1)} %refs_0_.2), custom_call_target="tpu_custom_call" | custom-call | tf_op jit(solution)/shard_map/fetch/pallas_call | solution.py:195
  10.8 5.5 %all-to-all-done.route_ref = s32[32,1,64]{2,1,0:T(1,128)S(1)} async-done(((s32[32,1,64]{2,1,0:T(1,128)}), s32[32,1,64]{2,1,0:T(1,128)S(1)}, u32[]{:S(2)}, u32[]{:S(2)}) %all-to-all-start) | async-done | bytes 8224 | tf_op jit(solution)/shard_map/all_to_all | solution.py:272
  16.3 2.1 %mix.2 = bf16[512,1024]{1,0:T(8,128)(2,1)} custom-call(s32[1]{0:T(128)} %bitcast.me_ref, s32[32,1,64]{2,1,0:T(1,128)S(1)} %all-to-all-done.route_ref, bf16[1024,1024]{1,0:T(8,128)(2,1)S(1)} %bitcast.56), custom_call_target="tpu_custom_call" | custom-call | tf_op jit(solution)/shard_map/mix/pallas_call | solution.py:88
  18.5 2.7 %all-to-all-start.1 = ((bf16[32,16,1024]{2,1,0:T(8,128)(2,1)}), bf16[32,16,1024]{2,1,0:T(8,128)(2,1)S(1)}, u32[]{:S(2)}, u32[]{:S(2)}) async-start(bf16[32,16,1024]{2,1,0:T(8,128)(2,1)} %bitcast.60), calls=%async_computation.1 | async-start | bytes 2097152 | tf_op jit(solution)/shard_map/all_to_all | solution.py:272
  21.1 4.0 %mix.3 = (bf16[256,1024]{1,0:T(8,128)(2,1)S(1)}, bf16[256,1024]{1,0:T(8,128)(2,1)}) custom-call(s32[1]{0:T(128)} %bitcast.me_ref, s32[32,1,64]{2,1,0:T(1,128)S(1)} %all-to-all-done.route_ref, bf16[1024,1024]{1,0:T(8,128)(2,1)} %bitcast.58), custom_call_target="tpu_custom_call" | custom-call | tf_op jit(solution)/shard_map/mix/pallas_call | solution.py:88
  25.2 0.2 collective-permute-start
  25.4 22.0 %all-to-all-done.1 = bf16[32,16,1024]{2,1,0:T(8,128)(2,1)S(1)} async-done(((bf16[32,16,1024]{2,1,0:T(8,128)(2,1)}), bf16[32,16,1024]{2,1,0:T(8,128)(2,1)S(1)}, u32[]{:S(2)}, u32[]{:S(2)}) %all-to-all-start.1) | async-done | bytes 1048608 | tf_op jit(solution)/shard_map/all_to_all | solution.py:272
  47.3 6.4 %convert_bitcast_fusion = (bf16[2048,512]{0,1:T(8,128)(2,1)}, bf16[2048,512]{0,1:T(8,128)(2,1)S(1)}) fusion(bf16[512,1024]{1,0:T(8,128)(2,1)S(1)} %bitcast.62, bf16[1,2048,1024]{2,1,0:T(8,128)(2,1)} %param.7), kind=kOutput, calls=%fused_computation.25 | convolution fusion | flops 2153775104 | bytes 9437184 | tf_op jit(solution)/shard_map/dot_general | solution.py:317
  53.7 3.3 %fusion.22 = bf16[512,1024]{1,0:T(8,128)(2,1)} fusion(bf16[2048,512]{0,1:T(8,128)(2,1)S(1)} %get-tuple-element.53, bf16[1,2048,1024]{2,1,0:T(8,128)(2,1)S(1)} %copy-done.3), kind=kOutput, calls=%fused_computation.28 | convolution fusion | flops 2148007936 | bytes 7340032 | tf_op jit(solution)/shard_map/dot_general | solution.py:322
  57.1 3.5 %all-to-all-start.2 = ((bf16[32,16,1024]{2,1,0:T(8,128)(2,1)}), bf16[32,16,1024]{2,1,0:T(8,128)(2,1)S(1)}, u32[]{:S(2)}, u32[]{:S(2)}) async-start(bf16[32,16,1024]{2,1,0:T(8,128)(2,1)} %bitcast.65), calls=%async_computation.2 | async-start | bytes 2097152 | tf_op jit(solution)/shard_map/all_to_all | solution.py:272
  60.6 0.0 collective-permute-done.refs_1_
  60.6 0.1 regroup.1
  60.7 1.8 %collective-permute-start.1 = (bf16[32,1024]{1,0:T(8,128)(2,1)S(1)}, bf16[32,1024]{1,0:T(8,128)(2,1)S(1)}, u32[]{:S(2)}, u32[]{:S(2)}) collective-permute-start(bf16[32,1024]{1,0:T(8,128)(2,1)S(1)} %get-tuple-element.37), channel_id=1, source_target_pairs={{0,2},{1,3},{2,0},{3,1},{4,6},{5,7},{6,4},{7,5},{8,10},{9,11},{10,... | collective-permute-start | bytes 196616 | tf_op jit(solution)/shard_map/ppermute | solution.py:158
  62.5 1.5 collective-permute-start.2
  64.0 0.3 collective-permute-start.3
  64.2 1.8 %collective-permute-start.4 = (bf16[32,1024]{1,0:T(8,128)(2,1)S(1)}, bf16[32,1024]{1,0:T(8,128)(2,1)S(1)}, u32[]{:S(2)}, u32[]{:S(2)}) collective-permute-start(bf16[32,1024]{1,0:T(8,128)(2,1)S(1)} %get-tuple-element.40), channel_id=1, source_target_pairs={{0,8},{1,9},{2,10},{3,11},{4,12},{5,13},{6,14},{7,15},{8,0},{9,1},... | collective-permute-start | bytes 196616 | tf_op jit(solution)/shard_map/ppermute | solution.py:158
  66.0 1.5 collective-permute-start.5
  67.5 4.9 %collective-permute-done.1.refs_2_ = bf16[32,1024]{1,0:T(8,128)(2,1)S(1)} collective-permute-done((bf16[32,1024]{1,0:T(8,128)(2,1)S(1)}, bf16[32,1024]{1,0:T(8,128)(2,1)S(1)}, u32[]{:S(2)}, u32[]{:S(2)}) %collective-permute-start.1) | collective-permute-done | bytes 65568 | tf_op jit(solution)/shard_map/ppermute | solution.py:158
  72.4 1.1 collective-permute-start.6
  73.4 0.0 collective-permute-done.2.refs_3_
  73.4 2.8 %collective-permute-start.7 = (bf16[32,1024]{1,0:T(8,128)(2,1)S(1)}, bf16[32,1024]{1,0:T(8,128)(2,1)S(1)}, u32[]{:S(2)}, u32[]{:S(2)}) collective-permute-start(bf16[32,1024]{1,0:T(8,128)(2,1)S(1)} %get-tuple-element.43), channel_id=1, source_target_pairs={{0,14},{1,15},{2,12},{3,13},{4,10},{5,11},{6,8},{7,9},{8,6},{9,7},... | collective-permute-start | bytes 196616 | tf_op jit(solution)/shard_map/ppermute | solution.py:158
  76.3 0.0 collective-permute-done.3.refs_4_
  76.3 1.8 %collective-permute-start.8 = (bf16[32,1024]{1,0:T(8,128)(2,1)S(1)}, bf16[32,1024]{1,0:T(8,128)(2,1)S(1)}, u32[]{:S(2)}, u32[]{:S(2)}) collective-permute-start(bf16[32,1024]{1,0:T(8,128)(2,1)S(1)} %get-tuple-element.44), channel_id=1, source_target_pairs={{0,16},{1,17},{2,18},{3,19},{4,20},{5,21},{6,22},{7,23},{8,24},{9,... | collective-permute-start | bytes 196616 | tf_op jit(solution)/shard_map/ppermute | solution.py:158
  78.1 1.9 %collective-permute-done.4.refs_5_ = bf16[32,1024]{1,0:T(8,128)(2,1)S(1)} collective-permute-done((bf16[32,1024]{1,0:T(8,128)(2,1)S(1)}, bf16[32,1024]{1,0:T(8,128)(2,1)S(1)}, u32[]{:S(2)}, u32[]{:S(2)}) %collective-permute-start.4) | collective-permute-done | bytes 65568 | tf_op jit(solution)/shard_map/ppermute | solution.py:158
  79.9 5.6 %collective-permute-start.9 = (bf16[32,1024]{1,0:T(8,128)(2,1)S(1)}, bf16[32,1024]{1,0:T(8,128)(2,1)S(1)}, u32[]{:S(2)}, u32[]{:S(2)}) collective-permute-start(bf16[32,1024]{1,0:T(8,128)(2,1)S(1)} %get-tuple-element.45), channel_id=1, source_target_pairs={{0,18},{1,19},{2,16},{3,17},{4,22},{5,23},{6,20},{7,21},{8,26},{9,... | collective-permute-start | bytes 196616 | tf_op jit(solution)/shard_map/ppermute | solution.py:158
  85.6 0.0 collective-permute-done.5.refs_6_
  85.6 2.3 %collective-permute-start.10 = (bf16[32,1024]{1,0:T(8,128)(2,1)S(1)}, bf16[32,1024]{1,0:T(8,128)(2,1)S(1)}, u32[]{:S(2)}, u32[]{:S(2)}) collective-permute-start(bf16[32,1024]{1,0:T(8,128)(2,1)S(1)} %get-tuple-element.46), channel_id=1, source_target_pairs={{0,20},{1,21},{2,22},{3,23},{4,16},{5,17},{6,18},{7,19},{8,28},{9,... | collective-permute-start | bytes 196616 | tf_op jit(solution)/shard_map/ppermute | solution.py:158
  87.9 0.0 collective-permute-done.6.refs_7_
  87.9 1.5 collective-permute-start.11
  89.4 0.0 collective-permute-done.7.refs_8_
  89.4 0.7 collective-permute-start.12
  90.1 5.7 %collective-permute-done.8.refs_9_ = bf16[32,1024]{1,0:T(8,128)(2,1)S(1)} collective-permute-done((bf16[32,1024]{1,0:T(8,128)(2,1)S(1)}, bf16[32,1024]{1,0:T(8,128)(2,1)S(1)}, u32[]{:S(2)}, u32[]{:S(2)}) %collective-permute-start.8) | collective-permute-done | bytes 65568 | tf_op jit(solution)/shard_map/ppermute | solution.py:158
  95.8 2.2 %collective-permute-start.13 = (bf16[32,1024]{1,0:T(8,128)(2,1)S(1)}, bf16[32,1024]{1,0:T(8,128)(2,1)S(1)}, u32[]{:S(2)}, u32[]{:S(2)}) collective-permute-start(bf16[32,1024]{1,0:T(8,128)(2,1)S(1)} %get-tuple-element.49), channel_id=1, source_target_pairs={{0,26},{1,27},{2,24},{3,25},{4,30},{5,31},{6,28},{7,29},{8,18},{9,... | collective-permute-start | bytes 196616 | tf_op jit(solution)/shard_map/ppermute | solution.py:158
  98.0 0.1 collective-permute-done.9.refs_10_
  98.1 3.4 %collective-permute-start.14 = (bf16[32,1024]{1,0:T(8,128)(2,1)S(1)}, bf16[32,1024]{1,0:T(8,128)(2,1)S(1)}, u32[]{:S(2)}, u32[]{:S(2)}) collective-permute-start(bf16[32,1024]{1,0:T(8,128)(2,1)S(1)} %get-tuple-element.50), channel_id=1, source_target_pairs={{0,28},{1,29},{2,30},{3,31},{4,24},{5,25},{6,26},{7,27},{8,20},{9,... | collective-permute-start | bytes 196616 | tf_op jit(solution)/shard_map/ppermute | solution.py:158
  101.4 0.0 collective-permute-done.10.refs_11_
  101.4 1.4 collective-permute-start.15
  102.8 1.1 collective-permute-done.11.refs_12_
  103.9 0.0 collective-permute-done.12.refs_13_
  103.9 0.0 collective-permute-done.13.refs_14_
  103.9 1.3 collective-permute-done.14.refs_15_
  105.3 4.2 %collective-permute-done.15.refs_16_ = bf16[32,1024]{1,0:T(8,128)(2,1)S(1)} collective-permute-done((bf16[32,1024]{1,0:T(8,128)(2,1)S(1)}, bf16[32,1024]{1,0:T(8,128)(2,1)S(1)}, u32[]{:S(2)}, u32[]{:S(2)}) %collective-permute-start.15) | collective-permute-done | bytes 65568 | tf_op jit(solution)/shard_map/ppermute | solution.py:158
  109.4 1.2 settle.1
  110.6 0.0 copy-start.4
  110.7 6.0 %fusion.15 = bf16[2048,512]{0,1:T(8,128)(2,1)S(1)} fusion(bf16[2048,512]{0,1:T(8,128)(2,1)} %get-tuple-element.52, bf16[512,1024]{1,0:T(8,128)(2,1)} %settle.1, bf16[1,2048,1024]{2,1,0:T(8,128)(2,1)} %param.8), kind=kOutput, calls=%fused_computation.22 | convolution fusion | flops 2159017984 | bytes 9437184 | tf_op jit(solution)/shard_map/dot_general | solution.py:324
  116.7 0.0 copy-start.7
  116.7 1.3 copy-done.7
  118.0 3.3 %fusion.19 = bf16[512,1024]{1,0:T(8,128)(2,1)} fusion(bf16[2048,512]{0,1:T(8,128)(2,1)S(1)} %fusion.15, bf16[1,2048,1024]{2,1,0:T(8,128)(2,1)S(1)} %copy-done.4), kind=kOutput, calls=%fused_computation.27 | convolution fusion | flops 2148007936 | bytes 7340032 | tf_op jit(solution)/shard_map/dot_general | solution.py:329
  121.3 0.0 all-to-all-done.2
  121.3 2.8 %all-to-all-start.3 = ((bf16[32,16,1024]{2,1,0:T(8,128)(2,1)}), bf16[32,16,1024]{2,1,0:T(8,128)(2,1)S(1)}, u32[]{:S(2)}, u32[]{:S(2)}) async-start(bf16[32,16,1024]{2,1,0:T(8,128)(2,1)} %bitcast.66), calls=%async_computation.3 | async-start | bytes 2097152 | tf_op jit(solution)/shard_map/all_to_all | solution.py:272
  124.2 0.4 turn.1
  124.5 0.0 copy-start
  124.5 0.0 copy-start.1
  124.5 1.3 fusion.27
  125.8 0.3 copy-done
  126.1 1.2 copy-done.1
  127.3 4.1 %subtract_convert_fusion = (bf16[64,16,1024]{2,1,0:T(8,128)(2,1)}, f32[64,16,1024]{2,1,0:T(8,128)}) fusion(bf16[64,16,1024]{2,1,0:T(8,128)(2,1)S(1)} %copy-done, f32[64,16,1024]{2,1,0:T(8,128)S(1)} %bitcast.61, f32[64,16,1024]{2,1,0:T(8,128)S(1)} %copy-done.1), kind=kLoop, calls=%fused_computation.19 | loop fusion | flops 6291456 | bytes 16777216 | tf_op jit(solution)/shard_map/convert_element_type | solution.py:305
  131.4 4.4 %convolution_convert_fusion.1 = bf16[2048,1024]{1,0:T(8,128)(2,1)} fusion(bf16[2048,512]{0,1:T(8,128)(2,1)S(1)} %copy-done.6, bf16[512,1024]{1,0:T(8,128)(2,1)S(1)} %copy-done.2), kind=kOutput, calls=%fused_computation.24 | convolution fusion | flops 2149580800 | bytes 7340032 | tf_op jit(solution)/shard_map/dot_general | solution.py:335
  135.8 4.4 %convolution_convert_fusion = bf16[2048,1024]{1,0:T(8,128)(2,1)} fusion(bf16[2048,512]{0,1:T(8,128)(2,1)S(1)} %copy-done.8, bf16[512,1024]{1,0:T(8,128)(2,1)S(1)} %bitcast.63), kind=kOutput, calls=%fused_computation.23 | convolution fusion | flops 2149580800 | bytes 7340032 | tf_op jit(solution)/shard_map/dot_general | solution.py:336
  140.3 1.6 %fetch.3 = bf16[64,16,1024]{2,1,0:T(8,128)(2,1)S(1)} custom-call(bf16[64,16,1024]{2,1,0:T(8,128)(2,1)} %refs_0_.2), custom_call_target="tpu_custom_call" | custom-call | tf_op jit(solution)/shard_map/fetch/pallas_call | solution.py:195
  141.9 8.3 %all-to-all-done.3 = bf16[32,16,1024]{2,1,0:T(8,128)(2,1)S(1)} async-done(((bf16[32,16,1024]{2,1,0:T(8,128)(2,1)}), bf16[32,16,1024]{2,1,0:T(8,128)(2,1)S(1)}, u32[]{:S(2)}, u32[]{:S(2)}) %all-to-all-start.3) | async-done | bytes 1048608 | tf_op jit(solution)/shard_map/all_to_all | solution.py:272
  150.2 4.3 %update_last.1 = (f32[1024,1024]{1,0:T(8,128)}, bf16[1024,1024]{1,0:T(8,128)(2,1)}) custom-call(s32[32,1,64]{2,1,0:T(1,128)S(1)} %all-to-all-done.route_ref, bf16[512,1024]{1,0:T(8,128)(2,1)S(1)} %bitcast.57, bf16[1024,1024]{1,0:T(8,128)(2,1)S(1)} %bitcast.55, f32[1024,1024]{1,0:T(8,128)} %bitcast.59), custom_call_target="tpu_custom_call" | custom-call | tf_op jit(solution)/shard_map/update_last/pallas_call | solution.py:249
  (11 shorter events, 0.0 us)
Async XLA Ops:
  1.9 14.4 %all-to-all-start = ((s32[32,1,64]{2,1,0:T(1,128)}), s32[32,1,64]{2,1,0:T(1,128)S(1)}, u32[]{:S(2)}, u32[]{:S(2)}) async-start(s32[32,1,64]{2,1,0:T(1,128)} %broadcast_in_dim.19), calls=%async_computation | async-start | bytes 32768 | tf_op jit(solution)/shard_map/all_to_all | solution.py:272
  18.5 28.9 %all-to-all-start.1 = ((bf16[32,16,1024]{2,1,0:T(8,128)(2,1)}), bf16[32,16,1024]{2,1,0:T(8,128)(2,1)S(1)}, u32[]{:S(2)}, u32[]{:S(2)}) async-start(bf16[32,16,1024]{2,1,0:T(8,128)(2,1)} %bitcast.60), calls=%async_computation.1 | async-start | bytes 2097152 | tf_op jit(solution)/shard_map/all_to_all | solution.py:272
  25.2 35.4 %collective-permute-start = (bf16[256,1024]{1,0:T(8,128)(2,1)}, bf16[256,1024]{1,0:T(8,128)(2,1)S(1)}, u32[]{:S(2)}, u32[]{:S(2)}) collective-permute-start(bf16[256,1024]{1,0:T(8,128)(2,1)} %get-tuple-element.36), channel_id=1, source_target_pairs={{0,1},{1,0},{2,3},{3,2},{4,5},{5,4},{6,7},{7,6},{8,9},{9,8},{10,11... | collective-permute-start | bytes 1572872 | tf_op jit(solution)/shard_map/ppermute | solution.py:158
  47.3 6.4 %copy-start.3 = (bf16[1,2048,1024]{2,1,0:T(8,128)(2,1)S(1)}, bf16[1,2048,1024]{2,1,0:T(8,128)(2,1)}, u32[]{:S(2)}) copy-start(bf16[1,2048,1024]{2,1,0:T(8,128)(2,1)} %param.8) | copy-start | bytes 12582916
  53.7 3.3 %copy-start.5 = (bf16[2048,512]{0,1:T(8,128)(2,1)}, bf16[2048,512]{0,1:T(8,128)(2,1)S(1)}, u32[]{:S(2)}) copy-start(bf16[2048,512]{0,1:T(8,128)(2,1)S(1)} %get-tuple-element.53) | copy-start | bytes 6291460
  57.1 64.2 %all-to-all-start.2 = ((bf16[32,16,1024]{2,1,0:T(8,128)(2,1)}), bf16[32,16,1024]{2,1,0:T(8,128)(2,1)S(1)}, u32[]{:S(2)}, u32[]{:S(2)}) async-start(bf16[32,16,1024]{2,1,0:T(8,128)(2,1)} %bitcast.65), calls=%async_computation.2 | async-start | bytes 2097152 | tf_op jit(solution)/shard_map/all_to_all | solution.py:272
  60.7 11.7 %collective-permute-start.1 = (bf16[32,1024]{1,0:T(8,128)(2,1)S(1)}, bf16[32,1024]{1,0:T(8,128)(2,1)S(1)}, u32[]{:S(2)}, u32[]{:S(2)}) collective-permute-start(bf16[32,1024]{1,0:T(8,128)(2,1)S(1)} %get-tuple-element.37), channel_id=1, source_target_pairs={{0,2},{1,3},{2,0},{3,1},{4,6},{5,7},{6,4},{7,5},{8,10},{9,11},{10,... | collective-permute-start | bytes 196616 | tf_op jit(solution)/shard_map/ppermute | solution.py:158
  62.5 10.9 %collective-permute-start.2 = (bf16[32,1024]{1,0:T(8,128)(2,1)S(1)}, bf16[32,1024]{1,0:T(8,128)(2,1)S(1)}, u32[]{:S(2)}, u32[]{:S(2)}) collective-permute-start(bf16[32,1024]{1,0:T(8,128)(2,1)S(1)} %get-tuple-element.38), channel_id=1, source_target_pairs={{0,4},{1,5},{2,6},{3,7},{4,0},{5,1},{6,2},{7,3},{8,12},{9,13},{10,... | collective-permute-start | bytes 196616 | tf_op jit(solution)/shard_map/ppermute | solution.py:158
  64.0 12.3 %collective-permute-start.3 = (bf16[32,1024]{1,0:T(8,128)(2,1)S(1)}, bf16[32,1024]{1,0:T(8,128)(2,1)S(1)}, u32[]{:S(2)}, u32[]{:S(2)}) collective-permute-start(bf16[32,1024]{1,0:T(8,128)(2,1)S(1)} %get-tuple-element.39), channel_id=1, source_target_pairs={{0,6},{1,7},{2,4},{3,5},{4,2},{5,3},{6,0},{7,1},{8,14},{9,15},{10,... | collective-permute-start | bytes 196616 | tf_op jit(solution)/shard_map/ppermute | solution.py:158
  64.2 15.7 %collective-permute-start.4 = (bf16[32,1024]{1,0:T(8,128)(2,1)S(1)}, bf16[32,1024]{1,0:T(8,128)(2,1)S(1)}, u32[]{:S(2)}, u32[]{:S(2)}) collective-permute-start(bf16[32,1024]{1,0:T(8,128)(2,1)S(1)} %get-tuple-element.40), channel_id=1, source_target_pairs={{0,8},{1,9},{2,10},{3,11},{4,12},{5,13},{6,14},{7,15},{8,0},{9,1},... | collective-permute-start | bytes 196616 | tf_op jit(solution)/shard_map/ppermute | solution.py:158
  66.0 19.6 %collective-permute-start.5 = (bf16[32,1024]{1,0:T(8,128)(2,1)S(1)}, bf16[32,1024]{1,0:T(8,128)(2,1)S(1)}, u32[]{:S(2)}, u32[]{:S(2)}) collective-permute-start(bf16[32,1024]{1,0:T(8,128)(2,1)S(1)} %get-tuple-element.41), channel_id=1, source_target_pairs={{0,10},{1,11},{2,8},{3,9},{4,14},{5,15},{6,12},{7,13},{8,2},{9,3},... | collective-permute-start | bytes 196616 | tf_op jit(solution)/shard_map/ppermute | solution.py:158
  72.4 15.5 %collective-permute-start.6 = (bf16[32,1024]{1,0:T(8,128)(2,1)S(1)}, bf16[32,1024]{1,0:T(8,128)(2,1)S(1)}, u32[]{:S(2)}, u32[]{:S(2)}) collective-permute-start(bf16[32,1024]{1,0:T(8,128)(2,1)S(1)} %get-tuple-element.42), channel_id=1, source_target_pairs={{0,12},{1,13},{2,14},{3,15},{4,8},{5,9},{6,10},{7,11},{8,4},{9,5},... | collective-permute-start | bytes 196616 | tf_op jit(solution)/shard_map/ppermute | solution.py:158
  73.4 15.9 %collective-permute-start.7 = (bf16[32,1024]{1,0:T(8,128)(2,1)S(1)}, bf16[32,1024]{1,0:T(8,128)(2,1)S(1)}, u32[]{:S(2)}, u32[]{:S(2)}) collective-permute-start(bf16[32,1024]{1,0:T(8,128)(2,1)S(1)} %get-tuple-element.43), channel_id=1, source_target_pairs={{0,14},{1,15},{2,12},{3,13},{4,10},{5,11},{6,8},{7,9},{8,6},{9,7},... | collective-permute-start | bytes 196616 | tf_op jit(solution)/shard_map/ppermute | solution.py:158
  76.3 19.5 %collective-permute-start.8 = (bf16[32,1024]{1,0:T(8,128)(2,1)S(1)}, bf16[32,1024]{1,0:T(8,128)(2,1)S(1)}, u32[]{:S(2)}, u32[]{:S(2)}) collective-permute-start(bf16[32,1024]{1,0:T(8,128)(2,1)S(1)} %get-tuple-element.44), channel_id=1, source_target_pairs={{0,16},{1,17},{2,18},{3,19},{4,20},{5,21},{6,22},{7,23},{8,24},{9,... | collective-permute-start | bytes 196616 | tf_op jit(solution)/shard_map/ppermute | solution.py:158
  79.9 18.2 %collective-permute-start.9 = (bf16[32,1024]{1,0:T(8,128)(2,1)S(1)}, bf16[32,1024]{1,0:T(8,128)(2,1)S(1)}, u32[]{:S(2)}, u32[]{:S(2)}) collective-permute-start(bf16[32,1024]{1,0:T(8,128)(2,1)S(1)} %get-tuple-element.45), channel_id=1, source_target_pairs={{0,18},{1,19},{2,16},{3,17},{4,22},{5,23},{6,20},{7,21},{8,26},{9,... | collective-permute-start | bytes 196616 | tf_op jit(solution)/shard_map/ppermute | solution.py:158
  85.6 15.9 %collective-permute-start.10 = (bf16[32,1024]{1,0:T(8,128)(2,1)S(1)}, bf16[32,1024]{1,0:T(8,128)(2,1)S(1)}, u32[]{:S(2)}, u32[]{:S(2)}) collective-permute-start(bf16[32,1024]{1,0:T(8,128)(2,1)S(1)} %get-tuple-element.46), channel_id=1, source_target_pairs={{0,20},{1,21},{2,22},{3,23},{4,16},{5,17},{6,18},{7,19},{8,28},{9,... | collective-permute-start | bytes 196616 | tf_op jit(solution)/shard_map/ppermute | solution.py:158
  87.9 16.0 %collective-permute-start.11 = (bf16[32,1024]{1,0:T(8,128)(2,1)S(1)}, bf16[32,1024]{1,0:T(8,128)(2,1)S(1)}, u32[]{:S(2)}, u32[]{:S(2)}) collective-permute-start(bf16[32,1024]{1,0:T(8,128)(2,1)S(1)} %get-tuple-element.47), channel_id=1, source_target_pairs={{0,22},{1,23},{2,20},{3,21},{4,18},{5,19},{6,16},{7,17},{8,30},{9,... | collective-permute-start | bytes 196616 | tf_op jit(solution)/shard_map/ppermute | solution.py:158
  89.4 14.5 %collective-permute-start.12 = (bf16[32,1024]{1,0:T(8,128)(2,1)S(1)}, bf16[32,1024]{1,0:T(8,128)(2,1)S(1)}, u32[]{:S(2)}, u32[]{:S(2)}) collective-permute-start(bf16[32,1024]{1,0:T(8,128)(2,1)S(1)} %get-tuple-element.48), channel_id=1, source_target_pairs={{0,24},{1,25},{2,26},{3,27},{4,28},{5,29},{6,30},{7,31},{8,16},{9,... | collective-permute-start | bytes 196616 | tf_op jit(solution)/shard_map/ppermute | solution.py:158
  95.8 8.2 %collective-permute-start.13 = (bf16[32,1024]{1,0:T(8,128)(2,1)S(1)}, bf16[32,1024]{1,0:T(8,128)(2,1)S(1)}, u32[]{:S(2)}, u32[]{:S(2)}) collective-permute-start(bf16[32,1024]{1,0:T(8,128)(2,1)S(1)} %get-tuple-element.49), channel_id=1, source_target_pairs={{0,26},{1,27},{2,24},{3,25},{4,30},{5,31},{6,28},{7,29},{8,18},{9,... | collective-permute-start | bytes 196616 | tf_op jit(solution)/shard_map/ppermute | solution.py:158
  98.1 7.2 %collective-permute-start.14 = (bf16[32,1024]{1,0:T(8,128)(2,1)S(1)}, bf16[32,1024]{1,0:T(8,128)(2,1)S(1)}, u32[]{:S(2)}, u32[]{:S(2)}) collective-permute-start(bf16[32,1024]{1,0:T(8,128)(2,1)S(1)} %get-tuple-element.50), channel_id=1, source_target_pairs={{0,28},{1,29},{2,30},{3,31},{4,24},{5,25},{6,26},{7,27},{8,20},{9,... | collective-permute-start | bytes 196616 | tf_op jit(solution)/shard_map/ppermute | solution.py:158
  101.4 8.0 %collective-permute-start.15 = (bf16[32,1024]{1,0:T(8,128)(2,1)S(1)}, bf16[32,1024]{1,0:T(8,128)(2,1)S(1)}, u32[]{:S(2)}, u32[]{:S(2)}) collective-permute-start(bf16[32,1024]{1,0:T(8,128)(2,1)S(1)} %get-tuple-element.51), channel_id=1, source_target_pairs={{0,30},{1,31},{2,28},{3,29},{4,26},{5,27},{6,24},{7,25},{8,22},{9,... | collective-permute-start | bytes 196616 | tf_op jit(solution)/shard_map/ppermute | solution.py:158
  110.6 7.4 %copy-start.4 = (bf16[1,2048,1024]{2,1,0:T(8,128)(2,1)S(1)}, bf16[1,2048,1024]{2,1,0:T(8,128)(2,1)}, u32[]{:S(2)}) copy-start(bf16[1,2048,1024]{2,1,0:T(8,128)(2,1)} %param.7) | copy-start | bytes 12582916
  116.7 1.3 copy-start.7
  121.3 28.9 %all-to-all-start.3 = ((bf16[32,16,1024]{2,1,0:T(8,128)(2,1)}), bf16[32,16,1024]{2,1,0:T(8,128)(2,1)S(1)}, u32[]{:S(2)}, u32[]{:S(2)}) async-start(bf16[32,16,1024]{2,1,0:T(8,128)(2,1)} %bitcast.66), calls=%async_computation.3 | async-start | bytes 2097152 | tf_op jit(solution)/shard_map/all_to_all | solution.py:272
  124.5 1.6 %copy-start = (bf16[64,16,1024]{2,1,0:T(8,128)(2,1)S(1)}, bf16[64,16,1024]{2,1,0:T(8,128)(2,1)}, u32[]{:S(2)}) copy-start(bf16[64,16,1024]{2,1,0:T(8,128)(2,1)} %param.11) | copy-start | bytes 6291460
  124.5 2.8 %copy-start.1 = (f32[64,16,1024]{2,1,0:T(8,128)S(1)}, f32[64,16,1024]{2,1,0:T(8,128)}, u32[]{:S(2)}) copy-start(f32[64,16,1024]{2,1,0:T(8,128)} %param.13) | copy-start | bytes 12582916
  127.3 4.1 %copy-start.2 = (bf16[512,1024]{1,0:T(8,128)(2,1)S(1)}, bf16[512,1024]{1,0:T(8,128)(2,1)}, u32[]{:S(2)}) copy-start(bf16[512,1024]{1,0:T(8,128)(2,1)} %settle.1) | copy-start | bytes 3145732
  127.3 4.1 %copy-start.6 = (bf16[2048,512]{0,1:T(8,128)(2,1)S(1)}, bf16[2048,512]{0,1:T(8,128)(2,1)}, u32[]{:S(2)}) copy-start(bf16[2048,512]{0,1:T(8,128)(2,1)} %copy-done.5) | copy-start | bytes 6291460
  131.4 4.4 %copy-start.8 = (bf16[2048,512]{0,1:T(8,128)(2,1)S(1)}, bf16[2048,512]{0,1:T(8,128)(2,1)}, u32[]{:S(2)}) copy-start(bf16[2048,512]{0,1:T(8,128)(2,1)} %copy-done.7) | copy-start | bytes 6291460

commit v8 on v7

--- a/solution.py
+++ b/solution.py
@@ -59,19 +59,18 @@
     if not resident:
         fetched.wait()
         weight_ref = held_ref
-    size = sum_ref.shape[0] // sems.shape[0]
+    tile = sum_ref.shape[1] // sems.shape[0]
     lines = outs[0].shape[0]
     copies = []
     for i in range(sems.shape[0]):
-        here = slice(i * size, (i + 1) * size)
-        sums = jnp.dot(mixer_ref[here, :], weight_ref[...], preferred_element_type=jnp.float32)
-        sum_ref[here, :] = sums.astype(jnp.bfloat16)
-        place = pl.ds(i * size % lines, size)
-        copy = pltpu.make_async_copy(
-            sum_ref.at[here, :], outs[i * size // lines].at[place, :], sems.at[i]
-        )
-        copy.start()
-        copies.append(copy)
+        here = slice(i * tile, (i + 1) * tile)
+        sums = jnp.dot(mixer_ref[...], weight_ref[:, here], preferred_element_type=jnp.float32)
+        sum_ref[:, here] = sums.astype(jnp.bfloat16)
+        for j, out in enumerate(outs):
+            source = sum_ref.at[j * lines : (j + 1) * lines, here]
+            copy = pltpu.make_async_copy(source, out.at[:, here], sems.at[i, j])
+            copy.start()
+            copies.append(copy)
     for copy in copies:
         copy.wait()
 
@@ -80,7 +79,7 @@
     segs = routes.shape[0]
     experts, rows, width = weights.shape
     lines = segs * rows // parts
-    steps = max(4, parts)
+    steps = 4
     weights = weights.reshape(experts * rows, width)
     whole, free = pl.BlockSpec(memory_space=pltpu.VMEM), pl.BlockSpec(memory_space=pl.ANY)
     if not resident:
@@ -98,7 +97,7 @@
             pltpu.VMEM((segs * rows, width), jnp.bfloat16),
             pltpu.VMEM((8, 128) if resident else (experts * rows, width), jnp.bfloat16),
             pltpu.SemaphoreType.DMA,
-            pltpu.SemaphoreType.DMA((steps,)),
+            pltpu.SemaphoreType.DMA((steps, parts)),
         ],
         compiler_params=pltpu.CompilerParams(vmem_limit_bytes=10 << 20),
         name="mix",

time: 155 us -> 155 us (level)
  no operation moved by 1% of the time
where the time goes in v8:
time: 155 us
  waiting for transfers between devices  53.8 us (35%)
  starting transfers between devices  46.1 us (30%)
  matrix products  29.1 us (19%)
  Pallas kernels  16.6 us (11%)
  local copies, waits for them, and re-layouts  4.15 us (3%)
  other arithmetic  4.07 us (3%)
    all_to_all x4, waiting for transfers between devices, exchange(): lax.all_to_all(blocks, 'seg', split_axis=0, concat_axis=0, tiled=True)  34.6 us
    ppermute x16, starting transfers between devices, swap(): return lax.ppermute(block, 'seg', [(i, i ^ apart) for i in range(segs)])  29.7 us
    ppermute x16, waiting for transfers between devices, swap(): return lax.ppermute(block, 'seg', [(i, i ^ apart) for i in range(segs)])  19.2 us
    all_to_all x4, starting transfers between devices, exchange(): lax.all_to_all(blocks, 'seg', split_axis=0, concat_axis=0, tiled=True)  16.4 us
    pallas_call x2, Pallas kernels, mix_call(): pl.pallas_call(functools.partial(mix_kernel, rows, top, resident), in_spe...  7.4 us
    dot_general x1, matrix products, step(): lax.dot_general(inputs, up, (((1,), (1,)), ((), ())), preferred_element_t...  6.37 us
    dot_general x1, matrix products, step(): lax.dot_general(grads, down, (((1,), (1,)), ((), ())), preferred_element_...  6.01 us
    dot_general x1, matrix products, step(): jnp.dot(act, down, preferred_element_type=jnp.float32).astype(jnp.bfloat16)  4.42 us
  transfers between devices with their start and end apart: 20, of which 10 were waited for; matrix products, arithmetic and copies ran while one was open for 21% of the time, Pallas kernels for 6%

profile of v8, /device:TPU:0, one launch (start us, length us, event | category | flops | bytes accessed | tf_op | source)
XLA Modules:
  0.0 154.8 jit_solution(15890981711744807225)
XLA Ops:
  0.6 1.3 broadcast_in_dim.19
  1.9 7.3 %all-to-all-start = ((s32[32,1,64]{2,1,0:T(1,128)}), s32[32,1,64]{2,1,0:T(1,128)S(1)}, u32[]{:S(2)}, u32[]{:S(2)}) async-start(s32[32,1,64]{2,1,0:T(1,128)} %broadcast_in_dim.19), calls=%async_computation | async-start | bytes 32768 | tf_op jit(solution)/shard_map/all_to_all | solution.py:271
  9.2 1.6 %fetch.2 = bf16[64,16,1024]{2,1,0:T(8,128)(2,1)S(1)} custom-call(bf16[64,16,1024]{2,1,0:T(8,128)(2,1)} %refs_0_.2), custom_call_target="tpu_custom_call" | custom-call | tf_op jit(solution)/shard_map/fetch/pallas_call | solution.py:194
  10.8 5.5 %all-to-all-done.route_ref = s32[32,1,64]{2,1,0:T(1,128)S(1)} async-done(((s32[32,1,64]{2,1,0:T(1,128)}), s32[32,1,64]{2,1,0:T(1,128)S(1)}, u32[]{:S(2)}, u32[]{:S(2)}) %all-to-all-start) | async-done | bytes 8224 | tf_op jit(solution)/shard_map/all_to_all | solution.py:271
  16.3 2.2 %mix.2 = bf16[512,1024]{1,0:T(8,128)(2,1)} custom-call(s32[1]{0:T(128)} %bitcast.me_ref, s32[32,1,64]{2,1,0:T(1,128)S(1)} %all-to-all-done.route_ref, bf16[1024,1024]{1,0:T(8,128)(2,1)S(1)} %bitcast.56), custom_call_target="tpu_custom_call" | custom-call | tf_op jit(solution)/shard_map/mix/pallas_call | solution.py:87
  18.6 2.7 %all-to-all-start.1 = ((bf16[32,16,1024]{2,1,0:T(8,128)(2,1)}), bf16[32,16,1024]{2,1,0:T(8,128)(2,1)S(1)}, u32[]{:S(2)}, u32[]{:S(2)}) async-start(bf16[32,16,1024]{2,1,0:T(8,128)(2,1)} %bitcast.60), calls=%async_computation.1 | async-start | bytes 2097152 | tf_op jit(solution)/shard_map/all_to_all | solution.py:271
  21.3 5.2 %mix.3 = (bf16[256,1024]{1,0:T(8,128)(2,1)S(1)}, bf16[256,1024]{1,0:T(8,128)(2,1)}) custom-call(s32[1]{0:T(128)} %bitcast.me_ref, s32[32,1,64]{2,1,0:T(1,128)S(1)} %all-to-all-done.route_ref, bf16[1024,1024]{1,0:T(8,128)(2,1)} %bitcast.58), custom_call_target="tpu_custom_call" | custom-call | tf_op jit(solution)/shard_map/mix/pallas_call | solution.py:87
  26.4 0.2 collective-permute-start
  26.6 20.8 %all-to-all-done.1 = bf16[32,16,1024]{2,1,0:T(8,128)(2,1)S(1)} async-done(((bf16[32,16,1024]{2,1,0:T(8,128)(2,1)}), bf16[32,16,1024]{2,1,0:T(8,128)(2,1)S(1)}, u32[]{:S(2)}, u32[]{:S(2)}) %all-to-all-start.1) | async-done | bytes 1048608 | tf_op jit(solution)/shard_map/all_to_all | solution.py:271
  47.5 6.4 %convert_bitcast_fusion = (bf16[2048,512]{0,1:T(8,128)(2,1)}, bf16[2048,512]{0,1:T(8,128)(2,1)S(1)}) fusion(bf16[512,1024]{1,0:T(8,128)(2,1)S(1)} %bitcast.62, bf16[1,2048,1024]{2,1,0:T(8,128)(2,1)} %param.7), kind=kOutput, calls=%fused_computation.25 | convolution fusion | flops 2153775104 | bytes 9437184 | tf_op jit(solution)/shard_map/dot_general | solution.py:316
  53.8 3.3 %fusion.22 = bf16[512,1024]{1,0:T(8,128)(2,1)} fusion(bf16[2048,512]{0,1:T(8,128)(2,1)S(1)} %get-tuple-element.53, bf16[1,2048,1024]{2,1,0:T(8,128)(2,1)S(1)} %copy-done.3), kind=kOutput, calls=%fused_computation.28 | convolution fusion | flops 2148007936 | bytes 7340032 | tf_op jit(solution)/shard_map/dot_general | solution.py:321
  57.2 3.6 %all-to-all-start.2 = ((bf16[32,16,1024]{2,1,0:T(8,128)(2,1)}), bf16[32,16,1024]{2,1,0:T(8,128)(2,1)S(1)}, u32[]{:S(2)}, u32[]{:S(2)}) async-start(bf16[32,16,1024]{2,1,0:T(8,128)(2,1)} %bitcast.65), calls=%async_computation.2 | async-start | bytes 2097152 | tf_op jit(solution)/shard_map/all_to_all | solution.py:271
  60.7 0.0 collective-permute-done.refs_1_
  60.7 0.1 regroup.1
  60.8 1.8 %collective-permute-start.1 = (bf16[32,1024]{1,0:T(8,128)(2,1)S(1)}, bf16[32,1024]{1,0:T(8,128)(2,1)S(1)}, u32[]{:S(2)}, u32[]{:S(2)}) collective-permute-start(bf16[32,1024]{1,0:T(8,128)(2,1)S(1)} %get-tuple-element.37), channel_id=1, source_target_pairs={{0,2},{1,3},{2,0},{3,1},{4,6},{5,7},{6,4},{7,5},{8,10},{9,11},{10,... | collective-permute-start | bytes 196616 | tf_op jit(solution)/shard_map/ppermute | solution.py:157
  62.6 1.5 collective-permute-start.2
  64.1 0.3 collective-permute-start.3
  64.4 1.8 %collective-permute-start.4 = (bf16[32,1024]{1,0:T(8,128)(2,1)S(1)}, bf16[32,1024]{1,0:T(8,128)(2,1)S(1)}, u32[]{:S(2)}, u32[]{:S(2)}) collective-permute-start(bf16[32,1024]{1,0:T(8,128)(2,1)S(1)} %get-tuple-element.40), channel_id=1, source_target_pairs={{0,8},{1,9},{2,10},{3,11},{4,12},{5,13},{6,14},{7,15},{8,0},{9,1},... | collective-permute-start | bytes 196616 | tf_op jit(solution)/shard_map/ppermute | solution.py:157
  66.1 1.5 collective-permute-start.5
  67.6 4.9 %collective-permute-done.1.refs_2_ = bf16[32,1024]{1,0:T(8,128)(2,1)S(1)} collective-permute-done((bf16[32,1024]{1,0:T(8,128)(2,1)S(1)}, bf16[32,1024]{1,0:T(8,128)(2,1)S(1)}, u32[]{:S(2)}, u32[]{:S(2)}) %collective-permute-start.1) | collective-permute-done | bytes 65568 | tf_op jit(solution)/shard_map/ppermute | solution.py:157
  72.5 1.1 collective-permute-start.6
  73.6 0.0 collective-permute-done.2.refs_3_
  73.6 2.8 %collective-permute-start.7 = (bf16[32,1024]{1,0:T(8,128)(2,1)S(1)}, bf16[32,1024]{1,0:T(8,128)(2,1)S(1)}, u32[]{:S(2)}, u32[]{:S(2)}) collective-permute-start(bf16[32,1024]{1,0:T(8,128)(2,1)S(1)} %get-tuple-element.43), channel_id=1, source_target_pairs={{0,14},{1,15},{2,12},{3,13},{4,10},{5,11},{6,8},{7,9},{8,6},{9,7},... | collective-permute-start | bytes 196616 | tf_op jit(solution)/shard_map/ppermute | solution.py:157
  76.4 0.0 collective-permute-done.3.refs_4_
  76.4 1.8 %collective-permute-start.8 = (bf16[32,1024]{1,0:T(8,128)(2,1)S(1)}, bf16[32,1024]{1,0:T(8,128)(2,1)S(1)}, u32[]{:S(2)}, u32[]{:S(2)}) collective-permute-start(bf16[32,1024]{1,0:T(8,128)(2,1)S(1)} %get-tuple-element.44), channel_id=1, source_target_pairs={{0,16},{1,17},{2,18},{3,19},{4,20},{5,21},{6,22},{7,23},{8,24},{9,... | collective-permute-start | bytes 196616 | tf_op jit(solution)/shard_map/ppermute | solution.py:157
  78.2 1.9 %collective-permute-done.4.refs_5_ = bf16[32,1024]{1,0:T(8,128)(2,1)S(1)} collective-permute-done((bf16[32,1024]{1,0:T(8,128)(2,1)S(1)}, bf16[32,1024]{1,0:T(8,128)(2,1)S(1)}, u32[]{:S(2)}, u32[]{:S(2)}) %collective-permute-start.4) | collective-permute-done | bytes 65568 | tf_op jit(solution)/shard_map/ppermute | solution.py:157
  80.1 5.6 %collective-permute-start.9 = (bf16[32,1024]{1,0:T(8,128)(2,1)S(1)}, bf16[32,1024]{1,0:T(8,128)(2,1)S(1)}, u32[]{:S(2)}, u32[]{:S(2)}) collective-permute-start(bf16[32,1024]{1,0:T(8,128)(2,1)S(1)} %get-tuple-element.45), channel_id=1, source_target_pairs={{0,18},{1,19},{2,16},{3,17},{4,22},{5,23},{6,20},{7,21},{8,26},{9,... | collective-permute-start | bytes 196616 | tf_op jit(solution)/shard_map/ppermute | solution.py:157
  85.7 0.0 collective-permute-done.5.refs_6_
  85.7 2.3 %collective-permute-start.10 = (bf16[32,1024]{1,0:T(8,128)(2,1)S(1)}, bf16[32,1024]{1,0:T(8,128)(2,1)S(1)}, u32[]{:S(2)}, u32[]{:S(2)}) collective-permute-start(bf16[32,1024]{1,0:T(8,128)(2,1)S(1)} %get-tuple-element.46), channel_id=1, source_target_pairs={{0,20},{1,21},{2,22},{3,23},{4,16},{5,17},{6,18},{7,19},{8,28},{9,... | collective-permute-start | bytes 196616 | tf_op jit(solution)/shard_map/ppermute | solution.py:157
  88.1 0.0 collective-permute-done.6.refs_7_
  88.1 1.5 collective-permute-start.11
  89.5 0.0 collective-permute-done.7.refs_8_
  89.5 0.7 collective-permute-start.12
  90.2 5.7 %collective-permute-done.8.refs_9_ = bf16[32,1024]{1,0:T(8,128)(2,1)S(1)} collective-permute-done((bf16[32,1024]{1,0:T(8,128)(2,1)S(1)}, bf16[32,1024]{1,0:T(8,128)(2,1)S(1)}, u32[]{:S(2)}, u32[]{:S(2)}) %collective-permute-start.8) | collective-permute-done | bytes 65568 | tf_op jit(solution)/shard_map/ppermute | solution.py:157
  95.9 2.2 %collective-permute-start.13 = (bf16[32,1024]{1,0:T(8,128)(2,1)S(1)}, bf16[32,1024]{1,0:T(8,128)(2,1)S(1)}, u32[]{:S(2)}, u32[]{:S(2)}) collective-permute-start(bf16[32,1024]{1,0:T(8,128)(2,1)S(1)} %get-tuple-element.49), channel_id=1, source_target_pairs={{0,26},{1,27},{2,24},{3,25},{4,30},{5,31},{6,28},{7,29},{8,18},{9,... | collective-permute-start | bytes 196616 | tf_op jit(solution)/shard_map/ppermute | solution.py:157
  98.2 0.1 collective-permute-done.9.refs_10_
  98.2 3.4 %collective-permute-start.14 = (bf16[32,1024]{1,0:T(8,128)(2,1)S(1)}, bf16[32,1024]{1,0:T(8,128)(2,1)S(1)}, u32[]{:S(2)}, u32[]{:S(2)}) collective-permute-start(bf16[32,1024]{1,0:T(8,128)(2,1)S(1)} %get-tuple-element.50), channel_id=1, source_target_pairs={{0,28},{1,29},{2,30},{3,31},{4,24},{5,25},{6,26},{7,27},{8,20},{9,... | collective-permute-start | bytes 196616 | tf_op jit(solution)/shard_map/ppermute | solution.py:157
  101.6 0.0 collective-permute-done.10.refs_11_
  101.6 1.4 collective-permute-start.15
  103.0 1.1 collective-permute-done.11.refs_12_
  104.1 0.0 collective-permute-done.12.refs_13_
  104.1 0.0 collective-permute-done.13.refs_14_
  104.1 1.3 collective-permute-done.14.refs_15_
  105.4 4.2 %collective-permute-done.15.refs_16_ = bf16[32,1024]{1,0:T(8,128)(2,1)S(1)} collective-permute-done((bf16[32,1024]{1,0:T(8,128)(2,1)S(1)}, bf16[32,1024]{1,0:T(8,128)(2,1)S(1)}, u32[]{:S(2)}, u32[]{:S(2)}) %collective-permute-start.15) | collective-permute-done | bytes 65568 | tf_op jit(solution)/shard_map/ppermute | solution.py:157
  109.5 1.2 settle.1
  110.8 0.0 copy-start.4
  110.8 6.0 %fusion.15 = bf16[2048,512]{0,1:T(8,128)(2,1)S(1)} fusion(bf16[2048,512]{0,1:T(8,128)(2,1)} %get-tuple-element.52, bf16[512,1024]{1,0:T(8,128)(2,1)} %settle.1, bf16[1,2048,1024]{2,1,0:T(8,128)(2,1)} %param.8), kind=kOutput, calls=%fused_computation.22 | convolution fusion | flops 2159017984 | bytes 9437184 | tf_op jit(solution)/shard_map/dot_general | solution.py:323
  116.8 0.0 copy-start.7
  116.8 1.3 copy-done.7
  118.1 3.3 %fusion.19 = bf16[512,1024]{1,0:T(8,128)(2,1)} fusion(bf16[2048,512]{0,1:T(8,128)(2,1)S(1)} %fusion.15, bf16[1,2048,1024]{2,1,0:T(8,128)(2,1)S(1)} %copy-done.4), kind=kOutput, calls=%fused_computation.27 | convolution fusion | flops 2148007936 | bytes 7340032 | tf_op jit(solution)/shard_map/dot_general | solution.py:328
  121.4 0.0 all-to-all-done.2
  121.4 2.8 %all-to-all-start.3 = ((bf16[32,16,1024]{2,1,0:T(8,128)(2,1)}), bf16[32,16,1024]{2,1,0:T(8,128)(2,1)S(1)}, u32[]{:S(2)}, u32[]{:S(2)}) async-start(bf16[32,16,1024]{2,1,0:T(8,128)(2,1)} %bitcast.66), calls=%async_computation.3 | async-start | bytes 2097152 | tf_op jit(solution)/shard_map/all_to_all | solution.py:271
  124.3 0.4 turn.1
  124.6 0.0 copy-start
  124.7 0.0 copy-start.1
  124.7 1.3 fusion.27
  125.9 0.3 copy-done
  126.2 1.2 copy-done.1
  127.5 4.1 %subtract_convert_fusion = (bf16[64,16,1024]{2,1,0:T(8,128)(2,1)}, f32[64,16,1024]{2,1,0:T(8,128)}) fusion(bf16[64,16,1024]{2,1,0:T(8,128)(2,1)S(1)} %copy-done, f32[64,16,1024]{2,1,0:T(8,128)S(1)} %bitcast.61, f32[64,16,1024]{2,1,0:T(8,128)S(1)} %copy-done.1), kind=kLoop, calls=%fused_computation.19 | loop fusion | flops 6291456 | bytes 16777216 | tf_op jit(solution)/shard_map/convert_element_type | solution.py:304
  131.6 4.4 %convolution_convert_fusion.1 = bf16[2048,1024]{1,0:T(8,128)(2,1)} fusion(bf16[2048,512]{0,1:T(8,128)(2,1)S(1)} %copy-done.6, bf16[512,1024]{1,0:T(8,128)(2,1)S(1)} %copy-done.2), kind=kOutput, calls=%fused_computation.24 | convolution fusion | flops 2149580800 | bytes 7340032 | tf_op jit(solution)/shard_map/dot_general | solution.py:334
  136.0 4.4 %convolution_convert_fusion = bf16[2048,1024]{1,0:T(8,128)(2,1)} fusion(bf16[2048,512]{0,1:T(8,128)(2,1)S(1)} %copy-done.8, bf16[512,1024]{1,0:T(8,128)(2,1)S(1)} %bitcast.63), kind=kOutput, calls=%fused_computation.23 | convolution fusion | flops 2149580800 | bytes 7340032 | tf_op jit(solution)/shard_map/dot_general | solution.py:335
  140.4 1.6 %fetch.3 = bf16[64,16,1024]{2,1,0:T(8,128)(2,1)S(1)} custom-call(bf16[64,16,1024]{2,1,0:T(8,128)(2,1)} %refs_0_.2), custom_call_target="tpu_custom_call" | custom-call | tf_op jit(solution)/shard_map/fetch/pallas_call | solution.py:194
  142.0 8.3 %all-to-all-done.3 = bf16[32,16,1024]{2,1,0:T(8,128)(2,1)S(1)} async-done(((bf16[32,16,1024]{2,1,0:T(8,128)(2,1)}), bf16[32,16,1024]{2,1,0:T(8,128)(2,1)S(1)}, u32[]{:S(2)}, u32[]{:S(2)}) %all-to-all-start.3) | async-done | bytes 1048608 | tf_op jit(solution)/shard_map/all_to_all | solution.py:271
  150.3 4.3 %update_last.1 = (f32[1024,1024]{1,0:T(8,128)}, bf16[1024,1024]{1,0:T(8,128)(2,1)}) custom-call(s32[32,1,64]{2,1,0:T(1,128)S(1)} %all-to-all-done.route_ref, bf16[512,1024]{1,0:T(8,128)(2,1)S(1)} %bitcast.57, bf16[1024,1024]{1,0:T(8,128)(2,1)S(1)} %bitcast.55, f32[1024,1024]{1,0:T(8,128)} %bitcast.59), custom_call_target="tpu_custom_call" | custom-call | tf_op jit(solution)/shard_map/update_last/pallas_call | solution.py:248
  (11 shorter events, 0.0 us)
Async XLA Ops:
  1.9 14.4 %all-to-all-start = ((s32[32,1,64]{2,1,0:T(1,128)}), s32[32,1,64]{2,1,0:T(1,128)S(1)}, u32[]{:S(2)}, u32[]{:S(2)}) async-start(s32[32,1,64]{2,1,0:T(1,128)} %broadcast_in_dim.19), calls=%async_computation | async-start | bytes 32768 | tf_op jit(solution)/shard_map/all_to_all | solution.py:271
  18.6 28.9 %all-to-all-start.1 = ((bf16[32,16,1024]{2,1,0:T(8,128)(2,1)}), bf16[32,16,1024]{2,1,0:T(8,128)(2,1)S(1)}, u32[]{:S(2)}, u32[]{:S(2)}) async-start(bf16[32,16,1024]{2,1,0:T(8,128)(2,1)} %bitcast.60), calls=%async_computation.1 | async-start | bytes 2097152 | tf_op jit(solution)/shard_map/all_to_all | solution.py:271
  26.4 34.3 %collective-permute-start = (bf16[256,1024]{1,0:T(8,128)(2,1)}, bf16[256,1024]{1,0:T(8,128)(2,1)S(1)}, u32[]{:S(2)}, u32[]{:S(2)}) collective-permute-start(bf16[256,1024]{1,0:T(8,128)(2,1)} %get-tuple-element.36), channel_id=1, source_target_pairs={{0,1},{1,0},{2,3},{3,2},{4,5},{5,4},{6,7},{7,6},{8,9},{9,8},{10,11... | collective-permute-start | bytes 1572872 | tf_op jit(solution)/shard_map/ppermute | solution.py:157
  47.5 6.4 %copy-start.3 = (bf16[1,2048,1024]{2,1,0:T(8,128)(2,1)S(1)}, bf16[1,2048,1024]{2,1,0:T(8,128)(2,1)}, u32[]{:S(2)}) copy-start(bf16[1,2048,1024]{2,1,0:T(8,128)(2,1)} %param.8) | copy-start | bytes 12582916
  53.8 3.3 %copy-start.5 = (bf16[2048,512]{0,1:T(8,128)(2,1)}, bf16[2048,512]{0,1:T(8,128)(2,1)S(1)}, u32[]{:S(2)}) copy-start(bf16[2048,512]{0,1:T(8,128)(2,1)S(1)} %get-tuple-element.53) | copy-start | bytes 6291460
  57.2 64.3 %all-to-all-start.2 = ((bf16[32,16,1024]{2,1,0:T(8,128)(2,1)}), bf16[32,16,1024]{2,1,0:T(8,128)(2,1)S(1)}, u32[]{:S(2)}, u32[]{:S(2)}) async-start(bf16[32,16,1024]{2,1,0:T(8,128)(2,1)} %bitcast.65), calls=%async_computation.2 | async-start | bytes 2097152 | tf_op jit(solution)/shard_map/all_to_all | solution.py:271
  60.8 11.7 %collective-permute-start.1 = (bf16[32,1024]{1,0:T(8,128)(2,1)S(1)}, bf16[32,1024]{1,0:T(8,128)(2,1)S(1)}, u32[]{:S(2)}, u32[]{:S(2)}) collective-permute-start(bf16[32,1024]{1,0:T(8,128)(2,1)S(1)} %get-tuple-element.37), channel_id=1, source_target_pairs={{0,2},{1,3},{2,0},{3,1},{4,6},{5,7},{6,4},{7,5},{8,10},{9,11},{10,... | collective-permute-start | bytes 196616 | tf_op jit(solution)/shard_map/ppermute | solution.py:157
  62.6 10.9 %collective-permute-start.2 = (bf16[32,1024]{1,0:T(8,128)(2,1)S(1)}, bf16[32,1024]{1,0:T(8,128)(2,1)S(1)}, u32[]{:S(2)}, u32[]{:S(2)}) collective-permute-start(bf16[32,1024]{1,0:T(8,128)(2,1)S(1)} %get-tuple-element.38), channel_id=1, source_target_pairs={{0,4},{1,5},{2,6},{3,7},{4,0},{5,1},{6,2},{7,3},{8,12},{9,13},{10,... | collective-permute-start | bytes 196616 | tf_op jit(solution)/shard_map/ppermute | solution.py:157
  64.1 12.3 %collective-permute-start.3 = (bf16[32,1024]{1,0:T(8,128)(2,1)S(1)}, bf16[32,1024]{1,0:T(8,128)(2,1)S(1)}, u32[]{:S(2)}, u32[]{:S(2)}) collective-permute-start(bf16[32,1024]{1,0:T(8,128)(2,1)S(1)} %get-tuple-element.39), channel_id=1, source_target_pairs={{0,6},{1,7},{2,4},{3,5},{4,2},{5,3},{6,0},{7,1},{8,14},{9,15},{10,... | collective-permute-start | bytes 196616 | tf_op jit(solution)/shard_map/ppermute | solution.py:157
  64.4 15.7 %collective-permute-start.4 = (bf16[32,1024]{1,0:T(8,128)(2,1)S(1)}, bf16[32,1024]{1,0:T(8,128)(2,1)S(1)}, u32[]{:S(2)}, u32[]{:S(2)}) collective-permute-start(bf16[32,1024]{1,0:T(8,128)(2,1)S(1)} %get-tuple-element.40), channel_id=1, source_target_pairs={{0,8},{1,9},{2,10},{3,11},{4,12},{5,13},{6,14},{7,15},{8,0},{9,1},... | collective-permute-start | bytes 196616 | tf_op jit(solution)/shard_map/ppermute | solution.py:157
  66.1 19.6 %collective-permute-start.5 = (bf16[32,1024]{1,0:T(8,128)(2,1)S(1)}, bf16[32,1024]{1,0:T(8,128)(2,1)S(1)}, u32[]{:S(2)}, u32[]{:S(2)}) collective-permute-start(bf16[32,1024]{1,0:T(8,128)(2,1)S(1)} %get-tuple-element.41), channel_id=1, source_target_pairs={{0,10},{1,11},{2,8},{3,9},{4,14},{5,15},{6,12},{7,13},{8,2},{9,3},... | collective-permute-start | bytes 196616 | tf_op jit(solution)/shard_map/ppermute | solution.py:157
  72.5 15.5 %collective-permute-start.6 = (bf16[32,1024]{1,0:T(8,128)(2,1)S(1)}, bf16[32,1024]{1,0:T(8,128)(2,1)S(1)}, u32[]{:S(2)}, u32[]{:S(2)}) collective-permute-start(bf16[32,1024]{1,0:T(8,128)(2,1)S(1)} %get-tuple-element.42), channel_id=1, source_target_pairs={{0,12},{1,13},{2,14},{3,15},{4,8},{5,9},{6,10},{7,11},{8,4},{9,5},... | collective-permute-start | bytes 196616 | tf_op jit(solution)/shard_map/ppermute | solution.py:157
  73.6 15.9 %collective-permute-start.7 = (bf16[32,1024]{1,0:T(8,128)(2,1)S(1)}, bf16[32,1024]{1,0:T(8,128)(2,1)S(1)}, u32[]{:S(2)}, u32[]{:S(2)}) collective-permute-start(bf16[32,1024]{1,0:T(8,128)(2,1)S(1)} %get-tuple-element.43), channel_id=1, source_target_pairs={{0,14},{1,15},{2,12},{3,13},{4,10},{5,11},{6,8},{7,9},{8,6},{9,7},... | collective-permute-start | bytes 196616 | tf_op jit(solution)/shard_map/ppermute | solution.py:157
  76.4 19.5 %collective-permute-start.8 = (bf16[32,1024]{1,0:T(8,128)(2,1)S(1)}, bf16[32,1024]{1,0:T(8,128)(2,1)S(1)}, u32[]{:S(2)}, u32[]{:S(2)}) collective-permute-start(bf16[32,1024]{1,0:T(8,128)(2,1)S(1)} %get-tuple-element.44), channel_id=1, source_target_pairs={{0,16},{1,17},{2,18},{3,19},{4,20},{5,21},{6,22},{7,23},{8,24},{9,... | collective-permute-start | bytes 196616 | tf_op jit(solution)/shard_map/ppermute | solution.py:157
  80.1 18.2 %collective-permute-start.9 = (bf16[32,1024]{1,0:T(8,128)(2,1)S(1)}, bf16[32,1024]{1,0:T(8,128)(2,1)S(1)}, u32[]{:S(2)}, u32[]{:S(2)}) collective-permute-start(bf16[32,1024]{1,0:T(8,128)(2,1)S(1)} %get-tuple-element.45), channel_id=1, source_target_pairs={{0,18},{1,19},{2,16},{3,17},{4,22},{5,23},{6,20},{7,21},{8,26},{9,... | collective-permute-start | bytes 196616 | tf_op jit(solution)/shard_map/ppermute | solution.py:157
  85.7 15.9 %collective-permute-start.10 = (bf16[32,1024]{1,0:T(8,128)(2,1)S(1)}, bf16[32,1024]{1,0:T(8,128)(2,1)S(1)}, u32[]{:S(2)}, u32[]{:S(2)}) collective-permute-start(bf16[32,1024]{1,0:T(8,128)(2,1)S(1)} %get-tuple-element.46), channel_id=1, source_target_pairs={{0,20},{1,21},{2,22},{3,23},{4,16},{5,17},{6,18},{7,19},{8,28},{9,... | collective-permute-start | bytes 196616 | tf_op jit(solution)/shard_map/ppermute | solution.py:157
  88.1 16.0 %collective-permute-start.11 = (bf16[32,1024]{1,0:T(8,128)(2,1)S(1)}, bf16[32,1024]{1,0:T(8,128)(2,1)S(1)}, u32[]{:S(2)}, u32[]{:S(2)}) collective-permute-start(bf16[32,1024]{1,0:T(8,128)(2,1)S(1)} %get-tuple-element.47), channel_id=1, source_target_pairs={{0,22},{1,23},{2,20},{3,21},{4,18},{5,19},{6,16},{7,17},{8,30},{9,... | collective-permute-start | bytes 196616 | tf_op jit(solution)/shard_map/ppermute | solution.py:157
  89.5 14.5 %collective-permute-start.12 = (bf16[32,1024]{1,0:T(8,128)(2,1)S(1)}, bf16[32,1024]{1,0:T(8,128)(2,1)S(1)}, u32[]{:S(2)}, u32[]{:S(2)}) collective-permute-start(bf16[32,1024]{1,0:T(8,128)(2,1)S(1)} %get-tuple-element.48), channel_id=1, source_target_pairs={{0,24},{1,25},{2,26},{3,27},{4,28},{5,29},{6,30},{7,31},{8,16},{9,... | collective-permute-start | bytes 196616 | tf_op jit(solution)/shard_map/ppermute | solution.py:157
  95.9 8.2 %collective-permute-start.13 = (bf16[32,1024]{1,0:T(8,128)(2,1)S(1)}, bf16[32,1024]{1,0:T(8,128)(2,1)S(1)}, u32[]{:S(2)}, u32[]{:S(2)}) collective-permute-start(bf16[32,1024]{1,0:T(8,128)(2,1)S(1)} %get-tuple-element.49), channel_id=1, source_target_pairs={{0,26},{1,27},{2,24},{3,25},{4,30},{5,31},{6,28},{7,29},{8,18},{9,... | collective-permute-start | bytes 196616 | tf_op jit(solution)/shard_map/ppermute | solution.py:157
  98.2 7.2 %collective-permute-start.14 = (bf16[32,1024]{1,0:T(8,128)(2,1)S(1)}, bf16[32,1024]{1,0:T(8,128)(2,1)S(1)}, u32[]{:S(2)}, u32[]{:S(2)}) collective-permute-start(bf16[32,1024]{1,0:T(8,128)(2,1)S(1)} %get-tuple-element.50), channel_id=1, source_target_pairs={{0,28},{1,29},{2,30},{3,31},{4,24},{5,25},{6,26},{7,27},{8,20},{9,... | collective-permute-start | bytes 196616 | tf_op jit(solution)/shard_map/ppermute | solution.py:157
  101.6 8.0 %collective-permute-start.15 = (bf16[32,1024]{1,0:T(8,128)(2,1)S(1)}, bf16[32,1024]{1,0:T(8,128)(2,1)S(1)}, u32[]{:S(2)}, u32[]{:S(2)}) collective-permute-start(bf16[32,1024]{1,0:T(8,128)(2,1)S(1)} %get-tuple-element.51), channel_id=1, source_target_pairs={{0,30},{1,31},{2,28},{3,29},{4,26},{5,27},{6,24},{7,25},{8,22},{9,... | collective-permute-start | bytes 196616 | tf_op jit(solution)/shard_map/ppermute | solution.py:157
  110.8 7.4 %copy-start.4 = (bf16[1,2048,1024]{2,1,0:T(8,128)(2,1)S(1)}, bf16[1,2048,1024]{2,1,0:T(8,128)(2,1)}, u32[]{:S(2)}) copy-start(bf16[1,2048,1024]{2,1,0:T(8,128)(2,1)} %param.7) | copy-start | bytes 12582916
  116.8 1.3 copy-start.7
  121.4 28.9 %all-to-all-start.3 = ((bf16[32,16,1024]{2,1,0:T(8,128)(2,1)}), bf16[32,16,1024]{2,1,0:T(8,128)(2,1)S(1)}, u32[]{:S(2)}, u32[]{:S(2)}) async-start(bf16[32,16,1024]{2,1,0:T(8,128)(2,1)} %bitcast.66), calls=%async_computation.3 | async-start | bytes 2097152 | tf_op jit(solution)/shard_map/all_to_all | solution.py:271
  124.6 1.6 %copy-start = (bf16[64,16,1024]{2,1,0:T(8,128)(2,1)S(1)}, bf16[64,16,1024]{2,1,0:T(8,128)(2,1)}, u32[]{:S(2)}) copy-start(bf16[64,16,1024]{2,1,0:T(8,128)(2,1)} %param.11) | copy-start | bytes 6291460
  124.7 2.8 %copy-start.1 = (f32[64,16,1024]{2,1,0:T(8,128)S(1)}, f32[64,16,1024]{2,1,0:T(8,128)}, u32[]{:S(2)}) copy-start(f32[64,16,1024]{2,1,0:T(8,128)} %param.13) | copy-start | bytes 12582916
  127.5 4.1 %copy-start.2 = (bf16[512,1024]{1,0:T(8,128)(2,1)S(1)}, bf16[512,1024]{1,0:T(8,128)(2,1)}, u32[]{:S(2)}) copy-start(bf16[512,1024]{1,0:T(8,128)(2,1)} %settle.1) | copy-start | bytes 3145732
  127.5 4.1 %copy-start.6 = (bf16[2048,512]{0,1:T(8,128)(2,1)S(1)}, bf16[2048,512]{0,1:T(8,128)(2,1)}, u32[]{:S(2)}) copy-start(bf16[2048,512]{0,1:T(8,128)(2,1)} %copy-done.5) | copy-start | bytes 6291460
  131.6 4.4 %copy-start.8 = (bf16[2048,512]{0,1:T(8,128)(2,1)S(1)}, bf16[2048,512]{0,1:T(8,128)(2,1)}, u32[]{:S(2)}) copy-start(bf16[2048,512]{0,1:T(8,128)(2,1)} %copy-done.7) | copy-start | bytes 6291460
